TPU v7x, 256 devices: a whole 4x4x8 slice. The times are simulated.
256 devices in a mesh: dp: 128 (over x, y, z_lo, core), sub: 2 (over z_hi).
Axes of the slice: x: 4, y: 4, z: 8 (z_hi: 2, z_lo: 4; z = z_hi * 4 + z_lo), core: 2. Of those that a mesh axis runs over, the one named last changes fastest.
Arguments:
- projections: float32 [49152, 128], P(('dp', 'sub')), may hold values from -6 to 6
- partner: int32 [49152], P(('dp', 'sub')), may hold values from 0 to 49151, as said below
Outputs:
- loss: float32 [], replicated
- grad_projections: float32 [49152, 128], P(('dp', 'sub'))
Inputs may be any that keep to these rules, and one draw needn't show every extreme that they name: partner pairs the views: partner[partner[i]] = i and partner[i] != i for every view.
All inputs are finite; a program needn't handle non-finite values.
Results may differ from a plain program's by a relative error of at most 0.0003.
The roundings to bfloat16 on the way count: a program that leaves them out, or rounds other values in their place, can miss the bound.
Values may be sent and summed in bfloat16 or wider, within the bound.
No kernel may reach another device: no remote copies, remote signals or barrier semaphores. Data moves between devices by JAX's collectives and lax.ppermute only.
A program may use at most 128 MiB of HBM per device.

v0:
```python
import jax
import jax.numpy as jnp
from jax import lax
from jax.sharding import Mesh
from jax.sharding import PartitionSpec as P

DP_SUB = ("dp_0", "dp_1", "dp_2", "dp_3", "sub")


TAU = 0.1
SHIFT = 10.0


def piece_ends(length, count):
    unit = 8 if length >= 8 * count else 1
    return [length // unit * k // count * unit for k in range(1, count)]


def all_blocks(value, axes, turns):
    pieces = value[None]
    for k in turns:
        pieces = lax.all_gather(pieces, axes[k], axis=0, tiled=True)
    current = [lax.axis_size(axes[k]) for k in reversed(turns)]
    pieces = pieces.reshape(*current, *value.shape)
    turned = sorted(range(len(turns)), key=lambda place: turns[len(turns) - 1 - place])
    return pieces.transpose(*turned, *range(len(turns), pieces.ndim)).reshape(-1, *value.shape)


def laid_out(pieces, dim):
    shape = list(pieces.shape[1:])
    shape[dim] *= pieces.shape[0]
    return jnp.moveaxis(pieces, 0, dim).reshape(shape)


def gather_at_once(value, axes, dim):
    numbers = list(range(len(axes)))[::-1]
    cut = value.shape.index(max(value.shape[:-1] or value.shape))
    edges = [0, *piece_ends(value.shape[cut], len(axes)), value.shape[cut]]
    gathered = []
    for k, (start, end) in enumerate(zip(edges, edges[1:])):
        if end > start:
            slab = lax.slice_in_dim(value, start, end, axis=cut)
            gathered.append(all_blocks(slab, axes, numbers[k:] + numbers[:k]))
    return laid_out(jnp.concatenate(gathered, axis=cut + 1), dim)


def by_axis(value, axes):
    for axis in axes:
        value = lax.psum(value, axis)
    return value


def tile_scores(left_low, piece):
    return (
        lax.dot_general(
            left_low, piece, (((1,), (1,)), ((), ())), preferred_element_type=jnp.float32
        )
        / TAU
    )


def local_fold(fn, init, gathered, width):
    blocks = gathered.shape[0] // width

    def step(index, carry):
        start = (index * width).astype(jnp.int32)
        piece = lax.dynamic_slice_in_dim(gathered, start, width, 0)
        return fn(carry, piece, start)

    return lax.fori_loop(0, blocks, step, init)


def make_forward(left_low, row_ids, mates, column_ids):

    def forward_step(carry, piece, start):
        total, pos = carry
        score = tile_scores(left_low, piece)
        cols = column_ids(start, piece.shape[0])
        diag = cols[None, :] == row_ids[:, None]
        hit = cols[None, :] == mates[:, None]
        total = total + jnp.sum(jnp.where(diag, 0.0, jnp.exp(score - SHIFT)), axis=1)
        pos = pos + jnp.sum(jnp.where(hit, score, 0.0), axis=1)
        return (total, pos)

    return forward_step


def make_backward(left_low, row_ids, mates, column_ids, lse_rows, lse_cols):

    def backward_step(carry, piece, start):
        score = tile_scores(left_low, piece)
        count = piece.shape[0]
        cols = column_ids(start, count)
        diag = cols[None, :] == row_ids[:, None]
        hit = cols[None, :] == mates[:, None]
        lse_piece = lax.dynamic_slice_in_dim(lse_cols, start, count, 0)
        weight = jnp.exp(score - lse_rows[:, None]) + jnp.exp(score - lse_piece[None, :])
        weight = weight - 2.0 * hit.astype(jnp.float32)
        weight = jnp.where(diag, 0.0, weight / TAU).astype(jnp.bfloat16)
        return carry + jnp.dot(weight, piece, preferred_element_type=jnp.float32)

    return backward_step


def body(projections, partner):
    vrows = projections.shape[0]
    width_d = projections.shape[1]
    groups = lax.axis_size(DP_SUB)
    views_all = vrows * groups
    inverse = lax.rsqrt(jnp.sum(projections * projections, axis=1) + 1e-06)
    unit = projections * inverse[:, None]
    unit_low = unit.astype(jnp.bfloat16)
    rows = lax.axis_index(DP_SUB) * vrows + jnp.arange(vrows, dtype=jnp.int32)

    def plain_ids(start, count):
        return start + jnp.arange(count, dtype=jnp.int32)

    forward_step = make_forward(unit_low, rows, partner, plain_ids)
    empty = jnp.zeros((vrows,), jnp.float32)
    width = vrows * 16
    gathered = gather_at_once(unit_low, DP_SUB, 0)
    total, pos = local_fold(forward_step, (empty, empty), gathered, width)
    lse = jnp.log(total) + SHIFT
    row_loss = lse - pos
    lse_all = lax.all_gather(lse, DP_SUB, axis=0, tiled=True)
    loss = by_axis(jnp.sum(row_loss), DP_SUB) / views_all
    backward_step = make_backward(unit_low, rows, partner, plain_ids, lse, lse_all)
    start_grad = jnp.zeros((vrows, width_d), jnp.float32)
    grad_unit = local_fold(backward_step, start_grad, gathered, width)
    inner = jnp.sum(unit * grad_unit, axis=1)
    grad = inverse[:, None] * (grad_unit - unit * inner[:, None])
    return (loss, grad)


def solution(mesh):
    finer = Mesh(
        mesh.devices.reshape(4, 4, 4, 2, mesh.shape["sub"]), ("dp_0", "dp_1", "dp_2", "dp_3", "sub")
    )
    in_specs = (P(DP_SUB, None), P(DP_SUB))
    out_specs = (P(), P(DP_SUB, None))
    return jax.shard_map(body, mesh=finer, in_specs=in_specs, out_specs=out_specs, check_vma=False)
```

profile of v0, /device:TPU:2, one launch (start us, length us, event | category | flops | bytes accessed | tf_op | source)
XLA Modules:
  0.0 717.1 jit_solution(9662809372564612045)
XLA Ops:
  9.2 14.0 %all-gather.2 = bf16[160,128]{1,0:T(8,128)(2,1)S(1)} all-gather(bf16[40,128]{1,0:T(8,128)(2,1)S(1)} %get-tuple-element.414), channel_id=4, replica_groups=mesh['dp_0'=4,'dp_1'=4,'dp_2'=4,'dp_3'=2,'sub'=2] {'dp_2'}, dimensions={0}, use_global_device_ids=true | all-gather | bytes 51200 | tf_op jit(solution)/shard_map/all_gather | solution.py:22
  23.3 12.6 %all_gather.89 = bf16[16,40,128]{2,1,0:T(8,128)(2,1)S(1)} all-gather(bf16[4,40,128]{2,1,0:T(8,128)(2,1)S(1)} %bitcast.53), channel_id=1, replica_groups=mesh['dp_0'=4,'dp_1'=4,'dp_2'=4,'dp_3'=2,'sub'=2] {'dp_1'}, dimensions={0}, use_global_device_ids=true | all-gather | bytes 204800 | tf_op jit(solution)/shard_map/all_gather | solution.py:22
  35.9 13.8 %all_gather.90 = bf16[64,40,128]{2,1,0:T(8,128)(2,1)} all-gather(bf16[16,40,128]{2,1,0:T(8,128)(2,1)S(1)} %all_gather.89), channel_id=1, replica_groups=mesh['dp_0'=4,'dp_1'=4,'dp_2'=4,'dp_3'=2,'sub'=2] {'dp_0'}, dimensions={0}, use_global_device_ids=true | all-gather | bytes 819200 | tf_op jit(solution)/shard_map/all_gather | solution.py:22
  51.6 13.3 %all_gather.84 = bf16[8,40,128]{2,1,0:T(8,128)(2,1)S(1)} all-gather(bf16[2,40,128]{2,1,0:T(8,128)(2,1)S(1)} %bitcast.56), channel_id=1, replica_groups=mesh['dp_0'=4,'dp_1'=4,'dp_2'=4,'dp_3'=2,'sub'=2] {'dp_2'}, dimensions={0}, use_global_device_ids=true | all-gather | bytes 102400 | tf_op jit(solution)/shard_map/all_gather | solution.py:22
  64.8 13.4 %all_gather.85 = bf16[32,40,128]{2,1,0:T(8,128)(2,1)} all-gather(bf16[8,40,128]{2,1,0:T(8,128)(2,1)S(1)} %all_gather.84), channel_id=1, replica_groups=mesh['dp_0'=4,'dp_1'=4,'dp_2'=4,'dp_3'=2,'sub'=2] {'dp_1'}, dimensions={0}, use_global_device_ids=true | all-gather | bytes 409600 | tf_op jit(solution)/shard_map/all_gather | solution.py:22
  78.3 8.8 %all-gather = bf16[64,128]{1,0:T(8,128)(2,1)S(1)} all-gather(bf16[32,128]{1,0:T(8,128)(2,1)S(1)} %slice.20), channel_id=2, replica_groups=mesh['dp_0'=4,'dp_1'=4,'dp_2'=4,'dp_3'=2,'sub'=2] {'sub'}, dimensions={0}, use_global_device_ids=true | all-gather | bytes 24576 | tf_op jit(solution)/shard_map/all_gather | solution.py:22
  89.0 15.7 %all_gather.80 = bf16[16,32,128]{2,1,0:T(8,128)(2,1)S(1)} all-gather(bf16[4,32,128]{2,1,0:T(8,128)(2,1)S(1)} %all_gather.79), channel_id=1, replica_groups=mesh['dp_0'=4,'dp_1'=4,'dp_2'=4,'dp_3'=2,'sub'=2] {'dp_2'}, dimensions={0}, use_global_device_ids=true | all-gather | bytes 163840 | tf_op jit(solution)/shard_map/all_gather | solution.py:22
  104.6 14.2 %all_gather.81 = bf16[64,32,128]{2,1,0:T(8,128)(2,1)} all-gather(bf16[16,32,128]{2,1,0:T(8,128)(2,1)S(1)} %all_gather.80), channel_id=1, replica_groups=mesh['dp_0'=4,'dp_1'=4,'dp_2'=4,'dp_3'=2,'sub'=2] {'dp_1'}, dimensions={0}, use_global_device_ids=true | all-gather | bytes 655360 | tf_op jit(solution)/shard_map/all_gather | solution.py:22
  119.4 11.9 %all-gather.3 = bf16[160,128]{1,0:T(8,128)(2,1)S(1)} all-gather(bf16[40,128]{1,0:T(8,128)(2,1)S(1)} %get-tuple-element.413), channel_id=5, replica_groups=mesh['dp_0'=4,'dp_1'=4,'dp_2'=4,'dp_3'=2,'sub'=2] {'dp_1'}, dimensions={0}, use_global_device_ids=true | all-gather | bytes 51200 | tf_op jit(solution)/shard_map/all_gather | solution.py:22
  131.3 12.3 %all_gather.94 = bf16[16,40,128]{2,1,0:T(8,128)(2,1)S(1)} all-gather(bf16[4,40,128]{2,1,0:T(8,128)(2,1)S(1)} %bitcast.54), channel_id=1, replica_groups=mesh['dp_0'=4,'dp_1'=4,'dp_2'=4,'dp_3'=2,'sub'=2] {'dp_0'}, dimensions={0}, use_global_device_ids=true | all-gather | bytes 204800 | tf_op jit(solution)/shard_map/all_gather | solution.py:22
  143.7 11.6 %all_gather.95 = bf16[32,40,128]{2,1,0:T(8,128)(2,1)S(1)} all-gather(bf16[16,40,128]{2,1,0:T(8,128)(2,1)S(1)} %all_gather.94), channel_id=1, replica_groups=mesh['dp_0'=4,'dp_1'=4,'dp_2'=4,'dp_3'=2,'sub'=2] {'sub'}, dimensions={0}, use_global_device_ids=true | all-gather | bytes 491520 | tf_op jit(solution)/shard_map/all_gather | solution.py:22
  155.3 2.4 all_gather.96
  157.8 11.8 %all-gather.4 = bf16[160,128]{1,0:T(8,128)(2,1)S(1)} all-gather(bf16[40,128]{1,0:T(8,128)(2,1)S(1)} %get-tuple-element.412), channel_id=6, replica_groups=mesh['dp_0'=4,'dp_1'=4,'dp_2'=4,'dp_3'=2,'sub'=2] {'dp_0'}, dimensions={0}, use_global_device_ids=true | all-gather | bytes 51200 | tf_op jit(solution)/shard_map/all_gather | solution.py:22
  169.6 8.6 %all_gather.99 = bf16[8,40,128]{2,1,0:T(8,128)(2,1)S(1)} all-gather(bf16[4,40,128]{2,1,0:T(8,128)(2,1)S(1)} %bitcast.55), channel_id=1, replica_groups=mesh['dp_0'=4,'dp_1'=4,'dp_2'=4,'dp_3'=2,'sub'=2] {'sub'}, dimensions={0}, use_global_device_ids=true | all-gather | bytes 122880 | tf_op jit(solution)/shard_map/all_gather | solution.py:22
  180.1 18.3 %all_gather.101 = bf16[64,40,128]{2,1,0:T(8,128)(2,1)} all-gather(bf16[16,40,128]{2,1,0:T(8,128)(2,1)S(1)} %all_gather.100), channel_id=1, replica_groups=mesh['dp_0'=4,'dp_1'=4,'dp_2'=4,'dp_3'=2,'sub'=2] {'dp_2'}, dimensions={0}, use_global_device_ids=true | all-gather | bytes 819200 | tf_op jit(solution)/shard_map/all_gather | solution.py:22
  199.3 3.5 constant_dynamic-update-slice_fusion.4
  202.8 2.4 copy.9
  205.2 35.6 %all-gather.23.cloned.1.call-done = bf16[256,40,128]{2,1,0:T(8,128)(2,1)} async-done(((bf16[64,40,128]{2,1,0:T(8,128)(2,1)}), bf16[256,40,128]{2,1,0:T(8,128)(2,1)}) %all-gather.23.cloned.1.call-update) | async-done | bytes 2621456 | tf_op jit(solution)/shard_map/all_gather | solution.py:22
  240.8 3.9 copy.10
  244.7 35.4 %all-gather.25.cloned.1.call-done = bf16[256,40,128]{2,1,0:T(8,128)(2,1)} async-done(((bf16[64,40,128]{2,1,0:T(8,128)(2,1)}), bf16[256,40,128]{2,1,0:T(8,128)(2,1)}) %all-gather.25.cloned.1.call-update) | async-done | bytes 2621456 | tf_op jit(solution)/shard_map/all_gather | solution.py:22
  280.1 3.9 copy.11
  284.0 74.9 %all-gather.17.cloned.1.call-done = bf16[256,40,128]{2,1,0:T(8,128)(2,1)} async-done(((bf16[128,40,128]{2,1,0:T(8,128)(2,1)}), bf16[256,40,128]{2,1,0:T(8,128)(2,1)}) %all-gather.17.cloned.1.call-update) | async-done | bytes 2621456 | tf_op jit(solution)/shard_map/all_gather | solution.py:22
  358.9 2.2 copy.8
  363.2 2.3 constant_dynamic-update-slice_fusion.2
  370.3 35.9 %while.32 = (s32[]{:T(128)}, f32[192]{0:T(256)S(1)}, f32[192]{0:T(256)S(1)}, bf16[49152,128]{1,0:T(8,128)(2,1)}, bf16[192,128]{1,0:T(8,128)(2,1)S(1)}, /*index=5...) while((s32[]{:T(128)}, f32[192]{0:T(256)S(1)}, ...), condition=%wide.region_4.5_spmd.clone, body=%wide.region_1.4_spmd.clone.sunk | while | flops 155717184 | bytes 868785 | solution.py:70
  370.4 2.2 select_reduce_fusion.3
  372.6 2.2 select_reduce_fusion.3
  374.9 2.2 select_reduce_fusion.3
  377.1 2.2 select_reduce_fusion.3
  379.4 2.2 select_reduce_fusion.3
  381.6 2.2 select_reduce_fusion.3
  383.8 2.2 select_reduce_fusion.3
  386.1 2.2 select_reduce_fusion.3
  388.3 2.2 select_reduce_fusion.3
  390.6 2.2 select_reduce_fusion.3
  392.8 2.2 select_reduce_fusion.3
  395.1 2.2 select_reduce_fusion.3
  397.3 2.2 select_reduce_fusion.3
  399.6 2.2 select_reduce_fusion.3
  401.8 2.2 select_reduce_fusion.3
  404.1 2.2 select_reduce_fusion.3
  407.7 9.2 %psum.35 = f32[]{:T(128)} all-reduce(f32[]{:T(128)} %get-tuple-element.417), channel_id=1, replica_groups=mesh['dp_0'=4,'dp_1'=4,'dp_2'=4,'dp_3'=2,'sub'=2] {'dp_0'}, use_global_device_ids=true, to_apply=%region_6.7 | all-reduce | flops 1 | bytes 8 | tf_op jit(solution)/shard_map/psum | solution.py:49
  417.0 11.1 %psum.36 = f32[]{:T(128)} all-reduce(f32[]{:T(128)} %psum.35), channel_id=1, replica_groups=mesh['dp_0'=4,'dp_1'=4,'dp_2'=4,'dp_3'=2,'sub'=2] {'dp_1'}, use_global_device_ids=true, to_apply=%region_7.8 | all-reduce | flops 1 | bytes 8 | tf_op jit(solution)/shard_map/psum | solution.py:49
  428.1 9.2 %psum.37 = f32[]{:T(128)} all-reduce(f32[]{:T(128)} %psum.36), channel_id=1, replica_groups=mesh['dp_0'=4,'dp_1'=4,'dp_2'=4,'dp_3'=2,'sub'=2] {'dp_2'}, use_global_device_ids=true, to_apply=%region_8.9 | all-reduce | flops 1 | bytes 8 | tf_op jit(solution)/shard_map/psum | solution.py:49
  437.3 3.1 psum.38
  440.4 9.5 %psum.39 = f32[]{:T(128)} all-reduce(f32[]{:T(128)} %psum.38), channel_id=1, replica_groups=mesh['dp_0'=4,'dp_1'=4,'dp_2'=4,'dp_3'=2,'sub'=2] {'sub'}, use_global_device_ids=true, to_apply=%region_10.11 | all-reduce | flops 1 | bytes 8 | tf_op jit(solution)/shard_map/psum | solution.py:49
  450.5 199.7 %all-reduce.3.cloned.1.call-done = f32[49152]{0:T(1024)} async-done(((f32[49152]{0:T(1024)}), f32[49152]{0:T(1024)}) %all-reduce.3.cloned.1.call-update) | async-done | bytes 196624
  650.2 57.9 %while.33 = (s32[]{:T(128)}, f32[192,128]{1,0:T(8,128)S(1)}, bf16[49152,128]{1,0:T(8,128)(2,1)}, bf16[192,128]{1,0:T(8,128)(2,1)S(1)}, f32[192]{0:T(256)S(1)}, /...) while((s32[]{:T(128)}, f32[192,128]{1,0:T(8,128)S(1)}, ...), condition=%wide.region_12.13_spmd.clone, body=%wide.region_11.12_spmd.clone.sunk | while | flops 308530368 | bytes 1884856 | solution.py:70
  651.0 2.8 fusion.41
  654.6 2.9 fusion.41
  658.2 2.8 fusion.41
  661.7 2.9 fusion.41
  665.4 2.8 fusion.41
  669.0 2.8 fusion.41
  672.5 2.9 fusion.41
  676.2 2.9 fusion.41
  679.9 2.9 fusion.41
  683.5 2.9 fusion.41
  687.1 2.9 fusion.41
  690.8 2.9 fusion.41
  694.5 2.8 fusion.41
  698.1 2.8 fusion.41
  701.6 2.9 fusion.41
  705.2 2.9 fusion.41
  (144 shorter events, 30.5 us)
Async XLA Ops:
  7.2 111.7 %all-gather.19.cloned.1.call-start = ((), (), s32[]{:S(2)}) async-start(), calls=%async_computation.3 | async-start | bytes 1966080 | tf_op jit(solution)/shard_map/all_gather | solution.py:22
  49.7 148.8 %all-gather.15.cloned.1.call-start = ((), (), s32[]{:S(2)}) async-start(), calls=%async_computation.1 | async-start | bytes 1638400 | tf_op jit(solution)/shard_map/all_gather | solution.py:22
  78.3 121.1 %all-gather.13.cloned.1.call-start = ((), (), s32[]{:S(2)}) async-start(), calls=%async_computation | async-start | bytes 2621440 | tf_op jit(solution)/shard_map/all_gather | solution.py:22
  118.8 84.0 %all-gather.21.cloned.1.call-start = ((), (), s32[]{:S(2)}) async-start(), calls=%async_computation.4 | async-start | bytes 3932160 | tf_op jit(solution)/shard_map/all_gather | solution.py:22
  119.4 121.4 %all-gather.23.cloned.1.call-start = ((), (), s32[]{:S(2)}) async-start(), calls=%async_computation.5 | async-start | bytes 3276800 | tf_op jit(solution)/shard_map/all_gather | solution.py:22
  157.7 122.3 %all-gather.25.cloned.1.call-start = ((), (), s32[]{:S(2)}) async-start(), calls=%async_computation.6 | async-start | bytes 3276800 | tf_op jit(solution)/shard_map/all_gather | solution.py:22
  198.5 160.4 %all-gather.17.cloned.1.call-start = ((), (), s32[]{:S(2)}) async-start(), calls=%async_computation.2 | async-start | bytes 3932160 | tf_op jit(solution)/shard_map/all_gather | solution.py:22
  199.2 451.0 %all-reduce.3.cloned.1.call-start = ((), (), s32[]{:S(2)}) async-start(), calls=%async_computation.7 | async-start | bytes 393216
  363.2 2.5 copy-start
  365.7 2.5 copy-start.1
  368.3 2.1 copy-start.4
  407.0 0.7 copy-start.3
  650.2 57.9 %copy-start.2 = (f32[192,128]{1,0:T(8,128)S(1)}, f32[192,128]{1,0:T(8,128)}, u32[]{:S(2)}) copy-start(f32[192,128]{1,0:T(8,128)} %param.6) | copy-start | bytes 294916
Sparse Core Ops, SparseCore 0:
  49.8 49.2 all-gather.18
  100.9 23.0 all-gather.14
  125.8 34.1 all-gather.12
  161.6 17.5 all-gather.20
  180.9 59.9 all-gather.22
  242.5 37.5 all-gather.24
  281.9 76.9 all-gather.16
  407.9 242.3 all-reduce.2
where the time goes:
time: 721 us; the launch traced here: 717 us
  waiting for transfers between devices  347 us (48%)
  blocking collectives  230 us (32%)
  matrix products  80.8 us (11%)
  local copies, waits for them, and re-layouts  37.2 us (5%)
  between operations  16.1 us (2%)
    unnamed x9, waiting for transfers between devices  201 us
    all_gather x18, blocking collectives, all_blocks(): pieces = lax.all_gather(pieces, axes[k], axis=0, tiled=True)  188 us
    all_gather x7, waiting for transfers between devices, all_blocks(): pieces = lax.all_gather(pieces, axes[k], axis=0, tiled=True)  146 us
    dot_general x16, matrix products, backward_step(): return carry + jnp.dot(weight, piece, preferred_element_type=jnp.float32)  45.9 us
    psum x5, blocking collectives, by_axis(): value = lax.psum(value, axis)  42.1 us
    dot_general x16, matrix products, tile_scores(): lax.dot_general(left_low, piece, (((1,), (1,)), ((), ())), preferred_elem...  34.9 us
  transfers between devices with their start and end apart: 8, of which 4 were waited for; matrix products, arithmetic and copies ran while one was open for 2% of the time, Pallas kernels for 0%

commit v1 on v0

v1 whole, which is shorter than its diff:
```python
import jax
import jax.numpy as jnp
from jax import lax
from jax.experimental import pallas as pl
from jax.experimental.pallas import tpu as pltpu
from jax.sharding import Mesh
from jax.sharding import PartitionSpec as P

AXES = ("x", "y", "zl", "c", "zh")
XY = ("x", "y")
Z = ("zl", "zh")
EPS = 1e-06
LOG2E=1.4426950408889634
TAU=0.1
KS=LOG2E/TAU
SH=192; PADR=208; NB=16; NA=16; C=NA*SH; CH=256; NCH=C//CH

def col_bcast(row):
    return jnp.transpose(jnp.broadcast_to(row,(128,row.shape[1])))

def mates_of(rows_ref, sh):
    code = rows_ref[sh, SH:PADR, :].astype(jnp.float32)
    lo = code[2:4]*1.0
    m = code[0:2]*256.0 + code[2:4]
    a = col_bcast(m[0:1])
    b = col_bcast(m[1:2])[:SH-128]
    return jnp.concatenate([a,b],axis=0)

def k1_body(own_ref, rows_ref, cols_ref, colid_ref, trow_ref, tcol_ref, colsT, cacc, pacc, tr):
    for c in range(NCH):
        colsT[:, c*CH:(c+1)*CH] = jnp.transpose(cols_ref[c*CH:(c+1)*CH, :])
    cacc[...] = jnp.zeros_like(cacc); pacc[...] = jnp.zeros_like(pacc)
    b = own_ref[0]; own_off = own_ref[1]
    def shard(sh, masked):
        u = rows_ref[sh, 0:SH, :]
        mates = mates_of(rows_ref, sh)
        racc = jnp.zeros((SH,128), jnp.float32)
        for c in range(NCH):
            s = jnp.dot(u, colsT[:, c*CH:(c+1)*CH], preferred_element_type=jnp.float32)
            e = jnp.exp2(s*KS)
            if masked:
                cidx = lax.broadcasted_iota(jnp.int32,(SH,CH),1)+c*CH-own_off
                ridx = lax.broadcasted_iota(jnp.int32,(SH,CH),0)
                e = jnp.where(cidx==ridx, 0.0, e)
            racc = racc + e[:, :128] + e[:, 128:]
            cacc[:, c*CH:(c+1)*CH] += jnp.sum(e.reshape(SH//8,8,CH),axis=0)
            cid = colid_ref[c:c+1, :]
            h0 = jnp.where(mates==cid[:, :128], s[:, :128], 0.0)
            h1 = jnp.where(mates==cid[:, 128:], s[:, 128:], 0.0)
            pacc[...] += jnp.sum((h0+h1).reshape(SH//8,8,128),axis=0)
        t = jnp.sum(jnp.transpose(racc), axis=0, keepdims=True)
        tr[pl.ds(sh,1), 0:SH] = t
    tr[...] = jnp.ones_like(tr)
    shard(b, True)
    def step(k,_):
        shard((b+k) & (NB-1), False); return 0
    lax.fori_loop(1, NB, step, 0)
    for d in range(NB):
        trow_ref[d] = tr[...]
    tc=jnp.zeros((16,CH),jnp.float32)
    rows=[jnp.sum(cacc[:, c*CH:(c+1)*CH],axis=0,keepdims=True) for c in range(NCH)]
    ps=jnp.sum(pacc[...],axis=0,keepdims=True)
    rows.append(jnp.concatenate([ps,jnp.zeros_like(ps)],axis=1))
    rows.append(jnp.zeros((3,CH),jnp.float32))
    tc=jnp.concatenate(rows,axis=0)
    for d in range(tcol_ref.shape[0]):
        tcol_ref[d]=tc

def k1(own, rows, cols, colid, dup_c=NA):
    return pl.pallas_call(k1_body,
      out_shape=(jax.ShapeDtypeStruct((NB,16,256),jnp.float32),jax.ShapeDtypeStruct((dup_c,16,CH),jnp.float32)),
      in_specs=[pl.BlockSpec(memory_space=pltpu.SMEM)]+[pl.BlockSpec(memory_space=pltpu.VMEM)]*3,
      out_specs=(pl.BlockSpec(memory_space=pltpu.VMEM),)*2,
      scratch_shapes=[pltpu.VMEM((128,C),jnp.bfloat16),pltpu.VMEM((8,C),jnp.float32),pltpu.VMEM((8,128),jnp.float32),pltpu.VMEM((16,256),jnp.float32)],
      compiler_params=pltpu.CompilerParams(vmem_limit_bytes=40<<20))(own,rows,cols,colid)

def k2_body(own_ref, rows_ref, cols_ref, colid_ref, trow_ref, tcol_ref, g_ref, colsT, rrow, rcol):
    for c in range(NCH):
        colsT[:, c*CH:(c+1)*CH] = jnp.transpose(cols_ref[c*CH:(c+1)*CH, :])
    b = own_ref[0]; own_off = own_ref[1]
    T=trow_ref[0]
    for d in range(1,trow_ref.shape[0]): T=T+trow_ref[d]
    rrow[...]=(1.0/TAU)/T
    Tc=tcol_ref[0]
    for d in range(1,tcol_ref.shape[0]): Tc=Tc+tcol_ref[d]
    rid=lax.broadcasted_iota(jnp.int32,(16,CH),0)
    isT=rid<NCH
    Ts=jnp.where(isT,Tc,1.0)
    rcol[...]=(1.0/TAU)/Ts
    S=jnp.where(isT,jnp.log(Ts),jnp.where(rid==NCH,Tc*(-1.0/TAU),0.0))
    Sv=S[0:8]+S[8:16]
    Sv=Sv[:, :128]+Sv[:, 128:]
    for d in range(NB):
        g_ref[d, SH:SH+8, :]=Sv
    def shard(sh, masked):
        u = rows_ref[sh, 0:SH, :]
        mates = mates_of(rows_ref, sh)
        ri = col_bcast(rrow[pl.ds(sh,1), 0:SH])
        acc = jnp.zeros((SH,128), jnp.float32)
        for c in range(NCH):
            s = jnp.dot(u, colsT[:, c*CH:(c+1)*CH], preferred_element_type=jnp.float32)
            e = jnp.exp2(s*KS)
            cid = colid_ref[c:c+1, :]; rj=rcol[c:c+1, :]
            ws=[]
            for l in (0,128):
                w = e[:, l:l+128]*(ri+rj[:, l:l+128])
                w = jnp.where(mates==cid[:, l:l+128], w-2.0/TAU, w)
                if masked:
                    cidx = lax.broadcasted_iota(jnp.int32,(SH,128),1)+(c*CH+l)-own_off
                    ridx = lax.broadcasted_iota(jnp.int32,(SH,128),0)
                    w = jnp.where(cidx==ridx, 0.0, w)
                ws.append(w.astype(jnp.bfloat16))
            w=jnp.concatenate(ws,axis=1)
            acc = acc + jnp.dot(w, cols_ref[c*CH:(c+1)*CH, :], preferred_element_type=jnp.float32)
        g_ref[sh, 0:SH, :] = acc
    shard(b, True)
    def step(k,_):
        shard((b+k) & (NB-1), False); return 0
    lax.fori_loop(1, NB, step, 0)

def k2(own, rows, cols, colid, trow, tcol):
    return pl.pallas_call(k2_body,
      out_shape=jax.ShapeDtypeStruct((NB,SH+8,128),jnp.float32),
      in_specs=[pl.BlockSpec(memory_space=pltpu.SMEM)]+[pl.BlockSpec(memory_space=pltpu.VMEM)]*5,
      out_specs=pl.BlockSpec(memory_space=pltpu.VMEM),
      scratch_shapes=[pltpu.VMEM((128,C),jnp.bfloat16),pltpu.VMEM((16,256),jnp.float32),pltpu.VMEM((16,CH),jnp.float32)],
      compiler_params=pltpu.CompilerParams(vmem_limit_bytes=40<<20))(own,rows,cols,colid,trow,tcol)


def inverse_norm(p):
    return lax.rsqrt(jnp.sum(p * p, axis=1, keepdims=True) + EPS)


def prep_body(p_ref, mate_ref, pay_ref, zpay_ref):
    p = p_ref[...]
    low = (p * inverse_norm(p)).astype(jnp.bfloat16)
    m = mate_ref[...]
    hi = (m >> 8).astype(jnp.float32)
    lo = (m & 255).astype(jnp.float32)
    code = jnp.concatenate([hi, lo, jnp.zeros((12, 128), jnp.float32)], axis=0).astype(jnp.bfloat16)
    for d in range(pay_ref.shape[0]):
        pay_ref[d, 0:SH, :] = low
        pay_ref[d, SH:PADR, :] = code
    for d in range(zpay_ref.shape[0]):
        zpay_ref[d] = low


def prep(p, mate):
    return pl.pallas_call(
        prep_body,
        out_shape=(
            jax.ShapeDtypeStruct((NB, PADR, 128), jnp.bfloat16),
            jax.ShapeDtypeStruct((8, SH, 128), jnp.bfloat16),
        ),
        in_specs=[pl.BlockSpec(memory_space=pltpu.VMEM)] * 2,
        out_specs=(pl.BlockSpec(memory_space=pltpu.VMEM),) * 2,
    )(p, mate)


def final_body(p_ref, g_ref, loss_ref, grad_ref):
    p = p_ref[...]
    inv = inverse_norm(p)
    unit = p * inv
    g = g_ref[0]
    for d in range(1, NB):
        g = g + g_ref[d]
    loss_ref[0, 0] = jnp.sum(g[SH:]) / (NA * NB * SH)
    gu = g[:SH]
    inner = jnp.sum(unit * gu, axis=1, keepdims=True)
    grad_ref[...] = inv * (gu - unit * inner)


def final(p, g):
    return pl.pallas_call(
        final_body,
        out_shape=(
            jax.ShapeDtypeStruct((1, 1), jnp.float32),
            jax.ShapeDtypeStruct((SH, 128), jnp.float32),
        ),
        in_specs=[pl.BlockSpec(memory_space=pltpu.VMEM)] * 2,
        out_specs=(pl.BlockSpec(memory_space=pltpu.SMEM), pl.BlockSpec(memory_space=pltpu.VMEM)),
    )(p, g)


def body(projections, partner):
    xy = lax.axis_index(XY)
    own_a = lax.axis_index(("c", "zl", "zh"))
    mate = jnp.pad(partner, (0, 64)).reshape(2, 128)
    pay, zpay = prep(projections, mate)
    rows = lax.all_to_all(pay, XY, 0, 0)
    zg = lax.all_to_all(zpay, Z, 0, 0)
    cols = lax.all_gather(zg, "c").reshape(C, 128)
    own = jnp.stack([xy, own_a * SH]).astype(jnp.int32)
    p = jnp.arange(16 * CH, dtype=jnp.int32)
    k = p // SH
    shard = ((k % 8) // 2) * 4 + (k // 8) * 2 + k % 2
    colid = ((xy * NA + shard) * SH + p % SH).astype(jnp.float32).reshape(16, CH)
    trow, tcol = k1(own, rows, cols, colid)
    trow = lax.all_to_all(trow, XY, 0, 0)
    tcol = lax.all_to_all(tcol, ("zl", "c", "zh"), 0, 0)
    g = k2(own, rows, cols, colid, trow, tcol)
    g = lax.all_to_all(g, XY, 0, 0)
    loss, grad = final(projections, g)
    return (loss[0, 0], grad)


def solution(mesh):
    finer = Mesh(mesh.devices.reshape(4, 4, 4, 2, mesh.shape["sub"]), AXES)
    in_specs = (P(AXES, None), P(AXES))
    out_specs = (P(), P(AXES, None))
    return jax.shard_map(body, mesh=finer, in_specs=in_specs, out_specs=out_specs, check_vma=False)
```

time: 721 us -> 136 us (0.19)
  waiting for transfers between devices: 347 us -> 7.48 us
  blocking collectives: 230 us -> 81.8 us
  matrix products: 80.8 us -> 0 us
  Pallas kernels: 0 us -> 36.7 us
  local copies, waits for them, and re-layouts: 37.2 us -> 1.24 us
  between operations: 16.1 us -> 0.65 us
    unnamed x9 -> x0, waiting for transfers between devices: 201 us -> none
    all_gather x18 -> x1, blocking collectives: 188 us -> 2.37 us  [body(): cols = lax.all_gather(zg, 'c').reshape(C, 128)]
    all_gather x7 -> x0, waiting for transfers between devices: 146 us -> none  [all_blocks(): pieces = lax.all_gather(pieces, axes[k], axis=0, tiled=True)]
    dot_general x32 -> x0, matrix products: 80.8 us -> none  [the longest x16 45.9 us: backward_step(): return carry + jnp.dot(weight, piece, preferred_element_type=jnp.float32)]
    all_to_all x0 -> x4, blocking collectives: none -> 79.5 us  [the longest x1 27 us: body(): g = lax.all_to_all(g, XY, 0, 0)]
    psum x5 -> x0, blocking collectives: 42.1 us -> none  [by_axis(): value = lax.psum(value, axis)]
    pallas_call x0 -> x4, Pallas kernels: none -> 36.7 us  [the longest x1 18 us: k2(): pl.pallas_call(k2_body, out_shape=jax.ShapeDtypeStruct((NB, SH + 8, 128),...]
    transpose x4 -> x0, local copies, waits for them, and re-layouts: 12.3 us -> none  [all_blocks(): pieces.transpose(*turned, *range(len(turns), pieces.ndim))]
  transfers between devices with their start and end apart: 8 -> 1, of which waited for: 4 -> 1; matrix products, arithmetic and copies ran while one was open for 2% -> 0% of each run, Pallas kernels for 0% -> 0%
where the time goes in v1:
time: 136 us
  blocking collectives  81.8 us (60%)
  Pallas kernels  36.7 us (27%)
  starting transfers between devices  7.48 us (6%)
  waiting for transfers between devices  7.48 us (6%)
    all_to_all x1, blocking collectives, body(): g = lax.all_to_all(g, XY, 0, 0)  27 us
    all_to_all x1, blocking collectives, body(): zg = lax.all_to_all(zpay, Z, 0, 0)  21.6 us
    all_to_all x1, blocking collectives, body(): tcol = lax.all_to_all(tcol, ('zl', 'c', 'zh'), 0, 0)  18.6 us
    pallas_call x1, Pallas kernels, k2(): pl.pallas_call(k2_body, out_shape=jax.ShapeDtypeStruct((NB, SH + 8, 128),...  18 us
    pallas_call x1, Pallas kernels, k1(): pl.pallas_call(k1_body, out_shape=(jax.ShapeDtypeStruct((NB, 16, 256), jn...  14.3 us
    all_to_all x1, blocking collectives, body(): trow = lax.all_to_all(trow, XY, 0, 0)  12.3 us
    all_to_all x1, starting transfers between devices, body(): rows = lax.all_to_all(pay, XY, 0, 0)  7.48 us
    all_to_all x1, waiting for transfers between devices, body(): rows = lax.all_to_all(pay, XY, 0, 0)  7.48 us
  transfers between devices with their start and end apart: 1, of which 1 were waited for; matrix products, arithmetic and copies ran while one was open for 0% of the time, Pallas kernels for 0%

profile of v1, /device:TPU:2, one launch (start us, length us, event | category | flops | bytes accessed | tf_op | source)
XLA Modules:
  0.0 135.6 jit_solution(2170767424510015084)
XLA Ops:
  0.6 1.2 pad_bitcast_fusion.mate_ref
  1.9 2.1 %shard_map.41 = (bf16[16,208,128]{2,1,0:T(8,128)(2,1)}, bf16[8,192,128]{2,1,0:T(8,128)(2,1)}) custom-call(f32[192,128]{1,0:T(8,128)} %p_ref.3, s32[2,128]{1,0:T(2,128)} %pad_bitcast_fusion.mate_ref), custom_call_target="tpu_custom_call" | custom-call | tf_op jit(solution)/shard_map/pallas_call | solution.py:149
  4.0 21.6 %all_to_all.25 = bf16[8,192,128]{2,1,0:T(8,128)(2,1)S(1)} all-to-all(bf16[8,192,128]{2,1,0:T(8,128)(2,1)} %get-tuple-element.9), channel_id=1, replica_groups=mesh['x'=4,'y'=4,'zl'=4,'c'=2,'zh'=2] {'zl','zh'}, dimensions={0} | all-to-all | bytes 786432 | tf_op jit(solution)/shard_map/all_to_all | solution.py:191
  25.6 7.5 %all-to-all-start = ((bf16[16,208,128]{2,1,0:T(8,128)(2,1)}), bf16[16,208,128]{2,1,0:T(8,128)(2,1)S(1)}, u32[]{:S(2)}, u32[]{:S(2)}) async-start(bf16[16,208,128]{2,1,0:T(8,128)(2,1)} %get-tuple-element.8), calls=%async_computation | async-start | bytes 1703936 | tf_op jit(solution)/shard_map/all_to_all | solution.py:190
  33.1 0.1 pad_add_fusion.own_ref
  33.2 0.1 fusion.7.colid_ref
  33.2 2.4 %all-gather = bf16[16,192,128]{2,1,0:T(8,128)(2,1)S(1)} all-gather(bf16[8,192,128]{2,1,0:T(8,128)(2,1)S(1)} %all_to_all.25), channel_id=2, replica_groups=mesh['x'=4,'y'=4,'zl'=4,'c'=2,'zh'=2] {'c'}, dimensions={0}, use_global_device_ids=true | all-gather | bytes 1179648 | tf_op jit(solution)/shard_map/all_gather | solution.py:192
  35.6 7.5 %all-to-all-done.rows_ref = bf16[16,208,128]{2,1,0:T(8,128)(2,1)S(1)} async-done(((bf16[16,208,128]{2,1,0:T(8,128)(2,1)}), bf16[16,208,128]{2,1,0:T(8,128)(2,1)S(1)}, u32[]{:S(2)}, u32[]{:S(2)}) %all-to-all-start) | async-done | bytes 852000 | tf_op jit(solution)/shard_map/all_to_all | solution.py:190
  43.1 14.3 %shard_map.42 = (f32[16,16,256]{2,1,0:T(8,128)S(1)}, f32[16,16,256]{2,1,0:T(8,128)S(1)}) custom-call(s32[2]{0:T(128)S(1)} %pad_add_fusion.own_ref, bf16[16,208,128]{2,1,0:T(8,128)(2,1)S(1)} %all-to-all-done.rows_ref, bf16[3072,128]{1,0:T(8,128)(2,1)S(1)} %bitcast.6, f32[16,256]{1,0:T(8,128)S(1)} %fusion.7.colid_ref), custom_call_target="tpu_custom_call" | custom-call | tf_op jit(solution)/shard_map/pallas_call | solution.py:70
  57.4 12.3 %all_to_all.26.trow_ref = f32[16,16,256]{2,1,0:T(8,128)S(1)} all-to-all(f32[16,16,256]{2,1,0:T(8,128)S(1)} %get-tuple-element.10), channel_id=1, replica_groups=mesh['x'=4,'y'=4,'zl'=4,'c'=2,'zh'=2] {'x','y'}, dimensions={0} | all-to-all | bytes 524288 | tf_op jit(solution)/shard_map/all_to_all | solution.py:199
  69.7 18.6 %all_to_all.27.tcol_ref = f32[16,16,256]{2,1,0:T(8,128)S(1)} all-to-all(f32[16,16,256]{2,1,0:T(8,128)S(1)} %get-tuple-element.11), channel_id=1, replica_groups=mesh['x'=4,'y'=4,'zl'=4,'c'=2,'zh'=2] {'zl','c','zh'}, dimensions={0} | all-to-all | bytes 524288 | tf_op jit(solution)/shard_map/all_to_all | solution.py:200
  88.3 18.0 %shard_map.43 = f32[16,200,128]{2,1,0:T(8,128)S(1)} custom-call(s32[2]{0:T(128)S(1)} %pad_add_fusion.own_ref, bf16[16,208,128]{2,1,0:T(8,128)(2,1)S(1)} %all-to-all-done.rows_ref, bf16[3072,128]{1,0:T(8,128)(2,1)S(1)} %bitcast.7, f32[16,256]{1,0:T(8,128)S(1)} %fusion.7.colid_ref, f32[16,16,256]{2,1,0:T(8,128)S(1)} %all_to_all.26.trow_ref, ...), custom_call_target="tpu_custom_call" | custom-call | tf_op jit(solution)/shard_map/pallas_call | solution.py:122
  106.2 27.0 %all_to_all.28.g_ref = f32[16,200,128]{2,1,0:T(8,128)} all-to-all(f32[16,200,128]{2,1,0:T(8,128)S(1)} %shard_map.43), channel_id=1, replica_groups=mesh['x'=4,'y'=4,'zl'=4,'c'=2,'zh'=2] {'x','y'}, dimensions={0} | all-to-all | bytes 3276800 | tf_op jit(solution)/shard_map/all_to_all | solution.py:202
  133.2 2.3 %shard_map.44 = (f32[1,1]{1,0:T(1,128)}, f32[192,128]{1,0:T(8,128)}) custom-call(f32[192,128]{1,0:T(8,128)} %p_ref.3, f32[16,200,128]{2,1,0:T(8,128)} %all_to_all.28.g_ref), custom_call_target="tpu_custom_call" | custom-call | tf_op jit(solution)/shard_map/pallas_call | solution.py:174
Async XLA Ops:
  25.6 17.5 %all-to-all-start = ((bf16[16,208,128]{2,1,0:T(8,128)(2,1)}), bf16[16,208,128]{2,1,0:T(8,128)(2,1)S(1)}, u32[]{:S(2)}, u32[]{:S(2)}) async-start(bf16[16,208,128]{2,1,0:T(8,128)(2,1)} %get-tuple-element.8), calls=%async_computation | async-start | bytes 1703936 | tf_op jit(solution)/shard_map/all_to_all | solution.py:190

commit v2 on v1

--- a/solution.py
+++ b/solution.py
@@ -8,7 +8,8 @@
 
 AXES = ("x", "y", "zl", "c", "zh")
 XY = ("x", "y")
-Z = ("zl", "zh")
+ZC = ("zl", "c", "zh")
+NZ = 8
 EPS = 1e-06
 LOG2E=1.4426950408889634
 TAU=0.1
@@ -26,7 +27,19 @@
     b = col_bcast(m[1:2])[:SH-128]
     return jnp.concatenate([a,b],axis=0)
 
-def k1_body(own_ref, rows_ref, cols_ref, colid_ref, trow_ref, tcol_ref, colsT, cacc, pacc, tr):
+def k1_body(own_ref, rows_ref, pair_ref, d1, d2, d3, s1, s2, s3, d4, s4, colid_ref, trow_ref, tcol_ref, cols_ref, colsT, cacc, pacc, tr):
+    z = own_ref[2]
+    core = own_ref[3]
+    sg = 1 - 2 * core
+    def put(at, piece):
+        n = piece.shape[0]
+        cols_ref[pl.ds(pl.multiple_of(at, SH), n), :] = piece
+    for off, ref in ((0, pair_ref), (-1, d1), (-2, d2), (-3, d3), (1, s1), (2, s2), (3, s3)):
+        zs = (z + off * sg + NZ) & (NZ - 1)
+        put(zs * (2 * SH), ref[...].reshape(2 * SH, 128))
+    z4 = ((z + 4) & (NZ - 1)) * (2 * SH)
+    put(z4 + core * SH, d4[...])
+    put(z4 + (1 - core) * SH, s4[...])
     for c in range(NCH):
         colsT[:, c*CH:(c+1)*CH] = jnp.transpose(cols_ref[c*CH:(c+1)*CH, :])
     cacc[...] = jnp.zeros_like(cacc); pacc[...] = jnp.zeros_like(pacc)
@@ -63,26 +76,37 @@
     rows.append(jnp.concatenate([ps,jnp.zeros_like(ps)],axis=1))
     rows.append(jnp.zeros((3,CH),jnp.float32))
     tc=jnp.concatenate(rows,axis=0)
-    for d in range(tcol_ref.shape[0]):
-        tcol_ref[d]=tc
-
-def k1(own, rows, cols, colid, dup_c=NA):
-    return pl.pallas_call(k1_body,
-      out_shape=(jax.ShapeDtypeStruct((NB,16,256),jnp.float32),jax.ShapeDtypeStruct((dup_c,16,CH),jnp.float32)),
-      in_specs=[pl.BlockSpec(memory_space=pltpu.SMEM)]+[pl.BlockSpec(memory_space=pltpu.VMEM)]*3,
-      out_specs=(pl.BlockSpec(memory_space=pltpu.VMEM),)*2,
-      scratch_shapes=[pltpu.VMEM((128,C),jnp.bfloat16),pltpu.VMEM((8,C),jnp.float32),pltpu.VMEM((8,128),jnp.float32),pltpu.VMEM((16,256),jnp.float32)],
-      compiler_params=pltpu.CompilerParams(vmem_limit_bytes=40<<20))(own,rows,cols,colid)
-
-def k2_body(own_ref, rows_ref, cols_ref, colid_ref, trow_ref, tcol_ref, g_ref, colsT, rrow, rcol):
+    tcol_ref[...]=tc
+
+def k1(own, rows, pieces, colid):
+    return pl.pallas_call(
+        k1_body,
+        out_shape=(
+            jax.ShapeDtypeStruct((NB, 16, 256), jnp.float32),
+            jax.ShapeDtypeStruct((16, CH), jnp.float32),
+            jax.ShapeDtypeStruct((C, 128), jnp.bfloat16),
+        ),
+        in_specs=[pl.BlockSpec(memory_space=pltpu.SMEM)] + [pl.BlockSpec(memory_space=pltpu.VMEM)] * (2 + len(pieces)),
+        out_specs=(pl.BlockSpec(memory_space=pltpu.VMEM),) * 3,
+        scratch_shapes=[
+            pltpu.VMEM((128, C), jnp.bfloat16),
+            pltpu.VMEM((8, C), jnp.float32),
+            pltpu.VMEM((8, 128), jnp.float32),
+            pltpu.VMEM((16, 256), jnp.float32),
+        ],
+        compiler_params=pltpu.CompilerParams(vmem_limit_bytes=40 << 20),
+    )(own, rows, *pieces, colid)
+
+
+def k2_body(own_ref, rows_ref, cols_ref, colid_ref, trow_ref, t0, t1, t2, g_ref, colsT, rrow, rcol):
+    tc_refs = (t0, t1, t2)
     for c in range(NCH):
         colsT[:, c*CH:(c+1)*CH] = jnp.transpose(cols_ref[c*CH:(c+1)*CH, :])
     b = own_ref[0]; own_off = own_ref[1]
     T=trow_ref[0]
     for d in range(1,trow_ref.shape[0]): T=T+trow_ref[d]
     rrow[...]=(1.0/TAU)/T
-    Tc=tcol_ref[0]
-    for d in range(1,tcol_ref.shape[0]): Tc=Tc+tcol_ref[d]
+    Tc=tc_refs[0][...]+tc_refs[1][...]+tc_refs[2][...]
     rid=lax.broadcasted_iota(jnp.int32,(16,CH),0)
     isT=rid<NCH
     Ts=jnp.where(isT,Tc,1.0)
@@ -121,19 +145,22 @@
 def k2(own, rows, cols, colid, trow, tcol):
     return pl.pallas_call(k2_body,
       out_shape=jax.ShapeDtypeStruct((NB,SH+8,128),jnp.float32),
-      in_specs=[pl.BlockSpec(memory_space=pltpu.SMEM)]+[pl.BlockSpec(memory_space=pltpu.VMEM)]*5,
+      in_specs=[pl.BlockSpec(memory_space=pltpu.SMEM)]+[pl.BlockSpec(memory_space=pltpu.VMEM)]*7,
       out_specs=pl.BlockSpec(memory_space=pltpu.VMEM),
       scratch_shapes=[pltpu.VMEM((128,C),jnp.bfloat16),pltpu.VMEM((16,256),jnp.float32),pltpu.VMEM((16,CH),jnp.float32)],
-      compiler_params=pltpu.CompilerParams(vmem_limit_bytes=40<<20))(own,rows,cols,colid,trow,tcol)
+      compiler_params=pltpu.CompilerParams(vmem_limit_bytes=40<<20))(own,rows,cols,colid,trow,*tcol)
 
 
 def inverse_norm(p):
     return lax.rsqrt(jnp.sum(p * p, axis=1, keepdims=True) + EPS)
 
 
-def prep_body(p_ref, mate_ref, pay_ref, zpay_ref):
+def prep_body(core_ref, p_ref, q_ref, mate_ref, pay_ref, pair_ref, low_ref):
+    core = core_ref[0]
     p = p_ref[...]
     low = (p * inverse_norm(p)).astype(jnp.bfloat16)
+    q = q_ref[...]
+    other = (q * inverse_norm(q)).astype(jnp.bfloat16)
     m = mate_ref[...]
     hi = (m >> 8).astype(jnp.float32)
     lo = (m & 255).astype(jnp.float32)
@@ -141,20 +168,22 @@
     for d in range(pay_ref.shape[0]):
         pay_ref[d, 0:SH, :] = low
         pay_ref[d, SH:PADR, :] = code
-    for d in range(zpay_ref.shape[0]):
-        zpay_ref[d] = low
-
-
-def prep(p, mate):
+    pair_ref[core] = low
+    pair_ref[1 - core] = other
+    low_ref[...] = low
+
+
+def prep(core, p, q, mate):
     return pl.pallas_call(
         prep_body,
         out_shape=(
             jax.ShapeDtypeStruct((NB, PADR, 128), jnp.bfloat16),
-            jax.ShapeDtypeStruct((8, SH, 128), jnp.bfloat16),
+            jax.ShapeDtypeStruct((2, SH, 128), jnp.bfloat16),
+            jax.ShapeDtypeStruct((SH, 128), jnp.bfloat16),
         ),
-        in_specs=[pl.BlockSpec(memory_space=pltpu.VMEM)] * 2,
-        out_specs=(pl.BlockSpec(memory_space=pltpu.VMEM),) * 2,
-    )(p, mate)
+        in_specs=[pl.BlockSpec(memory_space=pltpu.SMEM)] + [pl.BlockSpec(memory_space=pltpu.VMEM)] * 3,
+        out_specs=(pl.BlockSpec(memory_space=pltpu.VMEM),) * 3,
+    )(core, p, q, mate)
 
 
 def final_body(p_ref, g_ref, loss_ref, grad_ref):
@@ -182,23 +211,45 @@
     )(p, g)
 
 
+def swap(value):
+    return lax.ppermute(value, "c", [(0, 1), (1, 0)])
+
+
+def seat(z, core):
+    z = z % NZ
+    return ((z % 4) * 2 + core) * 2 + z // 4
+
+
+def along_z(value, k):
+    pairs = []
+    for z in range(NZ):
+        pairs.append((seat(z, 0), seat(z + k, 0)))
+        pairs.append((seat(z, 1), seat(z - k, 1)))
+    return lax.ppermute(value, ZC, pairs)
+
+
 def body(projections, partner):
     xy = lax.axis_index(XY)
-    own_a = lax.axis_index(("c", "zl", "zh"))
+    z = lax.axis_index(("zh", "zl"))
+    core = lax.axis_index("c")
+    own = jnp.stack([xy, (2 * z + core) * SH, z, core]).astype(jnp.int32)
     mate = jnp.pad(partner, (0, 64)).reshape(2, 128)
-    pay, zpay = prep(projections, mate)
+    pay, pair, low = prep(own[3:], projections, swap(projections), mate)
     rows = lax.all_to_all(pay, XY, 0, 0)
-    zg = lax.all_to_all(zpay, Z, 0, 0)
-    cols = lax.all_gather(zg, "c").reshape(C, 128)
-    own = jnp.stack([xy, own_a * SH]).astype(jnp.int32)
+    direct = [along_z(pair, k) for k in (1, 2, 3)] + [along_z(low, 4)]
+    crossed = [swap(piece) for piece in direct]
+    pieces = [pair, *direct[:3], *crossed[:3], direct[3], crossed[3]]
     p = jnp.arange(16 * CH, dtype=jnp.int32)
-    k = p // SH
-    shard = ((k % 8) // 2) * 4 + (k // 8) * 2 + k % 2
+    zp = p // (2 * SH)
+    shard = (zp % 4) * 4 + (p // SH % 2) * 2 + zp // 4
     colid = ((xy * NA + shard) * SH + p % SH).astype(jnp.float32).reshape(16, CH)
-    trow, tcol = k1(own, rows, cols, colid)
+    trow, tcol, cols = k1(own, rows, pieces, colid)
     trow = lax.all_to_all(trow, XY, 0, 0)
-    tcol = lax.all_to_all(tcol, ("zl", "c", "zh"), 0, 0)
-    g = k2(own, rows, cols, colid, trow, tcol)
+    chip = tcol + swap(tcol)
+    far = [along_z(chip, k) for k in (1, 2, 3)]
+    far.append(lax.ppermute(chip, ZC, [(seat(z, 0), seat(z + 4, 0)) for z in range(NZ)]))
+    part = (far[0] + far[1]) + (far[2] + far[3])
+    g = k2(own, rows, cols, colid, trow, (chip, part, swap(part)))
     g = lax.all_to_all(g, XY, 0, 0)
     loss, grad = final(projections, g)
     return (loss[0, 0], grad)

time: 136 us -> 117 us (0.86)
  blocking collectives: 81.8 us -> 24.3 us
  starting transfers between devices: 7.48 us -> 34.9 us
  waiting for transfers between devices: 7.48 us -> 17.2 us
    all_to_all x3 -> x0, blocking collectives: 52.5 us -> none  [the longest x1 21.6 us: body(): zg = lax.all_to_all(zpay, Z, 0, 0)]
    ppermute x0 -> x15, starting transfers between devices: none -> 20.1 us  [the longest x7 14.2 us: along_z(): return lax.ppermute(value, ZC, pairs)]
    ppermute x0 -> x15, waiting for transfers between devices: none -> 11.9 us  [the longest x7 8.77 us: along_z(): return lax.ppermute(value, ZC, pairs)]
    all_to_all x1, waiting for transfers between devices: 7.48 us -> 0.01 us  [body(): rows = lax.all_to_all(pay, XY, 0, 0)]
    all_to_all x0 -> x1, starting transfers between devices: none -> 7.23 us  [body(): trow = lax.all_to_all(trow, XY, 0, 0)]
    all_to_all x0 -> x1, waiting for transfers between devices: none -> 5.3 us  [body(): trow = lax.all_to_all(trow, XY, 0, 0)]
    all_to_all x1, blocking collectives: 27 us -> 24.3 us  [body(): g = lax.all_to_all(g, XY, 0, 0)]
    all_gather x1 -> x0, blocking collectives: 2.37 us -> none  [body(): cols = lax.all_gather(zg, 'c').reshape(C, 128)]
  transfers between devices with their start and end apart: 1 -> 17, of which waited for: 1 -> 9; matrix products, arithmetic and copies ran while one was open for 0% -> 1% of each run, Pallas kernels for 0% -> 0%
where the time goes in v2:
time: 117 us
  Pallas kernels  37.2 us (32%)
  starting transfers between devices  34.9 us (30%)
  blocking collectives  24.3 us (21%)
  waiting for transfers between devices  17.2 us (15%)
  local copies, waits for them, and re-layouts  1.92 us (2%)
    all_to_all x1, blocking collectives, body(): g = lax.all_to_all(g, XY, 0, 0)  24.3 us
    pallas_call x1, Pallas kernels, k2(): pl.pallas_call(k2_body, out_shape=jax.ShapeDtypeStruct((NB, SH + 8, 128),...  17.8 us
    pallas_call x1, Pallas kernels, k1(): pl.pallas_call(k1_body, out_shape=(jax.ShapeDtypeStruct((NB, 16, 256), jn...  15 us
    ppermute x7, starting transfers between devices, along_z(): return lax.ppermute(value, ZC, pairs)  14.2 us
    ppermute x7, waiting for transfers between devices, along_z(): return lax.ppermute(value, ZC, pairs)  8.77 us
    all_to_all x1, starting transfers between devices, body(): rows = lax.all_to_all(pay, XY, 0, 0)  7.61 us
    all_to_all x1, starting transfers between devices, body(): trow = lax.all_to_all(trow, XY, 0, 0)  7.23 us
    all_to_all x1, waiting for transfers between devices, body(): trow = lax.all_to_all(trow, XY, 0, 0)  5.3 us
  transfers between devices with their start and end apart: 17, of which 9 were waited for; matrix products, arithmetic and copies ran while one was open for 1% of the time, Pallas kernels for 0%

profile of v2, /device:TPU:2, one launch (start us, length us, event | category | flops | bytes accessed | tf_op | source)
XLA Modules:
  0.0 116.5 jit_solution(12658943262515113098)
XLA Ops:
  0.6 0.1 collective-permute-start
  0.7 1.3 %pad_bitcast_fusion.mate_ref = s32[2,128]{1,0:T(2,128)} fusion(s32[192]{0:T(256)} %param.3), kind=kLoop, calls=%fused_computation.34 | loop fusion | bytes 1792 | tf_op jit(solution)/shard_map/reshape | solution.py:236
  2.0 0.2 collective-permute-done.q_ref
  2.2 0.0 copy-start.1
  2.2 0.6 copy-done.1
  2.9 2.1 %shard_map.41 = (bf16[16,208,128]{2,1,0:T(8,128)(2,1)}, bf16[2,192,128]{2,1,0:T(8,128)(2,1)}, bf16[192,128]{1,0:T(8,128)(2,1)}) custom-call(s32[1]{0:T(128)} %bitcast.3.core_ref, f32[192,128]{1,0:T(8,128)} %p_ref.3, f32[192,128]{1,0:T(8,128)} %copy-done.1, s32[2,128]{1,0:T(2,128)} %pad_bitcast_fusion.mate_ref), custom_call_target="tpu_custom_call" | custom-call | tf_op jit(solution)/shard_map/pallas_call | solution.py:177
  4.9 0.0 copy-start
  4.9 0.0 copy-start.2
  4.9 7.6 %all-to-all-start = ((bf16[16,208,128]{2,1,0:T(8,128)(2,1)}), bf16[16,208,128]{2,1,0:T(8,128)(2,1)S(1)}, u32[]{:S(2)}, u32[]{:S(2)}) async-start(bf16[16,208,128]{2,1,0:T(8,128)(2,1)} %get-tuple-element.10), calls=%async_computation | async-start | bytes 1703936 | tf_op jit(solution)/shard_map/all_to_all | solution.py:238
  12.5 0.0 copy-done
  12.5 4.7 %collective-permute-start.3 = (bf16[2,192,128]{2,1,0:T(8,128)(2,1)S(1)}, bf16[2,192,128]{2,1,0:T(8,128)(2,1)S(1)}, u32[]{:S(2)}, u32[]{:S(2)}) collective-permute-start(bf16[2,192,128]{2,1,0:T(8,128)(2,1)S(1)} %copy-done), channel_id=1, source_target_pairs={{0,12},{2,7},{4,1},{6,11},{8,5},{10,15},{12,9},{14,2},{1,13},{3,6}... | collective-permute-start | bytes 294920 | tf_op jit(solution)/shard_map/ppermute | solution.py:228
  17.2 3.6 %collective-permute-start.2 = (bf16[2,192,128]{2,1,0:T(8,128)(2,1)S(1)}, bf16[2,192,128]{2,1,0:T(8,128)(2,1)S(1)}, u32[]{:S(2)}, u32[]{:S(2)}) collective-permute-start(bf16[2,192,128]{2,1,0:T(8,128)(2,1)S(1)} %copy-done), channel_id=1, source_target_pairs={{0,8},{2,11},{4,12},{6,15},{8,1},{10,2},{12,5},{14,6},{1,9},{3,10}... | collective-permute-start | bytes 294920 | tf_op jit(solution)/shard_map/ppermute | solution.py:228
  20.8 1.0 collective-permute-start.1
  21.9 0.0 copy-done.2
  21.9 0.5 collective-permute-start.7
  22.4 0.1 fusion.6.colid_ref
  22.5 8.8 %collective-permute-done.7.d4 = bf16[192,128]{1,0:T(8,128)(2,1)S(1)} collective-permute-done((bf16[192,128]{1,0:T(8,128)(2,1)S(1)}, bf16[192,128]{1,0:T(8,128)(2,1)S(1)}, u32[]{:S(2)}, u32[]{:S(2)}) %collective-permute-start.7) | collective-permute-done | bytes 49184 | tf_op jit(solution)/shard_map/ppermute | solution.py:228
  31.2 0.0 collective-permute-start.8
  31.2 0.0 collective-permute-done.3.d3
  31.2 0.5 collective-permute-start.6
  31.7 0.0 collective-permute-done.2.d2
  31.7 0.1 collective-permute-start.5
  31.8 0.0 collective-permute-done.1.d1
  31.8 0.4 collective-permute-start.4
  32.3 0.1 pad_add_fusion.own_ref
  32.3 0.1 collective-permute-done.8.s4
  32.5 0.2 collective-permute-done.6.s3
  32.7 0.4 collective-permute-done.5.s2
  33.0 0.2 collective-permute-done.4.s1
  33.2 0.0 all-to-all-done.rows_ref
  33.2 15.0 %shard_map.42 = (f32[16,16,256]{2,1,0:T(8,128)}, f32[16,256]{1,0:T(8,128)S(1)}, bf16[3072,128]{1,0:T(8,128)(2,1)S(1)}) custom-call(s32[4]{0:T(128)S(1)} %pad_add_fusion.own_ref, bf16[16,208,128]{2,1,0:T(8,128)(2,1)S(1)} %all-to-all-done.rows_ref, bf16[2,192,128]{2,1,0:T(8,128)(2,1)S(1)} %copy-done, bf16[2,192,128]{2,1,0:T(8,128)(2,1)S(1)} %collective-permute-done.1.d1, ...), custom_call_target="tpu_custom_call" | custom-call | tf_op jit(solution)/shard_map/pallas_call | solution.py:82
  48.2 0.4 collective-permute-start.9
  48.6 0.8 collective-permute-done.9
  49.4 4.2 %collective-permute-start.13 = (f32[16,256]{1,0:T(8,128)S(1)}, f32[16,256]{1,0:T(8,128)S(1)}, u32[]{:S(2)}, u32[]{:S(2)}) collective-permute-start(f32[16,256]{1,0:T(8,128)S(1)} %add.82.t0), channel_id=1, source_target_pairs={{0,1},{4,5},{8,9},{12,13},{1,0},{5,4},{9,8},{13,12},{16,17},{20,21... | collective-permute-start | bytes 49160 | tf_op jit(solution)/shard_map/ppermute | solution.py:250
  53.6 1.9 %collective-permute-start.12 = (f32[16,256]{1,0:T(8,128)S(1)}, f32[16,256]{1,0:T(8,128)S(1)}, u32[]{:S(2)}, u32[]{:S(2)}) collective-permute-start(f32[16,256]{1,0:T(8,128)S(1)} %add.82.t0), channel_id=1, source_target_pairs={{0,12},{2,7},{4,1},{6,11},{8,5},{10,15},{12,9},{14,2},{1,13},{3,6}... | collective-permute-start | bytes 49160 | tf_op jit(solution)/shard_map/ppermute | solution.py:228
  55.5 1.5 %collective-permute-start.11 = (f32[16,256]{1,0:T(8,128)S(1)}, f32[16,256]{1,0:T(8,128)S(1)}, u32[]{:S(2)}, u32[]{:S(2)}) collective-permute-start(f32[16,256]{1,0:T(8,128)S(1)} %add.82.t0), channel_id=1, source_target_pairs={{0,8},{2,11},{4,12},{6,15},{8,1},{10,2},{12,5},{14,6},{1,9},{3,10}... | collective-permute-start | bytes 49160 | tf_op jit(solution)/shard_map/ppermute | solution.py:228
  57.0 0.9 collective-permute-start.10
  57.9 7.2 %all-to-all-start.1 = ((f32[16,16,256]{2,1,0:T(8,128)}), f32[16,16,256]{2,1,0:T(8,128)S(1)}, u32[]{:S(2)}, u32[]{:S(2)}) async-start(f32[16,16,256]{2,1,0:T(8,128)} %get-tuple-element.14), calls=%async_computation.1 | async-start | bytes 524288 | tf_op jit(solution)/shard_map/all_to_all | solution.py:247
  65.2 0.0 collective-permute-done.13
  65.2 0.0 collective-permute-done.12
  65.2 0.0 collective-permute-done.11
  65.2 0.0 collective-permute-done.10
  65.2 0.3 collective-permute-start.14
  65.5 1.2 %collective-permute-done.14.t2 = f32[16,256]{1,0:T(8,128)S(1)} collective-permute-done((f32[16,256]{1,0:T(8,128)S(1)}, f32[16,256]{1,0:T(8,128)S(1)}, u32[]{:S(2)}, u32[]{:S(2)}) %collective-permute-start.14) | collective-permute-done | bytes 16416 | tf_op jit(solution)/shard_map/ppermute | solution.py:215
  66.7 5.3 %all-to-all-done.1.trow_ref = f32[16,16,256]{2,1,0:T(8,128)S(1)} async-done(((f32[16,16,256]{2,1,0:T(8,128)}), f32[16,16,256]{2,1,0:T(8,128)S(1)}, u32[]{:S(2)}, u32[]{:S(2)}) %all-to-all-start.1) | async-done | bytes 262176 | tf_op jit(solution)/shard_map/all_to_all | solution.py:247
  72.0 17.8 %shard_map.43 = f32[16,200,128]{2,1,0:T(8,128)S(1)} custom-call(s32[4]{0:T(128)S(1)} %pad_add_fusion.own_ref, bf16[16,208,128]{2,1,0:T(8,128)(2,1)S(1)} %all-to-all-done.rows_ref, bf16[3072,128]{1,0:T(8,128)(2,1)S(1)} %get-tuple-element.13.cols_ref, f32[16,256]{1,0:T(8,128)S(1)} %fusion.6.colid_ref, f32[16,16,256]{2,1,0:T(8,128)S(1)} %all-to-all-done.1.trow_ref, ...), custom_call_target="tpu_custom_call" | custom-call | tf_op jit(solution)/shard_map/pallas_call | solution.py:146
  89.8 24.3 %all_to_all.15.g_ref = f32[16,200,128]{2,1,0:T(8,128)} all-to-all(f32[16,200,128]{2,1,0:T(8,128)S(1)} %shard_map.43), channel_id=1, replica_groups=mesh['x'=4,'y'=4,'zl'=4,'c'=2,'zh'=2] {'x','y'}, dimensions={0} | all-to-all | bytes 3276800 | tf_op jit(solution)/shard_map/all_to_all | solution.py:253
  114.0 2.3 %shard_map.44 = (f32[1,1]{1,0:T(1,128)}, f32[192,128]{1,0:T(8,128)}) custom-call(f32[192,128]{1,0:T(8,128)} %p_ref.3, f32[16,200,128]{2,1,0:T(8,128)} %all_to_all.15.g_ref), custom_call_target="tpu_custom_call" | custom-call | tf_op jit(solution)/shard_map/pallas_call | solution.py:203
  (2 shorter events, 0.0 us)
Async XLA Ops:
  0.6 1.6 %collective-permute-start = (f32[192,128]{1,0:T(8,128)}, f32[192,128]{1,0:T(8,128)S(1)}, u32[]{:S(2)}, u32[]{:S(2)}) collective-permute-start(f32[192,128]{1,0:T(8,128)} %p_ref.3), channel_id=1, source_target_pairs={{0,2},{2,0},{1,3},{3,1},{4,6},{6,4},{5,7},{7,5},{8,10},{10,8},{9,1... | collective-permute-start | bytes 294920 | tf_op jit(solution)/shard_map/ppermute | solution.py:215
  2.2 0.6 copy-start.1
  4.9 7.6 %copy-start = (bf16[2,192,128]{2,1,0:T(8,128)(2,1)S(1)}, bf16[2,192,128]{2,1,0:T(8,128)(2,1)}, u32[]{:S(2)}) copy-start(bf16[2,192,128]{2,1,0:T(8,128)(2,1)} %get-tuple-element.11.pair_ref) | copy-start | bytes 294916
  4.9 16.9 %copy-start.2 = (bf16[192,128]{1,0:T(8,128)(2,1)S(1)}, bf16[192,128]{1,0:T(8,128)(2,1)}, u32[]{:S(2)}) copy-start(bf16[192,128]{1,0:T(8,128)(2,1)} %get-tuple-element.12) | copy-start | bytes 147460
  4.9 28.3 %all-to-all-start = ((bf16[16,208,128]{2,1,0:T(8,128)(2,1)}), bf16[16,208,128]{2,1,0:T(8,128)(2,1)S(1)}, u32[]{:S(2)}, u32[]{:S(2)}) async-start(bf16[16,208,128]{2,1,0:T(8,128)(2,1)} %get-tuple-element.10), calls=%async_computation | async-start | bytes 1703936 | tf_op jit(solution)/shard_map/all_to_all | solution.py:238
  12.5 18.7 %collective-permute-start.3 = (bf16[2,192,128]{2,1,0:T(8,128)(2,1)S(1)}, bf16[2,192,128]{2,1,0:T(8,128)(2,1)S(1)}, u32[]{:S(2)}, u32[]{:S(2)}) collective-permute-start(bf16[2,192,128]{2,1,0:T(8,128)(2,1)S(1)} %copy-done), channel_id=1, source_target_pairs={{0,12},{2,7},{4,1},{6,11},{8,5},{10,15},{12,9},{14,2},{1,13},{3,6}... | collective-permute-start | bytes 294920 | tf_op jit(solution)/shard_map/ppermute | solution.py:228
  17.2 14.5 %collective-permute-start.2 = (bf16[2,192,128]{2,1,0:T(8,128)(2,1)S(1)}, bf16[2,192,128]{2,1,0:T(8,128)(2,1)S(1)}, u32[]{:S(2)}, u32[]{:S(2)}) collective-permute-start(bf16[2,192,128]{2,1,0:T(8,128)(2,1)S(1)} %copy-done), channel_id=1, source_target_pairs={{0,8},{2,11},{4,12},{6,15},{8,1},{10,2},{12,5},{14,6},{1,9},{3,10}... | collective-permute-start | bytes 294920 | tf_op jit(solution)/shard_map/ppermute | solution.py:228
  20.8 11.0 %collective-permute-start.1 = (bf16[2,192,128]{2,1,0:T(8,128)(2,1)S(1)}, bf16[2,192,128]{2,1,0:T(8,128)(2,1)S(1)}, u32[]{:S(2)}, u32[]{:S(2)}) collective-permute-start(bf16[2,192,128]{2,1,0:T(8,128)(2,1)S(1)} %copy-done), channel_id=1, source_target_pairs={{0,4},{2,15},{4,8},{6,2},{8,12},{10,6},{12,1},{14,10},{1,5},{3,14}... | collective-permute-start | bytes 294920 | tf_op jit(solution)/shard_map/ppermute | solution.py:228
  21.9 9.4 %collective-permute-start.7 = (bf16[192,128]{1,0:T(8,128)(2,1)S(1)}, bf16[192,128]{1,0:T(8,128)(2,1)S(1)}, u32[]{:S(2)}, u32[]{:S(2)}) collective-permute-start(bf16[192,128]{1,0:T(8,128)(2,1)S(1)} %copy-done.2), channel_id=1, source_target_pairs={{0,1},{2,3},{4,5},{6,7},{8,9},{10,11},{12,13},{14,15},{1,0},{3,2},... | collective-permute-start | bytes 147464 | tf_op jit(solution)/shard_map/ppermute | solution.py:228
  31.2 1.2 %collective-permute-start.8 = (bf16[192,128]{1,0:T(8,128)(2,1)S(1)}, bf16[192,128]{1,0:T(8,128)(2,1)S(1)}, u32[]{:S(2)}, u32[]{:S(2)}) collective-permute-start(bf16[192,128]{1,0:T(8,128)(2,1)S(1)} %collective-permute-done.7.d4), channel_id=1, source_target_pairs={{0,2},{2,0},{1,3},{3,1},{4,6},{6,4},{5,7},{7,5},{8,10},{10,8},{9,1... | collective-permute-start | bytes 147464 | tf_op jit(solution)/shard_map/ppermute | solution.py:215
  31.2 1.5 %collective-permute-start.6 = (bf16[2,192,128]{2,1,0:T(8,128)(2,1)S(1)}, bf16[2,192,128]{2,1,0:T(8,128)(2,1)S(1)}, u32[]{:S(2)}, u32[]{:S(2)}) collective-permute-start(bf16[2,192,128]{2,1,0:T(8,128)(2,1)S(1)} %collective-permute-done.3.d3), channel_id=1, source_target_pairs={{0,2},{2,0},{1,3},{3,1},{4,6},{6,4},{5,7},{7,5},{8,10},{10,8},{9,1... | collective-permute-start | bytes 294920 | tf_op jit(solution)/shard_map/ppermute | solution.py:215
  31.7 1.3 %collective-permute-start.5 = (bf16[2,192,128]{2,1,0:T(8,128)(2,1)S(1)}, bf16[2,192,128]{2,1,0:T(8,128)(2,1)S(1)}, u32[]{:S(2)}, u32[]{:S(2)}) collective-permute-start(bf16[2,192,128]{2,1,0:T(8,128)(2,1)S(1)} %collective-permute-done.2.d2), channel_id=1, source_target_pairs={{0,2},{2,0},{1,3},{3,1},{4,6},{6,4},{5,7},{7,5},{8,10},{10,8},{9,1... | collective-permute-start | bytes 294920 | tf_op jit(solution)/shard_map/ppermute | solution.py:215
  31.8 1.4 %collective-permute-start.4 = (bf16[2,192,128]{2,1,0:T(8,128)(2,1)S(1)}, bf16[2,192,128]{2,1,0:T(8,128)(2,1)S(1)}, u32[]{:S(2)}, u32[]{:S(2)}) collective-permute-start(bf16[2,192,128]{2,1,0:T(8,128)(2,1)S(1)} %collective-permute-done.1.d1), channel_id=1, source_target_pairs={{0,2},{2,0},{1,3},{3,1},{4,6},{6,4},{5,7},{7,5},{8,10},{10,8},{9,1... | collective-permute-start | bytes 294920 | tf_op jit(solution)/shard_map/ppermute | solution.py:215
  48.2 1.2 %collective-permute-start.9 = (f32[16,256]{1,0:T(8,128)S(1)}, f32[16,256]{1,0:T(8,128)S(1)}, u32[]{:S(2)}, u32[]{:S(2)}) collective-permute-start(f32[16,256]{1,0:T(8,128)S(1)} %get-tuple-element.15), channel_id=1, source_target_pairs={{0,2},{2,0},{1,3},{3,1},{4,6},{6,4},{5,7},{7,5},{8,10},{10,8},{9,1... | collective-permute-start | bytes 49160 | tf_op jit(solution)/shard_map/ppermute | solution.py:215
  49.4 15.7 %collective-permute-start.13 = (f32[16,256]{1,0:T(8,128)S(1)}, f32[16,256]{1,0:T(8,128)S(1)}, u32[]{:S(2)}, u32[]{:S(2)}) collective-permute-start(f32[16,256]{1,0:T(8,128)S(1)} %add.82.t0), channel_id=1, source_target_pairs={{0,1},{4,5},{8,9},{12,13},{1,0},{5,4},{9,8},{13,12},{16,17},{20,21... | collective-permute-start | bytes 49160 | tf_op jit(solution)/shard_map/ppermute | solution.py:250
  53.6 11.6 %collective-permute-start.12 = (f32[16,256]{1,0:T(8,128)S(1)}, f32[16,256]{1,0:T(8,128)S(1)}, u32[]{:S(2)}, u32[]{:S(2)}) collective-permute-start(f32[16,256]{1,0:T(8,128)S(1)} %add.82.t0), channel_id=1, source_target_pairs={{0,12},{2,7},{4,1},{6,11},{8,5},{10,15},{12,9},{14,2},{1,13},{3,6}... | collective-permute-start | bytes 49160 | tf_op jit(solution)/shard_map/ppermute | solution.py:228
  55.5 9.6 %collective-permute-start.11 = (f32[16,256]{1,0:T(8,128)S(1)}, f32[16,256]{1,0:T(8,128)S(1)}, u32[]{:S(2)}, u32[]{:S(2)}) collective-permute-start(f32[16,256]{1,0:T(8,128)S(1)} %add.82.t0), channel_id=1, source_target_pairs={{0,8},{2,11},{4,12},{6,15},{8,1},{10,2},{12,5},{14,6},{1,9},{3,10}... | collective-permute-start | bytes 49160 | tf_op jit(solution)/shard_map/ppermute | solution.py:228
  57.0 8.2 %collective-permute-start.10 = (f32[16,256]{1,0:T(8,128)S(1)}, f32[16,256]{1,0:T(8,128)S(1)}, u32[]{:S(2)}, u32[]{:S(2)}) collective-permute-start(f32[16,256]{1,0:T(8,128)S(1)} %add.82.t0), channel_id=1, source_target_pairs={{0,4},{2,15},{4,8},{6,2},{8,12},{10,6},{12,1},{14,10},{1,5},{3,14}... | collective-permute-start | bytes 49160 | tf_op jit(solution)/shard_map/ppermute | solution.py:228
  57.9 14.0 %all-to-all-start.1 = ((f32[16,16,256]{2,1,0:T(8,128)}), f32[16,16,256]{2,1,0:T(8,128)S(1)}, u32[]{:S(2)}, u32[]{:S(2)}) async-start(f32[16,16,256]{2,1,0:T(8,128)} %get-tuple-element.14), calls=%async_computation.1 | async-start | bytes 524288 | tf_op jit(solution)/shard_map/all_to_all | solution.py:247
  65.2 1.5 %collective-permute-start.14 = (f32[16,256]{1,0:T(8,128)S(1)}, f32[16,256]{1,0:T(8,128)S(1)}, u32[]{:S(2)}, u32[]{:S(2)}) collective-permute-start(f32[16,256]{1,0:T(8,128)S(1)} %add_add_fusion.t1), channel_id=1, source_target_pairs={{0,2},{2,0},{1,3},{3,1},{4,6},{6,4},{5,7},{7,5},{8,10},{10,8},{9,1... | collective-permute-start | bytes 49160 | tf_op jit(solution)/shard_map/ppermute | solution.py:215

commit v3 on v2

v3 whole, which is shorter than its diff:
```python
import jax
import jax.numpy as jnp
from jax import lax
from jax.experimental import pallas as pl
from jax.experimental.pallas import tpu as pltpu
from jax.sharding import Mesh
from jax.sharding import PartitionSpec as P

AXES = ("x", "y", "zl", "c", "zh")
XY = ("x", "y")
ZC = ("zl", "c", "zh")
EPS = 1e-06
NZ = 8
LOG2E = 1.4426950408889634
TAU = 0.1
KS = LOG2E / TAU
SH = 192
PADR = 208
NB = 16
NA = 16
C = NA * SH
R = NB * SH
CH = 256
T1 = 1536
N1 = R // T1
PER1 = T1 // SH
T2 = 768
N2 = R // T2
PER2 = T2 // SH
NCH = C // CH
SUB = 64
CW = 256
NW = C // CW


def col_bcast(row):
    return jnp.transpose(jnp.broadcast_to(row, (128, row.shape[1])))


def load_rows(rows_ref, rows, mates, s):
    rows[pl.ds(s * SH, SH), :] = rows_ref[s, 0:SH, :]
    code = rows_ref[s, SH:PADR, :]
    code = code.astype(jnp.float32)
    m = code[0:2] * 256.0 + code[2:4]
    mates[pl.ds(s * SH, 128), :] = col_bcast(m[0:1])
    mates[pl.ds(s * SH + 128, 64), :] = col_bcast(m[1:2])[: SH - 128]


def diag_rows(b, count):
    r = lax.broadcasted_iota(jnp.int32, (count, 128), 0) - (b % (count // SH)) * SH
    return jnp.where((r >= 0) & (r < SH), r, -100000)


def diag_of(rid, lane_at, core):
    lanes = lax.broadcasted_iota(jnp.int32, (1, 128), 1) + (lane_at - core * SH)
    return rid == lanes


def k1_body(own_ref, rows_ref, pair_ref, d1, d2, d3, s1, s2, s3, d4, s4, colid_ref,
            trow_ref, tcol_ref, cols_ref, rows_out, mates, rows, colsT, racc, hval, cacc, tr, sems):
    b = own_ref[0]
    z = own_ref[1]
    core = own_ref[2]

    places = [(pair_ref.at[0], core), (pair_ref.at[1], 1 - core), (d4, 8 + core), (s4, 9 - core)]
    for off, ref in ((-1, d1), (-2, d2), (-3, d3), (1, s1), (2, s2), (3, s3)):
        slot = jnp.where(core == 0, off & 7, (-off) & 7) * 2
        first = core if off < 0 else 1 - core
        places += [(ref.at[0], slot + first), (ref.at[1], slot + 1 - first)]
    copies = []
    for n, (piece, slot) in enumerate(places):
        to = cols_ref.at[pl.ds(pl.multiple_of(slot * SH, SH), SH), :]
        copies.append(pltpu.make_async_copy(piece, to, sems.at[n]))
    for copy in copies:
        copy.start()
    for q in range(NB):
        load_rows(rows_ref, rows, mates, q)
    for copy in copies:
        copy.wait()
    keep = pltpu.make_async_copy(rows, rows_out, sems.at[16])
    keep.start()
    for c in range(NCH):
        colsT[:, c * CH : (c + 1) * CH] = jnp.transpose(cols_ref[c * CH : (c + 1) * CH, :])
    cacc[...] = jnp.zeros_like(cacc)

    def tile(t, masked):
        at = pl.multiple_of(t * T1, T1)
        u = rows[pl.ds(at, T1), :]
        rid = diag_rows(b, T1) if masked else None
        for c in range(NW):
            s = jnp.dot(u, colsT[:, c * CW : (c + 1) * CW], preferred_element_type=jnp.float32)
            sums = [None] * (CW // 128)
            for r in range(0, T1, SUB):
                m = mates[pl.ds(pl.multiple_of(at + r, SUB), SUB), :]
                ra = None if c == 0 else racc[r : r + SUB, :]
                hv = jnp.zeros((SUB, 128), jnp.float32) if c == 0 else hval[r : r + SUB, :]
                for l in range(0, CW, 128):
                    p = c * CW + l
                    sl = s[r : r + SUB, l : l + 128]
                    el = jnp.exp2(sl * KS)
                    if masked and p < 2 * SH:
                        el = jnp.where(diag_of(rid[r : r + SUB], p, core), 0.0, el)
                    ra = el if ra is None else ra + el
                    hv = jnp.where(m == colid_ref[p // 256 : p // 256 + 1, p % 256 : p % 256 + 128], sl, hv)
                    cs = jnp.sum(el.reshape(SUB // 8, 8, 128), axis=0)
                    sums[l // 128] = cs if r == 0 else sums[l // 128] + cs
                racc[r : r + SUB, :] = ra
                hval[r : r + SUB, :] = hv
            for l in range(0, CW, 128):
                cacc[:, c * CW + l : c * CW + l + 128] += sums[l // 128]
        for q in range(PER1):
            part = jnp.sum(jnp.transpose(racc[q * SH : (q + 1) * SH, :]), axis=0, keepdims=True)
            tr[pl.ds(t * PER1 + q, 1), 0:SH] = part
        return jnp.sum(hval[...].reshape(T1 // 8, 8, 128), axis=0)

    tr[...] = jnp.ones_like(tr)
    own_tile = b // PER1
    pos = tile(own_tile, True)

    def step(k, pos):
        return pos + tile((own_tile + k) & (N1 - 1), False)

    pos = lax.fori_loop(1, N1, step, pos)
    copies = [pltpu.make_async_copy(tr, trow_ref.at[d], sems.at[d]) for d in range(NB)]
    for copy in copies:
        copy.start()
    tcol_ref[...] = jnp.zeros_like(tcol_ref)
    tcol_ref[8:16, 0:128] = pos
    total = jnp.sum(cacc[...], axis=0, keepdims=True)
    for k in range(NZ):
        tcol_ref[pl.ds((z + k) & 7, 1), :] = total[:, k * 2 * SH : (k + 1) * 2 * SH]
    for copy in copies:
        copy.wait()
    keep.wait()


def k1(own, rows, pieces, colid):
    return pl.pallas_call(
        k1_body,
        out_shape=(
            jax.ShapeDtypeStruct((NB, 16, 256), jnp.float32),
            jax.ShapeDtypeStruct((16, 2 * SH), jnp.float32),
            jax.ShapeDtypeStruct((C, 128), jnp.bfloat16),
            jax.ShapeDtypeStruct((R, 128), jnp.bfloat16),
            jax.ShapeDtypeStruct((R, 128), jnp.float32),
        ),
        in_specs=[pl.BlockSpec(memory_space=pltpu.SMEM), pl.BlockSpec(memory_space=pltpu.VMEM)]
        + [pl.BlockSpec(memory_space=pltpu.HBM)] * len(pieces)
        + [pl.BlockSpec(memory_space=pltpu.VMEM)],
        out_specs=(
            pl.BlockSpec(memory_space=pltpu.HBM),
            pl.BlockSpec(memory_space=pltpu.VMEM),
            pl.BlockSpec(memory_space=pltpu.VMEM),
            pl.BlockSpec(memory_space=pltpu.HBM),
            pl.BlockSpec(memory_space=pltpu.VMEM),
        ),
        scratch_shapes=[
            pltpu.VMEM((R, 128), jnp.bfloat16),
            pltpu.VMEM((128, C), jnp.bfloat16),
            pltpu.VMEM((T1, 128), jnp.float32),
            pltpu.VMEM((T1, 128), jnp.float32),
            pltpu.VMEM((8, C), jnp.float32),
            pltpu.VMEM((NB, 256), jnp.float32),
            pltpu.SemaphoreType.DMA((17,)),
        ],
        compiler_params=pltpu.CompilerParams(vmem_limit_bytes=12 << 20),
    )(own, rows, *pieces, colid)


def mid_body(trow_ref, f1, f2, f3, f4, ris_ref, part_ref):
    part_ref[...] = (f1[...] + f2[...]) + (f3[...] + f4[...])
    total = trow_ref[0]
    for d in range(1, NB):
        total = total + trow_ref[d]
    rrow = (1.0 / TAU) / total
    for q in range(NB):
        ris_ref[q * SH : (q + 1) * SH, :] = col_bcast(rrow[q : q + 1, 0:SH])


def mid(trow, far):
    return pl.pallas_call(
        mid_body,
        out_shape=(
            jax.ShapeDtypeStruct((R, 128), jnp.float32),
            jax.ShapeDtypeStruct((16, 2 * SH), jnp.float32),
        ),
        in_specs=[pl.BlockSpec(memory_space=pltpu.VMEM)] * 5,
        out_specs=(pl.BlockSpec(memory_space=pltpu.VMEM),) * 2,
        compiler_params=pltpu.CompilerParams(vmem_limit_bytes=6 << 20),
    )(trow, *far)


def k2_body(own_ref, rows_in, mates, ris, cols_ref, colid_ref, t0, t1, t2, g_ref, rows, colsT, rcol, sem):
    fetch = pltpu.make_async_copy(rows_in, rows, sem)
    fetch.start()
    b = own_ref[0]
    z = own_ref[1]
    core = own_ref[2]
    for c in range(NCH):
        colsT[:, c * CH : (c + 1) * CH] = jnp.transpose(cols_ref[c * CH : (c + 1) * CH, :])
    tc = t0[...] + t1[...] + t2[...]
    logs = jnp.sum(jnp.log(tc[0:8]), axis=0, keepdims=True)
    pos = jnp.sum(tc[8:16], axis=0, keepdims=True)
    loss = logs - pos * (1.0 / TAU)
    loss = loss[:, 0:128] + loss[:, 128:256] + loss[:, 256:384]
    loss = jnp.concatenate([loss, jnp.zeros((7, 128), jnp.float32)], axis=0)
    for d in range(NB):
        g_ref[d, SH : SH + 8, :] = loss
    tall = t0[0:8] + t1[0:8] + t2[0:8]
    rall = (1.0 / TAU) / tall
    rcol[8:16, :] = rall
    for k in range(NZ):
        rcol[k : k + 1, :] = rcol[pl.ds(8 + ((z + k) & 7), 1), :]

    def tile(t, masked):
        at = pl.multiple_of(t * T2, T2)
        u = rows[pl.ds(at, T2), :]
        rid = diag_rows(b, T2) if masked else None
        acc = jnp.zeros((T2, 128), jnp.float32)
        for c in range(NW):
            s = jnp.dot(u, colsT[:, c * CW : (c + 1) * CW], preferred_element_type=jnp.float32)
            blocks = []
            for r in range(0, T2, SUB):
                here = pl.ds(pl.multiple_of(at + r, SUB), SUB)
                m = mates[here, :]
                ri = ris[here, :]
                ws = []
                for l in range(0, CW, 128):
                    p = c * CW + l
                    rj = rcol[p // 384 : p // 384 + 1, p % 384 : p % 384 + 128]
                    w = jnp.exp2(s[r : r + SUB, l : l + 128] * KS) * (ri + rj)
                    w = jnp.where(m == colid_ref[p // 256 : p // 256 + 1, p % 256 : p % 256 + 128], w - 2.0 / TAU, w)
                    if masked and p < 2 * SH:
                        w = jnp.where(diag_of(rid[r : r + SUB], p, core), 0.0, w)
                    ws.append(w.astype(jnp.bfloat16))
                blocks.append(jnp.concatenate(ws, axis=1))
            w = jnp.concatenate(blocks, axis=0)
            acc = acc + jnp.dot(w, cols_ref[c * CW : (c + 1) * CW, :], preferred_element_type=jnp.float32)
        for q in range(PER2):
            g_ref[t * PER2 + q, 0:SH, :] = acc[q * SH : (q + 1) * SH]

    fetch.wait()
    own_tile = b // PER2
    tile(own_tile, True)

    def step(k, _):
        tile((own_tile + k) & (N2 - 1), False)
        return 0

    lax.fori_loop(1, N2, step, 0)


def k2(own, rows, mates, ris, cols, colid, tcol):
    return pl.pallas_call(
        k2_body,
        out_shape=jax.ShapeDtypeStruct((NB, SH + 8, 128), jnp.float32),
        in_specs=[pl.BlockSpec(memory_space=pltpu.SMEM), pl.BlockSpec(memory_space=pltpu.HBM)]
        + [pl.BlockSpec(memory_space=pltpu.VMEM)] * 7,
        out_specs=pl.BlockSpec(memory_space=pltpu.VMEM),
        scratch_shapes=[
            pltpu.VMEM((R, 128), jnp.bfloat16),
            pltpu.VMEM((128, C), jnp.bfloat16),
            pltpu.VMEM((16, 2 * SH), jnp.float32),
            pltpu.SemaphoreType.DMA,
        ],
        compiler_params=pltpu.CompilerParams(vmem_limit_bytes=12 << 20),
    )(own, rows, mates, ris, cols, colid, *tcol)


def inverse_norm(p):
    return lax.rsqrt(jnp.sum(p * p, axis=1, keepdims=True) + EPS)


def prep_body(p_ref, mate_ref, pay_ref, low_ref, one, sems):
    p = p_ref[...]
    low = (p * inverse_norm(p)).astype(jnp.bfloat16)
    m = mate_ref[...].reshape(1, SH)
    m = jnp.concatenate([m[:, 0:128], jnp.concatenate([m[:, 128:], jnp.zeros((1, 64), jnp.int32)], axis=1)], axis=0)
    hi = (m >> 8).astype(jnp.float32)
    lo = (m & 255).astype(jnp.float32)
    code = jnp.concatenate([hi, lo, jnp.zeros((12, 128), jnp.float32)], axis=0).astype(jnp.bfloat16)
    one[0:SH, :] = low
    one[SH:PADR, :] = code
    copies = [pltpu.make_async_copy(one, pay_ref.at[d], sems.at[d]) for d in range(NB)]
    for copy in copies:
        copy.start()
    low_ref[...] = low
    for copy in copies:
        copy.wait()


def prep(p, mate):
    return pl.pallas_call(
        prep_body,
        out_shape=(
            jax.ShapeDtypeStruct((NB, PADR, 128), jnp.bfloat16),
            jax.ShapeDtypeStruct((SH, 128), jnp.bfloat16),
        ),
        in_specs=[pl.BlockSpec(memory_space=pltpu.VMEM)] * 2,
        out_specs=(pl.BlockSpec(memory_space=pltpu.HBM), pl.BlockSpec(memory_space=pltpu.VMEM)),
        scratch_shapes=[pltpu.VMEM((PADR, 128), jnp.bfloat16), pltpu.SemaphoreType.DMA((NB,))],
        compiler_params=pltpu.CompilerParams(vmem_limit_bytes=6 << 20),
    )(p, mate)


def final_body(p_ref, g_ref, loss_ref, grad_ref):
    p = p_ref[...]
    inv = inverse_norm(p)
    unit = p * inv
    g = g_ref[0]
    for d in range(1, NB):
        g = g + g_ref[d]
    loss_ref[0, 0] = jnp.sum(g[SH:]) / (NA * NB * SH)
    gu = g[:SH]
    inner = jnp.sum(unit * gu, axis=1, keepdims=True)
    grad_ref[...] = inv * (gu - unit * inner)


def final(p, g):
    return pl.pallas_call(
        final_body,
        out_shape=(
            jax.ShapeDtypeStruct((1, 1), jnp.float32),
            jax.ShapeDtypeStruct((SH, 128), jnp.float32),
        ),
        in_specs=[pl.BlockSpec(memory_space=pltpu.VMEM)] * 2,
        out_specs=(pl.BlockSpec(memory_space=pltpu.SMEM), pl.BlockSpec(memory_space=pltpu.VMEM)),
        compiler_params=pltpu.CompilerParams(vmem_limit_bytes=6 << 20),
    )(p, g)


def swap(value):
    return lax.ppermute(value, "c", [(0, 1), (1, 0)])


def seat(z, core):
    z = z % NZ
    return ((z % 4) * 2 + core) * 2 + z // 4


def along_z(value, k):
    pairs = []
    for z in range(NZ):
        pairs.append((seat(z, 0), seat(z + k, 0)))
        pairs.append((seat(z, 1), seat(z - k, 1)))
    return lax.ppermute(value, ZC, pairs)


def body(projections, partner):
    xy = lax.axis_index(XY)
    z = lax.axis_index(("zh", "zl"))
    core = lax.axis_index("c")
    own = jnp.stack([xy, z, core, core]).astype(jnp.int32)
    pay, low = prep(projections, partner)
    rows = lax.all_to_all(pay, XY, 0, 0)
    pair = jnp.stack([low, swap(low)])
    direct = [along_z(pair, k) for k in (1, 2, 3)] + [along_z(low, 4)]
    crossed = [swap(piece) for piece in direct]
    pieces = [pair, *direct[:3], *crossed[:3], direct[3], crossed[3]]
    p = jnp.arange(16 * CH, dtype=jnp.int32)
    zp = (z + p // (2 * SH)) % NZ
    shard = (zp % 4) * 4 + (p // SH % 2) * 2 + zp // 4
    colid = ((xy * NA + shard) * SH + p % SH).astype(jnp.float32).reshape(16, CH)
    trow, tcol, cols, rows, mates = k1(own, rows, pieces, colid)
    trow = lax.all_to_all(trow, XY, 0, 0)
    chip = tcol + swap(tcol)
    far = [along_z(chip, k) for k in (1, 2, 3)]
    far.append(lax.ppermute(chip, ZC, [(seat(z, 0), seat(z + 4, 0)) for z in range(NZ)]))
    ris, part = mid(trow, far)
    g = k2(own, rows, mates, ris, cols, colid, (chip, part, swap(part)))
    g = lax.all_to_all(g, XY, 0, 0)
    loss, grad = final(projections, g)
    return (loss[0, 0], grad)


def solution(mesh):
    finer = Mesh(mesh.devices.reshape(4, 4, 4, 2, mesh.shape["sub"]), AXES)
    in_specs = (P(AXES, None), P(AXES))
    out_specs = (P(), P(AXES, None))
    return jax.shard_map(body, mesh=finer, in_specs=in_specs, out_specs=out_specs, check_vma=False)
```

time: 117 us -> 121 us (1.034)
  local copies, waits for them, and re-layouts: 1.92 us -> 13.2 us
  Pallas kernels: 37.2 us -> 26.4 us
  blocking collectives: 24.3 us -> 29.5 us
  waiting for transfers between devices: 17.2 us -> 13.7 us
    unnamed x6 -> x36, local copies, waits for them, and re-layouts: 0.65 us -> 13.2 us
    pallas_call x1, Pallas kernels: 17.8 us -> 12.2 us  [k2(): pl.pallas_call(k2_body, out_shape=jax.ShapeDtypeStruct((NB, SH + 8, 128),...]
    all_to_all x1, waiting for transfers between devices: 5.3 us -> 0.01 us  [body(): trow = lax.all_to_all(trow, XY, 0, 0)]
    all_to_all x1, blocking collectives: 24.3 us -> 29.5 us  [body(): g = lax.all_to_all(g, XY, 0, 0)]
    pallas_call x1, Pallas kernels: 15 us -> 11.5 us  [k1(): pl.pallas_call(k1_body, out_shape=(jax.ShapeDtypeStruct((NB, 16, 256), jn...]
    ppermute x7, waiting for transfers between devices: 8.77 us -> 10.5 us  [along_z(): return lax.ppermute(value, ZC, pairs)]
    pallas_call x1, Pallas kernels: 2.33 us -> 0.84 us  [final(): pl.pallas_call(final_body, out_shape=(jax.ShapeDtypeStruct((1, 1), jnp.fl...]
    reshape x1 -> x0, local copies, waits for them, and re-layouts: 1.27 us -> none  [body(): mate = jnp.pad(partner, (0, 64)).reshape(2, 128)]
  transfers between devices with their start and end apart: 17 -> 17, of which waited for: 9 -> 9; matrix products, arithmetic and copies ran while one was open for 1% -> 0% of each run, Pallas kernels for 0% -> 0%
where the time goes in v3:
time: 121 us; the launch traced here: 120 us
  starting transfers between devices  36 us (30%)
  blocking collectives  29.5 us (24%)
  Pallas kernels  26.4 us (22%)
  waiting for transfers between devices  13.7 us (11%)
  local copies, waits for them, and re-layouts  13.2 us (11%)
    all_to_all x1, blocking collectives, body(): g = lax.all_to_all(g, XY, 0, 0)  29.5 us
    ppermute x7, starting transfers between devices, along_z(): return lax.ppermute(value, ZC, pairs)  14.8 us
    unnamed x36, local copies, waits for them, and re-layouts  13.2 us
    pallas_call x1, Pallas kernels, k2(): pl.pallas_call(k2_body, out_shape=jax.ShapeDtypeStruct((NB, SH + 8, 128),...  12.2 us
    pallas_call x1, Pallas kernels, k1(): pl.pallas_call(k1_body, out_shape=(jax.ShapeDtypeStruct((NB, 16, 256), jn...  11.5 us
    ppermute x7, waiting for transfers between devices, along_z(): return lax.ppermute(value, ZC, pairs)  10.5 us
    all_to_all x1, starting transfers between devices, body(): rows = lax.all_to_all(pay, XY, 0, 0)  7.49 us
    all_to_all x1, starting transfers between devices, body(): trow = lax.all_to_all(trow, XY, 0, 0)  7.23 us
  transfers between devices with their start and end apart: 17, of which 9 were waited for; matrix products, arithmetic and copies ran while one was open for 0% of the time, Pallas kernels for 0%

profile of v3, /device:TPU:2, one launch (start us, length us, event | category | flops | bytes accessed | tf_op | source)
XLA Modules:
  0.0 119.9 jit_solution(7483708308507868721)
XLA Ops:
  0.6 0.0 copy-start.2
  0.6 0.9 copy-done.2
  1.5 0.0 copy-start.17
  1.5 0.7 copy-done.17
  2.2 1.2 shard_map.41
  3.4 7.5 %all-to-all-start = ((bf16[16,208,128]{2,1,0:T(8,128)(2,1)}), bf16[16,208,128]{2,1,0:T(8,128)(2,1)S(1)}, u32[]{:S(2)}, u32[]{:S(2)}) async-start(bf16[16,208,128]{2,1,0:T(8,128)(2,1)} %get-tuple-element.13), calls=%async_computation | async-start | bytes 1703936 | tf_op jit(solution)/shard_map/all_to_all | solution.py:355
  10.9 0.0 collective-permute-start
  10.9 7.3 %collective-permute-start.7 = (bf16[192,128]{1,0:T(8,128)(2,1)S(1)}, bf16[192,128]{1,0:T(8,128)(2,1)S(1)}, u32[]{:S(2)}, u32[]{:S(2)}) collective-permute-start(bf16[192,128]{1,0:T(8,128)(2,1)S(1)} %get-tuple-element.14), channel_id=1, source_target_pairs={{0,1},{2,3},{4,5},{6,7},{8,9},{10,11},{12,13},{14,15},{1,0},{3,2},... | collective-permute-start | bytes 147464 | tf_op jit(solution)/shard_map/ppermute | solution.py:346
  18.2 0.0 collective-permute-done
  18.2 2.0 %collective-permute-start.3 = (bf16[2,192,128]{2,1,0:T(8,128)(2,1)S(1)}, bf16[2,192,128]{2,1,0:T(8,128)(2,1)S(1)}, u32[]{:S(2)}, u32[]{:S(2)}) collective-permute-start(bf16[2,192,128]{2,1,0:T(8,128)(2,1)S(1)} %pad_maximum_fusion.pair_ref), channel_id=1, source_target_pairs={{0,12},{2,7},{4,1},{6,11},{8,5},{10,15},{12,9},{14,2},{1,13},{3,6}... | collective-permute-start | bytes 294920 | tf_op jit(solution)/shard_map/ppermute | solution.py:346
  20.2 0.2 collective-permute-start.2
  20.4 1.0 collective-permute-start.1
  21.4 0.1 fusion.8.colid_ref
  21.5 0.0 collective-permute-done.7.d4
  21.5 1.8 %collective-permute-start.8 = (bf16[192,128]{1,0:T(8,128)(2,1)S(1)}, bf16[192,128]{1,0:T(8,128)(2,1)S(1)}, u32[]{:S(2)}, u32[]{:S(2)}) collective-permute-start(bf16[192,128]{1,0:T(8,128)(2,1)S(1)} %collective-permute-done.7.d4), channel_id=1, source_target_pairs={{0,2},{2,0},{1,3},{3,1},{4,6},{6,4},{5,7},{7,5},{8,10},{10,8},{9,1... | collective-permute-start | bytes 147464 | tf_op jit(solution)/shard_map/ppermute | solution.py:333
  23.3 0.6 copy-done.13
  24.0 2.5 %collective-permute-done.3.d3 = bf16[2,192,128]{2,1,0:T(8,128)(2,1)S(1)} collective-permute-done((bf16[2,192,128]{2,1,0:T(8,128)(2,1)S(1)}, bf16[2,192,128]{2,1,0:T(8,128)(2,1)S(1)}, u32[]{:S(2)}, u32[]{:S(2)}) %collective-permute-start.3) | collective-permute-done | bytes 98336 | tf_op jit(solution)/shard_map/ppermute | solution.py:346
  26.4 0.0 collective-permute-start.6
  26.4 2.0 %collective-permute-done.2.d2 = bf16[2,192,128]{2,1,0:T(8,128)(2,1)S(1)} collective-permute-done((bf16[2,192,128]{2,1,0:T(8,128)(2,1)S(1)}, bf16[2,192,128]{2,1,0:T(8,128)(2,1)S(1)}, u32[]{:S(2)}, u32[]{:S(2)}) %collective-permute-start.2) | collective-permute-done | bytes 98336 | tf_op jit(solution)/shard_map/ppermute | solution.py:346
  28.5 0.0 collective-permute-start.5
  28.5 1.8 %collective-permute-done.1.d1 = bf16[2,192,128]{2,1,0:T(8,128)(2,1)S(1)} collective-permute-done((bf16[2,192,128]{2,1,0:T(8,128)(2,1)S(1)}, bf16[2,192,128]{2,1,0:T(8,128)(2,1)S(1)}, u32[]{:S(2)}, u32[]{:S(2)}) %collective-permute-start.1) | collective-permute-done | bytes 98336 | tf_op jit(solution)/shard_map/ppermute | solution.py:346
  30.3 0.0 collective-permute-start.4
  30.3 0.6 copy-done.5
  30.9 0.1 pad_add_fusion.own_ref
  31.0 0.0 collective-permute-done.8.s4
  31.0 0.6 copy-done.15
  31.6 0.0 collective-permute-done.6.s3
  31.6 0.6 copy-done.7
  32.3 0.0 collective-permute-done.5.s2
  32.3 0.6 copy-done.9
  32.9 0.0 collective-permute-done.4.s1
  32.9 0.6 copy-done.11
  33.5 0.0 all-to-all-done.rows_ref
  33.5 0.9 copy-done.6
  34.4 0.9 copy-done.8
  35.3 0.9 copy-done.10
  36.2 0.9 copy-done.12
  37.1 0.8 copy-done.14
  37.9 0.8 copy-done.16
  38.7 11.5 %shard_map.42 = (f32[16,16,256]{2,1,0:T(8,128)S(1)}, f32[16,384]{1,0:T(8,128)S(1)}, bf16[3072,128]{1,0:T(8,128)(2,1)S(1)}, bf16[3072,128]{1,0:T(8,128)(2,1)S(1)}, f32[3072,128]{1,0:T(8,128)S(1)}) custom-call(s32[4]{0:T(128)S(1)} %pad_add_fusion.own_ref, bf16[16,208,128]{2,1,0:T(8,128)(2,1)S(1)} %all-to-all-done.rows_ref, ...), custom_call_target="tpu_custom_call" | custom-call | tf_op jit(solution)/shard_map/pallas_call | solution.py:138
  50.2 0.0 copy-start
  50.2 0.9 copy-done
  51.1 0.7 copy-done.4
  51.8 7.2 %all-to-all-start.1 = ((f32[16,16,256]{2,1,0:T(8,128)}), f32[16,16,256]{2,1,0:T(8,128)S(1)}, u32[]{:S(2)}, u32[]{:S(2)}) async-start(f32[16,16,256]{2,1,0:T(8,128)} %copy-done.4), calls=%async_computation.1 | async-start | bytes 524288 | tf_op jit(solution)/shard_map/all_to_all | solution.py:365
  59.0 0.0 collective-permute-start.9
  59.0 1.2 collective-permute-done.9
  60.2 4.5 %collective-permute-start.13 = (f32[16,384]{1,0:T(8,128)S(1)}, f32[16,384]{1,0:T(8,128)S(1)}, u32[]{:S(2)}, u32[]{:S(2)}) collective-permute-start(f32[16,384]{1,0:T(8,128)S(1)} %add.82.t0), channel_id=1, source_target_pairs={{0,1},{4,5},{8,9},{12,13},{1,0},{5,4},{9,8},{13,12},{16,17},{20,21... | collective-permute-start | bytes 73736 | tf_op jit(solution)/shard_map/ppermute | solution.py:368
  64.7 1.6 %collective-permute-start.12 = (f32[16,384]{1,0:T(8,128)S(1)}, f32[16,384]{1,0:T(8,128)S(1)}, u32[]{:S(2)}, u32[]{:S(2)}) collective-permute-start(f32[16,384]{1,0:T(8,128)S(1)} %add.82.t0), channel_id=1, source_target_pairs={{0,12},{2,7},{4,1},{6,11},{8,5},{10,15},{12,9},{14,2},{1,13},{3,6}... | collective-permute-start | bytes 73736 | tf_op jit(solution)/shard_map/ppermute | solution.py:346
  66.3 2.8 %collective-permute-start.11 = (f32[16,384]{1,0:T(8,128)S(1)}, f32[16,384]{1,0:T(8,128)S(1)}, u32[]{:S(2)}, u32[]{:S(2)}) collective-permute-start(f32[16,384]{1,0:T(8,128)S(1)} %add.82.t0), channel_id=1, source_target_pairs={{0,8},{2,11},{4,12},{6,15},{8,1},{10,2},{12,5},{14,6},{1,9},{3,10}... | collective-permute-start | bytes 73736 | tf_op jit(solution)/shard_map/ppermute | solution.py:346
  69.0 0.0 collective-permute-start.10
  69.1 0.8 collective-permute-done.13.f4
  69.8 1.8 %collective-permute-done.12.f3 = f32[16,384]{1,0:T(8,128)S(1)} collective-permute-done((f32[16,384]{1,0:T(8,128)S(1)}, f32[16,384]{1,0:T(8,128)S(1)}, u32[]{:S(2)}, u32[]{:S(2)}) %collective-permute-start.12) | collective-permute-done | bytes 24608 | tf_op jit(solution)/shard_map/ppermute | solution.py:346
  71.7 0.6 collective-permute-done.11.f2
  72.3 1.8 %collective-permute-done.10.f1 = f32[16,384]{1,0:T(8,128)S(1)} collective-permute-done((f32[16,384]{1,0:T(8,128)S(1)}, f32[16,384]{1,0:T(8,128)S(1)}, u32[]{:S(2)}, u32[]{:S(2)}) %collective-permute-start.10) | collective-permute-done | bytes 24608 | tf_op jit(solution)/shard_map/ppermute | solution.py:346
  74.1 0.0 all-to-all-done.1.trow_ref
  74.1 0.6 shard_map.43
  74.7 0.1 collective-permute-start.14
  74.8 1.2 collective-permute-done.14.t2
  76.0 1.1 copy-done.1
  77.1 12.2 %shard_map.44 = f32[16,200,128]{2,1,0:T(8,128)S(1)} custom-call(s32[4]{0:T(128)S(1)} %pad_add_fusion.own_ref, bf16[3072,128]{1,0:T(8,128)(2,1)S(1)} %copy-done.1, f32[3072,128]{1,0:T(8,128)S(1)} %get-tuple-element.16.mates, f32[3072,128]{1,0:T(8,128)S(1)} %get-tuple-element.19.ris, bf16[3072,128]{1,0:T(8,128)(2,1)S(1)} %get-tuple-element.20.cols_ref, ...), custom_call_target="tpu_custom_call" | custom-call | tf_op jit(solution)/shard_map/pallas_call | solution.py:254
  89.4 0.0 copy-start.3
  89.4 29.5 %all_to_all.15.g_ref = f32[16,200,128]{2,1,0:T(8,128)S(1)} all-to-all(f32[16,200,128]{2,1,0:T(8,128)S(1)} %shard_map.44), channel_id=1, replica_groups=mesh['x'=4,'y'=4,'zl'=4,'c'=2,'zh'=2] {'x','y'}, dimensions={0} | all-to-all | bytes 3276800 | tf_op jit(solution)/shard_map/all_to_all | solution.py:371
  118.9 0.0 copy-done.3
  118.9 0.8 shard_map.45
  (16 shorter events, 0.0 us)
Async XLA Ops:
  0.6 0.9 copy-start.2
  1.5 0.7 copy-start.17
  3.4 30.1 %all-to-all-start = ((bf16[16,208,128]{2,1,0:T(8,128)(2,1)}), bf16[16,208,128]{2,1,0:T(8,128)(2,1)S(1)}, u32[]{:S(2)}, u32[]{:S(2)}) async-start(bf16[16,208,128]{2,1,0:T(8,128)(2,1)} %get-tuple-element.13), calls=%async_computation | async-start | bytes 1703936 | tf_op jit(solution)/shard_map/all_to_all | solution.py:355
  10.9 7.3 %collective-permute-start = (bf16[192,128]{1,0:T(8,128)(2,1)S(1)}, bf16[192,128]{1,0:T(8,128)(2,1)S(1)}, u32[]{:S(2)}, u32[]{:S(2)}) collective-permute-start(bf16[192,128]{1,0:T(8,128)(2,1)S(1)} %get-tuple-element.14), channel_id=1, source_target_pairs={{0,2},{2,0},{1,3},{3,1},{4,6},{6,4},{5,7},{7,5},{8,10},{10,8},{9,1... | collective-permute-start | bytes 147464 | tf_op jit(solution)/shard_map/ppermute | solution.py:333
  10.9 10.6 %collective-permute-start.7 = (bf16[192,128]{1,0:T(8,128)(2,1)S(1)}, bf16[192,128]{1,0:T(8,128)(2,1)S(1)}, u32[]{:S(2)}, u32[]{:S(2)}) collective-permute-start(bf16[192,128]{1,0:T(8,128)(2,1)S(1)} %get-tuple-element.14), channel_id=1, source_target_pairs={{0,1},{2,3},{4,5},{6,7},{8,9},{10,11},{12,13},{14,15},{1,0},{3,2},... | collective-permute-start | bytes 147464 | tf_op jit(solution)/shard_map/ppermute | solution.py:346
  18.2 8.2 %collective-permute-start.3 = (bf16[2,192,128]{2,1,0:T(8,128)(2,1)S(1)}, bf16[2,192,128]{2,1,0:T(8,128)(2,1)S(1)}, u32[]{:S(2)}, u32[]{:S(2)}) collective-permute-start(bf16[2,192,128]{2,1,0:T(8,128)(2,1)S(1)} %pad_maximum_fusion.pair_ref), channel_id=1, source_target_pairs={{0,12},{2,7},{4,1},{6,11},{8,5},{10,15},{12,9},{14,2},{1,13},{3,6}... | collective-permute-start | bytes 294920 | tf_op jit(solution)/shard_map/ppermute | solution.py:346
  20.2 8.3 %collective-permute-start.2 = (bf16[2,192,128]{2,1,0:T(8,128)(2,1)S(1)}, bf16[2,192,128]{2,1,0:T(8,128)(2,1)S(1)}, u32[]{:S(2)}, u32[]{:S(2)}) collective-permute-start(bf16[2,192,128]{2,1,0:T(8,128)(2,1)S(1)} %pad_maximum_fusion.pair_ref), channel_id=1, source_target_pairs={{0,8},{2,11},{4,12},{6,15},{8,1},{10,2},{12,5},{14,6},{1,9},{3,10}... | collective-permute-start | bytes 294920 | tf_op jit(solution)/shard_map/ppermute | solution.py:346
  20.4 9.9 %collective-permute-start.1 = (bf16[2,192,128]{2,1,0:T(8,128)(2,1)S(1)}, bf16[2,192,128]{2,1,0:T(8,128)(2,1)S(1)}, u32[]{:S(2)}, u32[]{:S(2)}) collective-permute-start(bf16[2,192,128]{2,1,0:T(8,128)(2,1)S(1)} %pad_maximum_fusion.pair_ref), channel_id=1, source_target_pairs={{0,4},{2,15},{4,8},{6,2},{8,12},{10,6},{12,1},{14,10},{1,5},{3,14}... | collective-permute-start | bytes 294920 | tf_op jit(solution)/shard_map/ppermute | solution.py:346
  21.5 9.5 %collective-permute-start.8 = (bf16[192,128]{1,0:T(8,128)(2,1)S(1)}, bf16[192,128]{1,0:T(8,128)(2,1)S(1)}, u32[]{:S(2)}, u32[]{:S(2)}) collective-permute-start(bf16[192,128]{1,0:T(8,128)(2,1)S(1)} %collective-permute-done.7.d4), channel_id=1, source_target_pairs={{0,2},{2,0},{1,3},{3,1},{4,6},{6,4},{5,7},{7,5},{8,10},{10,8},{9,1... | collective-permute-start | bytes 147464 | tf_op jit(solution)/shard_map/ppermute | solution.py:333
  23.3 0.6 copy-start.13
  26.4 5.2 %collective-permute-start.6 = (bf16[2,192,128]{2,1,0:T(8,128)(2,1)S(1)}, bf16[2,192,128]{2,1,0:T(8,128)(2,1)S(1)}, u32[]{:S(2)}, u32[]{:S(2)}) collective-permute-start(bf16[2,192,128]{2,1,0:T(8,128)(2,1)S(1)} %collective-permute-done.3.d3), channel_id=1, source_target_pairs={{0,2},{2,0},{1,3},{3,1},{4,6},{6,4},{5,7},{7,5},{8,10},{10,8},{9,1... | collective-permute-start | bytes 294920 | tf_op jit(solution)/shard_map/ppermute | solution.py:333
  28.5 3.8 %collective-permute-start.5 = (bf16[2,192,128]{2,1,0:T(8,128)(2,1)S(1)}, bf16[2,192,128]{2,1,0:T(8,128)(2,1)S(1)}, u32[]{:S(2)}, u32[]{:S(2)}) collective-permute-start(bf16[2,192,128]{2,1,0:T(8,128)(2,1)S(1)} %collective-permute-done.2.d2), channel_id=1, source_target_pairs={{0,2},{2,0},{1,3},{3,1},{4,6},{6,4},{5,7},{7,5},{8,10},{10,8},{9,1... | collective-permute-start | bytes 294920 | tf_op jit(solution)/shard_map/ppermute | solution.py:333
  30.3 2.6 %collective-permute-start.4 = (bf16[2,192,128]{2,1,0:T(8,128)(2,1)S(1)}, bf16[2,192,128]{2,1,0:T(8,128)(2,1)S(1)}, u32[]{:S(2)}, u32[]{:S(2)}) collective-permute-start(bf16[2,192,128]{2,1,0:T(8,128)(2,1)S(1)} %collective-permute-done.1.d1), channel_id=1, source_target_pairs={{0,2},{2,0},{1,3},{3,1},{4,6},{6,4},{5,7},{7,5},{8,10},{10,8},{9,1... | collective-permute-start | bytes 294920 | tf_op jit(solution)/shard_map/ppermute | solution.py:333
  30.3 0.6 copy-start.5
  31.0 0.6 copy-start.15
  31.6 0.6 copy-start.7
  32.3 0.6 copy-start.9
  32.9 0.6 copy-start.11
  33.5 0.9 copy-start.6
  34.4 0.9 copy-start.8
  35.3 0.9 copy-start.10
  36.2 0.9 copy-start.12
  37.1 0.8 copy-start.14
  37.9 0.8 copy-start.16
  50.2 0.9 copy-start
  51.1 0.7 copy-start.4
  51.8 22.3 %all-to-all-start.1 = ((f32[16,16,256]{2,1,0:T(8,128)}), f32[16,16,256]{2,1,0:T(8,128)S(1)}, u32[]{:S(2)}, u32[]{:S(2)}) async-start(f32[16,16,256]{2,1,0:T(8,128)} %copy-done.4), calls=%async_computation.1 | async-start | bytes 524288 | tf_op jit(solution)/shard_map/all_to_all | solution.py:365
  59.0 1.2 collective-permute-start.9
  60.2 9.6 %collective-permute-start.13 = (f32[16,384]{1,0:T(8,128)S(1)}, f32[16,384]{1,0:T(8,128)S(1)}, u32[]{:S(2)}, u32[]{:S(2)}) collective-permute-start(f32[16,384]{1,0:T(8,128)S(1)} %add.82.t0), channel_id=1, source_target_pairs={{0,1},{4,5},{8,9},{12,13},{1,0},{5,4},{9,8},{13,12},{16,17},{20,21... | collective-permute-start | bytes 73736 | tf_op jit(solution)/shard_map/ppermute | solution.py:368
  64.7 6.9 %collective-permute-start.12 = (f32[16,384]{1,0:T(8,128)S(1)}, f32[16,384]{1,0:T(8,128)S(1)}, u32[]{:S(2)}, u32[]{:S(2)}) collective-permute-start(f32[16,384]{1,0:T(8,128)S(1)} %add.82.t0), channel_id=1, source_target_pairs={{0,12},{2,7},{4,1},{6,11},{8,5},{10,15},{12,9},{14,2},{1,13},{3,6}... | collective-permute-start | bytes 73736 | tf_op jit(solution)/shard_map/ppermute | solution.py:346
  66.3 6.0 %collective-permute-start.11 = (f32[16,384]{1,0:T(8,128)S(1)}, f32[16,384]{1,0:T(8,128)S(1)}, u32[]{:S(2)}, u32[]{:S(2)}) collective-permute-start(f32[16,384]{1,0:T(8,128)S(1)} %add.82.t0), channel_id=1, source_target_pairs={{0,8},{2,11},{4,12},{6,15},{8,1},{10,2},{12,5},{14,6},{1,9},{3,10}... | collective-permute-start | bytes 73736 | tf_op jit(solution)/shard_map/ppermute | solution.py:346
  69.0 5.0 %collective-permute-start.10 = (f32[16,384]{1,0:T(8,128)S(1)}, f32[16,384]{1,0:T(8,128)S(1)}, u32[]{:S(2)}, u32[]{:S(2)}) collective-permute-start(f32[16,384]{1,0:T(8,128)S(1)} %add.82.t0), channel_id=1, source_target_pairs={{0,4},{2,15},{4,8},{6,2},{8,12},{10,6},{12,1},{14,10},{1,5},{3,14}... | collective-permute-start | bytes 73736 | tf_op jit(solution)/shard_map/ppermute | solution.py:346
  74.7 1.3 %collective-permute-start.14 = (f32[16,384]{1,0:T(8,128)S(1)}, f32[16,384]{1,0:T(8,128)S(1)}, u32[]{:S(2)}, u32[]{:S(2)}) collective-permute-start(f32[16,384]{1,0:T(8,128)S(1)} %get-tuple-element.21.t1), channel_id=1, source_target_pairs={{0,2},{2,0},{1,3},{3,1},{4,6},{6,4},{5,7},{7,5},{8,10},{10,8},{9,1... | collective-permute-start | bytes 73736 | tf_op jit(solution)/shard_map/ppermute | solution.py:333
  76.0 1.1 copy-start.1
  89.4 29.5 %copy-start.3 = (f32[192,128]{1,0:T(8,128)S(1)}, f32[192,128]{1,0:T(8,128)}, u32[]{:S(2)}) copy-start(f32[192,128]{1,0:T(8,128)} %p_ref.3) | copy-start | bytes 294916

commit v4 on v3

--- a/solution.py
+++ b/solution.py
@@ -57,7 +57,7 @@
 
 
 def k1_body(own_ref, rows_ref, pair_ref, d1, d2, d3, s1, s2, s3, d4, s4, colid_ref,
-            trow_ref, tcol_ref, cols_ref, rows_out, mates, rows, colsT, racc, hval, cacc, tr, sems):
+            keep_ref, give_ref, cols_ref, rows_out, mates, rows, colsT, racc, hval, cacc, tr, tc, tail, sems):
     b = own_ref[0]
     z = own_ref[1]
     core = own_ref[2]
@@ -121,16 +121,15 @@
         return pos + tile((own_tile + k) & (N1 - 1), False)
 
     pos = lax.fori_loop(1, N1, step, pos)
-    copies = [pltpu.make_async_copy(tr, trow_ref.at[d], sems.at[d]) for d in range(NB)]
-    for copy in copies:
-        copy.start()
-    tcol_ref[...] = jnp.zeros_like(tcol_ref)
-    tcol_ref[8:16, 0:128] = pos
     total = jnp.sum(cacc[...], axis=0, keepdims=True)
     for k in range(NZ):
-        tcol_ref[pl.ds((z + k) & 7, 1), :] = total[:, k * 2 * SH : (k + 1) * 2 * SH]
-    for copy in copies:
-        copy.wait()
+        at = (z + k) & 7
+        tc[pl.ds(at, 1), :] = total[:, k * 2 * SH : k * 2 * SH + 256]
+        tail[pl.ds(at, 1), :] = total[:, k * 2 * SH + 256 : (k + 1) * 2 * SH]
+    by_rows = tr[...]
+    by_cols = jnp.concatenate([tc[...], jnp.concatenate([tail[...], pos], axis=1)], axis=0)
+    keep_ref[...] = jnp.where(core == 0, by_rows, by_cols)
+    give_ref[...] = jnp.where(core == 0, by_cols, by_rows)
     keep.wait()
 
 
@@ -138,17 +137,17 @@
     return pl.pallas_call(
         k1_body,
         out_shape=(
-            jax.ShapeDtypeStruct((NB, 16, 256), jnp.float32),
-            jax.ShapeDtypeStruct((16, 2 * SH), jnp.float32),
+            jax.ShapeDtypeStruct((16, 256), jnp.float32),
+            jax.ShapeDtypeStruct((16, 256), jnp.float32),
             jax.ShapeDtypeStruct((C, 128), jnp.bfloat16),
-            jax.ShapeDtypeStruct((R, 128), jnp.bfloat16),
+            pltpu.HBM((R, 128), jnp.bfloat16),
             jax.ShapeDtypeStruct((R, 128), jnp.float32),
         ),
         in_specs=[pl.BlockSpec(memory_space=pltpu.SMEM), pl.BlockSpec(memory_space=pltpu.VMEM)]
         + [pl.BlockSpec(memory_space=pltpu.HBM)] * len(pieces)
         + [pl.BlockSpec(memory_space=pltpu.VMEM)],
         out_specs=(
-            pl.BlockSpec(memory_space=pltpu.HBM),
+            pl.BlockSpec(memory_space=pltpu.VMEM),
             pl.BlockSpec(memory_space=pltpu.VMEM),
             pl.BlockSpec(memory_space=pltpu.VMEM),
             pl.BlockSpec(memory_space=pltpu.HBM),
@@ -161,36 +160,68 @@
             pltpu.VMEM((T1, 128), jnp.float32),
             pltpu.VMEM((8, C), jnp.float32),
             pltpu.VMEM((NB, 256), jnp.float32),
+            pltpu.VMEM((8, 256), jnp.float32),
+            pltpu.VMEM((8, 128), jnp.float32),
             pltpu.SemaphoreType.DMA((17,)),
         ],
         compiler_params=pltpu.CompilerParams(vmem_limit_bytes=12 << 20),
     )(own, rows, *pieces, colid)
 
 
-def mid_body(trow_ref, f1, f2, f3, f4, ris_ref, part_ref):
-    part_ref[...] = (f1[...] + f2[...]) + (f3[...] + f4[...])
-    total = trow_ref[0]
-    for d in range(1, NB):
-        total = total + trow_ref[d]
-    rrow = (1.0 / TAU) / total
-    for q in range(NB):
-        ris_ref[q * SH : (q + 1) * SH, :] = col_bcast(rrow[q : q + 1, 0:SH])
-
-
-def mid(trow, far):
+def pack_body(own_ref, keep_ref, got_ref, pay_ref, both, sems):
+    core = own_ref[2]
+    mine = keep_ref[...]
+    got = got_ref[...]
+    both[0] = mine + jnp.where(core == 0, 0.0, got)
+    both[1] = got
+    copies = [pltpu.make_async_copy(both, pay_ref.at[d], sems.at[d]) for d in range(NB)]
+    for copy in copies:
+        copy.start()
+    for copy in copies:
+        copy.wait()
+
+
+def pack(own, keep, got):
+    return pl.pallas_call(
+        pack_body,
+        out_shape=pltpu.HBM((NB, 2, 16, 256), jnp.float32),
+        in_specs=[pl.BlockSpec(memory_space=pltpu.SMEM)] + [pl.BlockSpec(memory_space=pltpu.VMEM)] * 2,
+        out_specs=pl.BlockSpec(memory_space=pltpu.HBM),
+        scratch_shapes=[pltpu.VMEM((2, 16, 256), jnp.float32), pltpu.SemaphoreType.DMA((NB,))],
+        compiler_params=pltpu.CompilerParams(vmem_limit_bytes=6 << 20),
+    )(own, keep, got)
+
+
+def mid_body(own_ref, part_ref, keep_ref, give_ref):
+    core = own_ref[2]
+    line = own_ref[3]
+
+    def total(lo, hi, which):
+        out = part_ref[lo, which]
+        for d in range(lo + 1, hi):
+            out = out + part_ref[d, which]
+        return out
+
+    low = total(0, 8, 0)
+    high = total(8, 16, 0)
+    rows = low + high
+    other = total(0, 16, 1)
+    cols = jnp.where(line == 0, low, high)
+    keep_ref[...] = jnp.where(core == 0, rows, cols)
+    give_ref[...] = jnp.where(core == 0, other, cols)
+
+
+def mid(own, part):
     return pl.pallas_call(
         mid_body,
-        out_shape=(
-            jax.ShapeDtypeStruct((R, 128), jnp.float32),
-            jax.ShapeDtypeStruct((16, 2 * SH), jnp.float32),
-        ),
-        in_specs=[pl.BlockSpec(memory_space=pltpu.VMEM)] * 5,
+        out_shape=(jax.ShapeDtypeStruct((16, 256), jnp.float32),) * 2,
+        in_specs=[pl.BlockSpec(memory_space=pltpu.SMEM), pl.BlockSpec(memory_space=pltpu.VMEM)],
         out_specs=(pl.BlockSpec(memory_space=pltpu.VMEM),) * 2,
         compiler_params=pltpu.CompilerParams(vmem_limit_bytes=6 << 20),
-    )(trow, *far)
-
-
-def k2_body(own_ref, rows_in, mates, ris, cols_ref, colid_ref, t0, t1, t2, g_ref, rows, colsT, rcol, sem):
+    )(own, part)
+
+
+def k2_body(own_ref, rows_in, mates, cols_ref, colid_ref, keep_ref, got_ref, g_ref, rows, ris, colsT, rcol, sem):
     fetch = pltpu.make_async_copy(rows_in, rows, sem)
     fetch.start()
     b = own_ref[0]
@@ -198,17 +229,21 @@
     core = own_ref[2]
     for c in range(NCH):
         colsT[:, c * CH : (c + 1) * CH] = jnp.transpose(cols_ref[c * CH : (c + 1) * CH, :])
-    tc = t0[...] + t1[...] + t2[...]
-    logs = jnp.sum(jnp.log(tc[0:8]), axis=0, keepdims=True)
-    pos = jnp.sum(tc[8:16], axis=0, keepdims=True)
-    loss = logs - pos * (1.0 / TAU)
-    loss = loss[:, 0:128] + loss[:, 128:256] + loss[:, 256:384]
+    mine = keep_ref[...]
+    got = got_ref[...]
+    by_rows = jnp.where(core == 0, mine, got)
+    by_cols = jnp.where(core == 0, got, mine)
+    rrow = (1.0 / TAU) / by_rows
+    for q in range(NB):
+        ris[q * SH : (q + 1) * SH, :] = col_bcast(rrow[q : q + 1, 0:SH])
+    tall = jnp.concatenate([by_cols[0:8], by_cols[8:16, 0:128]], axis=1)
+    logs = jnp.sum(jnp.log(tall), axis=0, keepdims=True)
+    pos = jnp.sum(by_cols[8:16, 128:256], axis=0, keepdims=True)
+    loss = logs[:, 0:128] + logs[:, 128:256] + logs[:, 256:384] - pos * (1.0 / TAU)
     loss = jnp.concatenate([loss, jnp.zeros((7, 128), jnp.float32)], axis=0)
     for d in range(NB):
         g_ref[d, SH : SH + 8, :] = loss
-    tall = t0[0:8] + t1[0:8] + t2[0:8]
-    rall = (1.0 / TAU) / tall
-    rcol[8:16, :] = rall
+    rcol[8:16, :] = (1.0 / TAU) / tall
     for k in range(NZ):
         rcol[k : k + 1, :] = rcol[pl.ds(8 + ((z + k) & 7), 1), :]
 
@@ -250,21 +285,22 @@
     lax.fori_loop(1, N2, step, 0)
 
 
-def k2(own, rows, mates, ris, cols, colid, tcol):
+def k2(own, rows, mates, cols, colid, keep, got):
     return pl.pallas_call(
         k2_body,
         out_shape=jax.ShapeDtypeStruct((NB, SH + 8, 128), jnp.float32),
         in_specs=[pl.BlockSpec(memory_space=pltpu.SMEM), pl.BlockSpec(memory_space=pltpu.HBM)]
-        + [pl.BlockSpec(memory_space=pltpu.VMEM)] * 7,
+        + [pl.BlockSpec(memory_space=pltpu.VMEM)] * 5,
         out_specs=pl.BlockSpec(memory_space=pltpu.VMEM),
         scratch_shapes=[
             pltpu.VMEM((R, 128), jnp.bfloat16),
+            pltpu.VMEM((R, 128), jnp.float32),
             pltpu.VMEM((128, C), jnp.bfloat16),
             pltpu.VMEM((16, 2 * SH), jnp.float32),
             pltpu.SemaphoreType.DMA,
         ],
         compiler_params=pltpu.CompilerParams(vmem_limit_bytes=12 << 20),
-    )(own, rows, mates, ris, cols, colid, *tcol)
+    )(own, rows, mates, cols, colid, keep, got)
 
 
 def inverse_norm(p):
@@ -293,7 +329,7 @@
     return pl.pallas_call(
         prep_body,
         out_shape=(
-            jax.ShapeDtypeStruct((NB, PADR, 128), jnp.bfloat16),
+            pltpu.HBM((NB, PADR, 128), jnp.bfloat16),
             jax.ShapeDtypeStruct((SH, 128), jnp.bfloat16),
         ),
         in_specs=[pl.BlockSpec(memory_space=pltpu.VMEM)] * 2,
@@ -338,6 +374,15 @@
     return ((z % 4) * 2 + core) * 2 + z // 4
 
 
+def total_groups():
+    def place(x, y, z, core):
+        return ((x * 4 + y) * 4 + z % 4) * 4 + core * 2 + z // 4
+
+    planes = [[place(x, y, z, 0) for x in range(4) for y in range(4)] for z in range(NZ)]
+    lines = [[place(x, 2 * h + y, z, 1) for y in (0, 1) for z in range(NZ)] for x in range(4) for h in (0, 1)]
+    return planes + lines
+
+
 def along_z(value, k):
     pairs = []
     for z in range(NZ):
@@ -350,7 +395,7 @@
     xy = lax.axis_index(XY)
     z = lax.axis_index(("zh", "zl"))
     core = lax.axis_index("c")
-    own = jnp.stack([xy, z, core, core]).astype(jnp.int32)
+    own = jnp.stack([xy, z, core, lax.axis_index("y") % 2]).astype(jnp.int32)
     pay, low = prep(projections, partner)
     rows = lax.all_to_all(pay, XY, 0, 0)
     pair = jnp.stack([low, swap(low)])
@@ -361,14 +406,13 @@
     zp = (z + p // (2 * SH)) % NZ
     shard = (zp % 4) * 4 + (p // SH % 2) * 2 + zp // 4
     colid = ((xy * NA + shard) * SH + p % SH).astype(jnp.float32).reshape(16, CH)
-    trow, tcol, cols, rows, mates = k1(own, rows, pieces, colid)
-    trow = lax.all_to_all(trow, XY, 0, 0)
-    chip = tcol + swap(tcol)
-    far = [along_z(chip, k) for k in (1, 2, 3)]
-    far.append(lax.ppermute(chip, ZC, [(seat(z, 0), seat(z + 4, 0)) for z in range(NZ)]))
-    ris, part = mid(trow, far)
-    g = k2(own, rows, mates, ris, cols, colid, (chip, part, swap(part)))
-    g = lax.all_to_all(g, XY, 0, 0)
+    pieces = [pltpu.with_memory_space_constraint(piece, pltpu.HBM) for piece in pieces]
+    keep, give, cols, rows, mates = k1(own, rows, pieces, colid)
+    part = lax.all_to_all(pack(own, keep, swap(give)), AXES, 0, 0, axis_index_groups=total_groups())
+    keep, give = mid(own, part)
+    rows = pltpu.with_memory_space_constraint(rows, pltpu.HBM)
+    g = k2(own, rows, mates, cols, colid, keep, swap(give))
+    g = pltpu.with_memory_space_constraint(lax.all_to_all(g, XY, 0, 0), pltpu.HBM)
     loss, grad = final(projections, g)
     return (loss[0, 0], grad)
 

time: 121 us -> 110 us (0.909)
  starting transfers between devices: 36 us -> 20.4 us
  blocking collectives: 29.5 us -> 44.3 us
  local copies, waits for them, and re-layouts: 13.2 us -> 2.16 us
  Pallas kernels: 26.4 us -> 30 us
  waiting for transfers between devices: 13.7 us -> 10.3 us
    all_to_all x1 -> x2, blocking collectives: 29.5 us -> 44.3 us  [the longest x1 28.5 us: body(): lax.all_to_all(g, XY, 0, 0)]
    unnamed x36 -> x24, local copies, waits for them, and re-layouts: 13.2 us -> 2.16 us
    all_to_all x1 -> x0, starting transfers between devices: 7.23 us -> none  [body(): trow = lax.all_to_all(trow, XY, 0, 0)]
    ppermute x1 -> x0, starting transfers between devices: 4.52 us -> none  [body(): lax.ppermute(chip, ZC, [(seat(z, 0), seat(z + 4, 0)) for z in range(NZ)])]
    ppermute x7 -> x4, starting transfers between devices: 14.8 us -> 10.5 us  [along_z(): return lax.ppermute(value, ZC, pairs)]
    ppermute x7 -> x4, waiting for transfers between devices: 10.5 us -> 6.88 us  [along_z(): return lax.ppermute(value, ZC, pairs)]
    pallas_call x1, Pallas kernels: 0.84 us -> 2.27 us  [final(): pl.pallas_call(final_body, out_shape=(jax.ShapeDtypeStruct((1, 1), jnp.fl...]
    pallas_call x3 -> x4, Pallas kernels: 13.3 us -> 14.3 us  [the longest x1 11.1 us: k1(): pl.pallas_call(k1_body, out_shape=(jax.ShapeDtypeStruct((16, 256), jnp.fl...]
  transfers between devices with their start and end apart: 17 -> 12, of which waited for: 9 -> 6; matrix products, arithmetic and copies ran while one was open for 0% -> 0% of each run, Pallas kernels for 0% -> 0%
where the time goes in v4:
time: 110 us; the launch traced here: 108 us
  blocking collectives  44.3 us (40%)
  Pallas kernels  30 us (27%)
  starting transfers between devices  20.4 us (19%)
  waiting for transfers between devices  10.3 us (9%)
  local copies, waits for them, and re-layouts  2.16 us (2%)
    all_to_all x1, blocking collectives, body(): lax.all_to_all(g, XY, 0, 0)  28.5 us
    all_to_all x1, blocking collectives, body(): lax.all_to_all(pack(own, keep, swap(give)), AXES, 0, 0, axis_index_groups...  15.8 us
    pallas_call x1, Pallas kernels, k2(): pl.pallas_call(k2_body, out_shape=jax.ShapeDtypeStruct((NB, SH + 8, 128),...  13.4 us
    pallas_call x1, Pallas kernels, k1(): pl.pallas_call(k1_body, out_shape=(jax.ShapeDtypeStruct((16, 256), jnp.fl...  11.1 us
    ppermute x4, starting transfers between devices, along_z(): return lax.ppermute(value, ZC, pairs)  10.5 us
    all_to_all x1, starting transfers between devices, body(): rows = lax.all_to_all(pay, XY, 0, 0)  7.49 us
    ppermute x4, waiting for transfers between devices, along_z(): return lax.ppermute(value, ZC, pairs)  6.88 us
    ppermute x7, waiting for transfers between devices, swap(): return lax.ppermute(value, 'c', [(0, 1), (1, 0)])  3.4 us
  transfers between devices with their start and end apart: 12, of which 6 were waited for; matrix products, arithmetic and copies ran while one was open for 0% of the time, Pallas kernels for 0%

profile of v4, /device:TPU:2, one launch (start us, length us, event | category | flops | bytes accessed | tf_op | source)
XLA Modules:
  0.0 108.3 jit_solution(14716710743967215038)
XLA Ops:
  0.6 0.0 copy-start
  0.6 0.9 copy-done
  1.5 0.0 copy-start.2
  1.5 0.7 copy-done.2
  2.2 1.2 %shard_map.41 = (bf16[16,208,128]{2,1,0:T(8,128)(2,1)}, bf16[192,128]{1,0:T(8,128)(2,1)S(1)}) custom-call(f32[192,128]{1,0:T(8,128)S(1)} %copy-done, s32[192]{0:T(256)S(1)} %copy-done.2), custom_call_target="tpu_custom_call" | custom-call | tf_op jit(solution)/shard_map/pallas_call | solution.py:329
  3.4 7.5 %all-to-all-start = ((bf16[16,208,128]{2,1,0:T(8,128)(2,1)}), bf16[16,208,128]{2,1,0:T(8,128)(2,1)S(1)}, u32[]{:S(2)}, u32[]{:S(2)}) async-start(bf16[16,208,128]{2,1,0:T(8,128)(2,1)} %get-tuple-element.13), calls=%async_computation | async-start | bytes 1703936 | tf_op jit(solution)/shard_map/all_to_all | solution.py:400
  10.9 0.0 collective-permute-start
  10.9 7.3 %collective-permute-start.7 = (bf16[192,128]{1,0:T(8,128)(2,1)S(1)}, bf16[192,128]{1,0:T(8,128)(2,1)S(1)}, u32[]{:S(2)}, u32[]{:S(2)}) collective-permute-start(bf16[192,128]{1,0:T(8,128)(2,1)S(1)} %get-tuple-element.14), channel_id=1, source_target_pairs={{0,1},{2,3},{4,5},{6,7},{8,9},{10,11},{12,13},{14,15},{1,0},{3,2},... | collective-permute-start | bytes 147464 | tf_op jit(solution)/shard_map/ppermute | solution.py:391
  18.2 0.0 collective-permute-done
  18.2 0.0 copy-start.3
  18.2 2.0 %collective-permute-start.3 = (bf16[2,192,128]{2,1,0:T(8,128)(2,1)S(1)}, bf16[2,192,128]{2,1,0:T(8,128)(2,1)S(1)}, u32[]{:S(2)}, u32[]{:S(2)}) collective-permute-start(bf16[2,192,128]{2,1,0:T(8,128)(2,1)S(1)} %pad_maximum_fusion.pair_ref), channel_id=1, source_target_pairs={{0,12},{2,7},{4,1},{6,11},{8,5},{10,15},{12,9},{14,2},{1,13},{3,6}... | collective-permute-start | bytes 294920 | tf_op jit(solution)/shard_map/ppermute | solution.py:391
  20.2 0.2 collective-permute-start.2
  20.4 1.0 collective-permute-start.1
  21.4 0.1 fusion.8.colid_ref
  21.5 0.0 collective-permute-done.7.d4
  21.5 0.0 copy-start.10
  21.5 1.8 %collective-permute-start.8 = (bf16[192,128]{1,0:T(8,128)(2,1)S(1)}, bf16[192,128]{1,0:T(8,128)(2,1)S(1)}, u32[]{:S(2)}, u32[]{:S(2)}) collective-permute-start(bf16[192,128]{1,0:T(8,128)(2,1)S(1)} %collective-permute-done.7.d4), channel_id=1, source_target_pairs={{0,2},{2,0},{1,3},{3,1},{4,6},{6,4},{5,7},{7,5},{8,10},{10,8},{9,1... | collective-permute-start | bytes 147464 | tf_op jit(solution)/shard_map/ppermute | solution.py:369
  23.4 3.1 %collective-permute-done.3.d3 = bf16[2,192,128]{2,1,0:T(8,128)(2,1)S(1)} collective-permute-done((bf16[2,192,128]{2,1,0:T(8,128)(2,1)S(1)}, bf16[2,192,128]{2,1,0:T(8,128)(2,1)S(1)}, u32[]{:S(2)}, u32[]{:S(2)}) %collective-permute-start.3) | collective-permute-done | bytes 98336 | tf_op jit(solution)/shard_map/ppermute | solution.py:391
  26.4 0.0 copy-start.4
  26.4 0.0 collective-permute-start.6
  26.4 2.0 %collective-permute-done.2.d2 = bf16[2,192,128]{2,1,0:T(8,128)(2,1)S(1)} collective-permute-done((bf16[2,192,128]{2,1,0:T(8,128)(2,1)S(1)}, bf16[2,192,128]{2,1,0:T(8,128)(2,1)S(1)}, u32[]{:S(2)}, u32[]{:S(2)}) %collective-permute-start.2) | collective-permute-done | bytes 98336 | tf_op jit(solution)/shard_map/ppermute | solution.py:391
  28.5 0.0 copy-start.5
  28.5 0.0 collective-permute-start.5
  28.5 1.8 %collective-permute-done.1.d1 = bf16[2,192,128]{2,1,0:T(8,128)(2,1)S(1)} collective-permute-done((bf16[2,192,128]{2,1,0:T(8,128)(2,1)S(1)}, bf16[2,192,128]{2,1,0:T(8,128)(2,1)S(1)}, u32[]{:S(2)}, u32[]{:S(2)}) %collective-permute-start.1) | collective-permute-done | bytes 98336 | tf_op jit(solution)/shard_map/ppermute | solution.py:391
  30.3 0.0 copy-start.6
  30.3 0.0 collective-permute-start.4
  30.3 0.1 pad_add_fusion.own_ref
  30.4 0.0 collective-permute-done.8.s4
  30.4 0.0 copy-start.11
  30.4 0.0 collective-permute-done.6.s3
  30.4 0.0 copy-start.7
  30.4 0.0 collective-permute-done.5.s2
  30.4 0.0 copy-start.8
  30.4 1.2 %collective-permute-done.4.s1 = bf16[2,192,128]{2,1,0:T(8,128)(2,1)S(1)} collective-permute-done((bf16[2,192,128]{2,1,0:T(8,128)(2,1)S(1)}, bf16[2,192,128]{2,1,0:T(8,128)(2,1)S(1)}, u32[]{:S(2)}, u32[]{:S(2)}) %collective-permute-start.4) | collective-permute-done | bytes 98336 | tf_op jit(solution)/shard_map/ppermute | solution.py:369
  31.6 0.0 copy-start.9
  31.6 0.0 all-to-all-done.rows_ref
  31.6 0.0 copy-done.3
  31.6 0.0 copy-done.10
  31.6 0.0 copy-done.4
  31.6 0.0 copy-done.5
  31.6 0.0 copy-done.6
  31.6 0.0 copy-done.11
  31.6 0.0 copy-done.7
  31.6 0.0 copy-done.8
  31.7 0.6 copy-done.9
  32.2 11.1 %shard_map.42 = (f32[16,256]{1,0:T(8,128)S(1)}, f32[16,256]{1,0:T(8,128)S(1)}, bf16[3072,128]{1,0:T(8,128)(2,1)S(1)}, bf16[3072,128]{1,0:T(8,128)(2,1)}, f32[3072,128]{1,0:T(8,128)S(1)}) custom-call(s32[4]{0:T(128)S(1)} %pad_add_fusion.own_ref, bf16[16,208,128]{2,1,0:T(8,128)(2,1)S(1)} %all-to-all-done.rows_ref, bf16[2,192,128]{2,1,0:T(8,128)(2,1)} %copy-done.3, ...), custom_call_target="tpu_custom_call" | custom-call | tf_op jit(solution)/shard_map/pallas_call | solution.py:137
  43.3 0.2 collective-permute-start.9
  43.5 1.0 collective-permute-done.9.got_ref
  44.6 1.5 %shard_map.43 = f32[16,2,16,256]{3,2,1,0:T(8,128)} custom-call(s32[4]{0:T(128)S(1)} %pad_add_fusion.own_ref, f32[16,256]{1,0:T(8,128)S(1)} %get-tuple-element.18.keep_ref, f32[16,256]{1,0:T(8,128)S(1)} %collective-permute-done.9.got_ref), custom_call_target="tpu_custom_call" | custom-call | tf_op jit(solution)/shard_map/pallas_call | solution.py:185
  46.1 15.8 %all_to_all.15.part_ref = f32[16,2,16,256]{3,2,1,0:T(8,128)S(1)} all-to-all(f32[16,2,16,256]{3,2,1,0:T(8,128)} %shard_map.43), channel_id=1, replica_groups={{0,16,32,48,64,80,96,112,128,144,160,176,192,208,224,240},{4,20,36,52,6..., dimensions={0} | all-to-all | bytes 1048576 | tf_op jit(solution)/shard_map/all_to_all | solution.py:411
  61.9 0.6 shard_map.44
  62.4 0.3 collective-permute-start.10
  62.8 1.2 %collective-permute-done.10.got_ref = f32[16,256]{1,0:T(8,128)S(1)} collective-permute-done((f32[16,256]{1,0:T(8,128)S(1)}, f32[16,256]{1,0:T(8,128)S(1)}, u32[]{:S(2)}, u32[]{:S(2)}) %collective-permute-start.10) | collective-permute-done | bytes 16416 | tf_op jit(solution)/shard_map/ppermute | solution.py:369
  63.9 13.4 %shard_map.45 = f32[16,200,128]{2,1,0:T(8,128)S(1)} custom-call(s32[4]{0:T(128)S(1)} %pad_add_fusion.own_ref, bf16[3072,128]{1,0:T(8,128)(2,1)} %get-tuple-element.15.rows_in, f32[3072,128]{1,0:T(8,128)S(1)} %get-tuple-element.16.mates, bf16[3072,128]{1,0:T(8,128)(2,1)S(1)} %get-tuple-element.17.cols_ref, f32[16,256]{1,0:T(8,128)S(1)} %fusion.8.colid_ref, ...), custom_call_target="tpu_custom_call" | custom-call | tf_op jit(solution)/shard_map/pallas_call | solution.py:289
  77.4 0.0 copy-start.1
  77.4 28.5 %all_to_all.16.g_ref = f32[16,200,128]{2,1,0:T(8,128)} all-to-all(f32[16,200,128]{2,1,0:T(8,128)S(1)} %shard_map.45), channel_id=1, replica_groups=mesh['x'=4,'y'=4,'zl'=4,'c'=2,'zh'=2] {'x','y'}, dimensions={0} | all-to-all | bytes 3276800 | tf_op jit(solution)/shard_map/all_to_all | solution.py:415
  105.9 0.0 copy-done.1
  105.9 2.3 %shard_map.46 = (f32[1,1]{1,0:T(1,128)}, f32[192,128]{1,0:T(8,128)}) custom-call(f32[192,128]{1,0:T(8,128)S(1)} %copy-done.1, f32[16,200,128]{2,1,0:T(8,128)} %all_to_all.16.g_ref), custom_call_target="tpu_custom_call" | custom-call | tf_op jit(solution)/shard_map/pallas_call | solution.py:356
  (1 shorter events, 0.0 us)
Async XLA Ops:
  0.6 0.9 copy-start
  1.5 0.7 copy-start.2
  3.4 28.2 %all-to-all-start = ((bf16[16,208,128]{2,1,0:T(8,128)(2,1)}), bf16[16,208,128]{2,1,0:T(8,128)(2,1)S(1)}, u32[]{:S(2)}, u32[]{:S(2)}) async-start(bf16[16,208,128]{2,1,0:T(8,128)(2,1)} %get-tuple-element.13), calls=%async_computation | async-start | bytes 1703936 | tf_op jit(solution)/shard_map/all_to_all | solution.py:400
  10.9 7.3 %collective-permute-start = (bf16[192,128]{1,0:T(8,128)(2,1)S(1)}, bf16[192,128]{1,0:T(8,128)(2,1)S(1)}, u32[]{:S(2)}, u32[]{:S(2)}) collective-permute-start(bf16[192,128]{1,0:T(8,128)(2,1)S(1)} %get-tuple-element.14), channel_id=1, source_target_pairs={{0,2},{2,0},{1,3},{3,1},{4,6},{6,4},{5,7},{7,5},{8,10},{10,8},{9,1... | collective-permute-start | bytes 147464 | tf_op jit(solution)/shard_map/ppermute | solution.py:369
  10.9 10.6 %collective-permute-start.7 = (bf16[192,128]{1,0:T(8,128)(2,1)S(1)}, bf16[192,128]{1,0:T(8,128)(2,1)S(1)}, u32[]{:S(2)}, u32[]{:S(2)}) collective-permute-start(bf16[192,128]{1,0:T(8,128)(2,1)S(1)} %get-tuple-element.14), channel_id=1, source_target_pairs={{0,1},{2,3},{4,5},{6,7},{8,9},{10,11},{12,13},{14,15},{1,0},{3,2},... | collective-permute-start | bytes 147464 | tf_op jit(solution)/shard_map/ppermute | solution.py:391
  18.2 13.4 %copy-start.3 = (bf16[2,192,128]{2,1,0:T(8,128)(2,1)}, bf16[2,192,128]{2,1,0:T(8,128)(2,1)S(1)}, u32[]{:S(2)}) copy-start(bf16[2,192,128]{2,1,0:T(8,128)(2,1)S(1)} %pad_maximum_fusion.pair_ref) | copy-start | bytes 294916
  18.2 8.2 %collective-permute-start.3 = (bf16[2,192,128]{2,1,0:T(8,128)(2,1)S(1)}, bf16[2,192,128]{2,1,0:T(8,128)(2,1)S(1)}, u32[]{:S(2)}, u32[]{:S(2)}) collective-permute-start(bf16[2,192,128]{2,1,0:T(8,128)(2,1)S(1)} %pad_maximum_fusion.pair_ref), channel_id=1, source_target_pairs={{0,12},{2,7},{4,1},{6,11},{8,5},{10,15},{12,9},{14,2},{1,13},{3,6}... | collective-permute-start | bytes 294920 | tf_op jit(solution)/shard_map/ppermute | solution.py:391
  20.2 8.3 %collective-permute-start.2 = (bf16[2,192,128]{2,1,0:T(8,128)(2,1)S(1)}, bf16[2,192,128]{2,1,0:T(8,128)(2,1)S(1)}, u32[]{:S(2)}, u32[]{:S(2)}) collective-permute-start(bf16[2,192,128]{2,1,0:T(8,128)(2,1)S(1)} %pad_maximum_fusion.pair_ref), channel_id=1, source_target_pairs={{0,8},{2,11},{4,12},{6,15},{8,1},{10,2},{12,5},{14,6},{1,9},{3,10}... | collective-permute-start | bytes 294920 | tf_op jit(solution)/shard_map/ppermute | solution.py:391
  20.4 9.9 %collective-permute-start.1 = (bf16[2,192,128]{2,1,0:T(8,128)(2,1)S(1)}, bf16[2,192,128]{2,1,0:T(8,128)(2,1)S(1)}, u32[]{:S(2)}, u32[]{:S(2)}) collective-permute-start(bf16[2,192,128]{2,1,0:T(8,128)(2,1)S(1)} %pad_maximum_fusion.pair_ref), channel_id=1, source_target_pairs={{0,4},{2,15},{4,8},{6,2},{8,12},{10,6},{12,1},{14,10},{1,5},{3,14}... | collective-permute-start | bytes 294920 | tf_op jit(solution)/shard_map/ppermute | solution.py:391
  21.5 10.1 %copy-start.10 = (bf16[192,128]{1,0:T(8,128)(2,1)}, bf16[192,128]{1,0:T(8,128)(2,1)S(1)}, u32[]{:S(2)}) copy-start(bf16[192,128]{1,0:T(8,128)(2,1)S(1)} %collective-permute-done.7.d4) | copy-start | bytes 147460
  21.5 8.8 %collective-permute-start.8 = (bf16[192,128]{1,0:T(8,128)(2,1)S(1)}, bf16[192,128]{1,0:T(8,128)(2,1)S(1)}, u32[]{:S(2)}, u32[]{:S(2)}) collective-permute-start(bf16[192,128]{1,0:T(8,128)(2,1)S(1)} %collective-permute-done.7.d4), channel_id=1, source_target_pairs={{0,2},{2,0},{1,3},{3,1},{4,6},{6,4},{5,7},{7,5},{8,10},{10,8},{9,1... | collective-permute-start | bytes 147464 | tf_op jit(solution)/shard_map/ppermute | solution.py:369
  26.4 5.2 %copy-start.4 = (bf16[2,192,128]{2,1,0:T(8,128)(2,1)}, bf16[2,192,128]{2,1,0:T(8,128)(2,1)S(1)}, u32[]{:S(2)}) copy-start(bf16[2,192,128]{2,1,0:T(8,128)(2,1)S(1)} %collective-permute-done.3.d3) | copy-start | bytes 294916
  26.4 3.9 %collective-permute-start.6 = (bf16[2,192,128]{2,1,0:T(8,128)(2,1)S(1)}, bf16[2,192,128]{2,1,0:T(8,128)(2,1)S(1)}, u32[]{:S(2)}, u32[]{:S(2)}) collective-permute-start(bf16[2,192,128]{2,1,0:T(8,128)(2,1)S(1)} %collective-permute-done.3.d3), channel_id=1, source_target_pairs={{0,2},{2,0},{1,3},{3,1},{4,6},{6,4},{5,7},{7,5},{8,10},{10,8},{9,1... | collective-permute-start | bytes 294920 | tf_op jit(solution)/shard_map/ppermute | solution.py:369
  28.5 3.1 %copy-start.5 = (bf16[2,192,128]{2,1,0:T(8,128)(2,1)}, bf16[2,192,128]{2,1,0:T(8,128)(2,1)S(1)}, u32[]{:S(2)}) copy-start(bf16[2,192,128]{2,1,0:T(8,128)(2,1)S(1)} %collective-permute-done.2.d2) | copy-start | bytes 294916
  28.5 1.9 %collective-permute-start.5 = (bf16[2,192,128]{2,1,0:T(8,128)(2,1)S(1)}, bf16[2,192,128]{2,1,0:T(8,128)(2,1)S(1)}, u32[]{:S(2)}, u32[]{:S(2)}) collective-permute-start(bf16[2,192,128]{2,1,0:T(8,128)(2,1)S(1)} %collective-permute-done.2.d2), channel_id=1, source_target_pairs={{0,2},{2,0},{1,3},{3,1},{4,6},{6,4},{5,7},{7,5},{8,10},{10,8},{9,1... | collective-permute-start | bytes 294920 | tf_op jit(solution)/shard_map/ppermute | solution.py:369
  30.3 1.3 %copy-start.6 = (bf16[2,192,128]{2,1,0:T(8,128)(2,1)}, bf16[2,192,128]{2,1,0:T(8,128)(2,1)S(1)}, u32[]{:S(2)}) copy-start(bf16[2,192,128]{2,1,0:T(8,128)(2,1)S(1)} %collective-permute-done.1.d1) | copy-start | bytes 294916
  30.3 1.3 %collective-permute-start.4 = (bf16[2,192,128]{2,1,0:T(8,128)(2,1)S(1)}, bf16[2,192,128]{2,1,0:T(8,128)(2,1)S(1)}, u32[]{:S(2)}, u32[]{:S(2)}) collective-permute-start(bf16[2,192,128]{2,1,0:T(8,128)(2,1)S(1)} %collective-permute-done.1.d1), channel_id=1, source_target_pairs={{0,2},{2,0},{1,3},{3,1},{4,6},{6,4},{5,7},{7,5},{8,10},{10,8},{9,1... | collective-permute-start | bytes 294920 | tf_op jit(solution)/shard_map/ppermute | solution.py:369
  30.4 1.3 %copy-start.11 = (bf16[192,128]{1,0:T(8,128)(2,1)}, bf16[192,128]{1,0:T(8,128)(2,1)S(1)}, u32[]{:S(2)}) copy-start(bf16[192,128]{1,0:T(8,128)(2,1)S(1)} %collective-permute-done.8.s4) | copy-start | bytes 147460
  30.4 1.3 %copy-start.7 = (bf16[2,192,128]{2,1,0:T(8,128)(2,1)}, bf16[2,192,128]{2,1,0:T(8,128)(2,1)S(1)}, u32[]{:S(2)}) copy-start(bf16[2,192,128]{2,1,0:T(8,128)(2,1)S(1)} %collective-permute-done.6.s3) | copy-start | bytes 294916
  30.4 1.3 %copy-start.8 = (bf16[2,192,128]{2,1,0:T(8,128)(2,1)}, bf16[2,192,128]{2,1,0:T(8,128)(2,1)S(1)}, u32[]{:S(2)}) copy-start(bf16[2,192,128]{2,1,0:T(8,128)(2,1)S(1)} %collective-permute-done.5.s2) | copy-start | bytes 294916
  31.6 0.6 copy-start.9
  43.3 1.3 %collective-permute-start.9 = (f32[16,256]{1,0:T(8,128)S(1)}, f32[16,256]{1,0:T(8,128)S(1)}, u32[]{:S(2)}, u32[]{:S(2)}) collective-permute-start(f32[16,256]{1,0:T(8,128)S(1)} %get-tuple-element.19), channel_id=1, source_target_pairs={{0,2},{2,0},{1,3},{3,1},{4,6},{6,4},{5,7},{7,5},{8,10},{10,8},{9,1... | collective-permute-start | bytes 49160 | tf_op jit(solution)/shard_map/ppermute | solution.py:369
  62.4 1.5 %collective-permute-start.10 = (f32[16,256]{1,0:T(8,128)S(1)}, f32[16,256]{1,0:T(8,128)S(1)}, u32[]{:S(2)}, u32[]{:S(2)}) collective-permute-start(f32[16,256]{1,0:T(8,128)S(1)} %get-tuple-element.21), channel_id=1, source_target_pairs={{0,2},{2,0},{1,3},{3,1},{4,6},{6,4},{5,7},{7,5},{8,10},{10,8},{9,1... | collective-permute-start | bytes 49160 | tf_op jit(solution)/shard_map/ppermute | solution.py:369
  77.4 28.5 %copy-start.1 = (f32[192,128]{1,0:T(8,128)S(1)}, f32[192,128]{1,0:T(8,128)}, u32[]{:S(2)}) copy-start(f32[192,128]{1,0:T(8,128)} %p_ref.3) | copy-start | bytes 294916

commit v5 on v4

--- a/solution.py
+++ b/solution.py
@@ -38,12 +38,12 @@
 
 
 def load_rows(rows_ref, rows, mates, s):
-    rows[pl.ds(s * SH, SH), :] = rows_ref[s, 0:SH, :]
-    code = rows_ref[s, SH:PADR, :]
-    code = code.astype(jnp.float32)
+    at = pl.multiple_of(s * SH, SH)
+    rows[pl.ds(at, SH), :] = rows_ref[s, 0:SH, :]
+    code = rows_ref[s, SH:PADR, :].astype(jnp.float32)
     m = code[0:2] * 256.0 + code[2:4]
-    mates[pl.ds(s * SH, 128), :] = col_bcast(m[0:1])
-    mates[pl.ds(s * SH + 128, 64), :] = col_bcast(m[1:2])[: SH - 128]
+    mates[pl.ds(at, 128), :] = col_bcast(m[0:1])
+    mates[pl.ds(pl.multiple_of(at + 128, 64), 64), :] = col_bcast(m[1:2])[: SH - 128]
 
 
 def diag_rows(b, count):
@@ -56,12 +56,8 @@
     return rid == lanes
 
 
-def k1_body(own_ref, rows_ref, pair_ref, d1, d2, d3, s1, s2, s3, d4, s4, colid_ref,
-            keep_ref, give_ref, cols_ref, rows_out, mates, rows, colsT, racc, hval, cacc, tr, tc, tail, sems):
-    b = own_ref[0]
-    z = own_ref[1]
+def kcols_body(own_ref, pair_ref, d1, d2, d3, s1, s2, s3, d4, s4, cols_ref, colsT, sems):
     core = own_ref[2]
-
     places = [(pair_ref.at[0], core), (pair_ref.at[1], 1 - core), (d4, 8 + core), (s4, 9 - core)]
     for off, ref in ((-1, d1), (-2, d2), (-3, d3), (1, s1), (2, s2), (3, s3)):
         slot = jnp.where(core == 0, off & 7, (-off) & 7) * 2
@@ -73,18 +69,37 @@
         copies.append(pltpu.make_async_copy(piece, to, sems.at[n]))
     for copy in copies:
         copy.start()
-    for q in range(NB):
-        load_rows(rows_ref, rows, mates, q)
     for copy in copies:
         copy.wait()
-    keep = pltpu.make_async_copy(rows, rows_out, sems.at[16])
-    keep.start()
     for c in range(NCH):
         colsT[:, c * CH : (c + 1) * CH] = jnp.transpose(cols_ref[c * CH : (c + 1) * CH, :])
+
+
+def kcols(own, pieces):
+    return pl.pallas_call(
+        kcols_body,
+        out_shape=(
+            jax.ShapeDtypeStruct((C, 128), jnp.bfloat16),
+            jax.ShapeDtypeStruct((128, C), jnp.bfloat16),
+        ),
+        in_specs=[pl.BlockSpec(memory_space=pltpu.SMEM)] + [pl.BlockSpec(memory_space=pltpu.HBM)] * len(pieces),
+        out_specs=(pl.BlockSpec(memory_space=pltpu.VMEM),) * 2,
+        scratch_shapes=[pltpu.SemaphoreType.DMA((16,))],
+        compiler_params=pltpu.CompilerParams(vmem_limit_bytes=6 << 20),
+        cost_estimate=pl.CostEstimate(flops=8*10**9, transcendentals=0, bytes_accessed=1 << 21),
+    )(own, *pieces)
+
+
+def k1_body(own_ref, rows_ref, colsT, colid_ref, keep_ref, give_ref, rows_out, mates, rows, racc, hval, cacc, tr, tc, sems):
+    b = own_ref[0]
+    z = own_ref[1]
+    core = own_ref[2]
     cacc[...] = jnp.zeros_like(cacc)
 
     def tile(t, masked):
         at = pl.multiple_of(t * T1, T1)
+        for q in range(PER1):
+            load_rows(rows_ref, rows, mates, t * PER1 + q)
         u = rows[pl.ds(at, T1), :]
         rid = diag_rows(b, T1) if masked else None
         for c in range(NW):
@@ -108,12 +123,11 @@
                 hval[r : r + SUB, :] = hv
             for l in range(0, CW, 128):
                 cacc[:, c * CW + l : c * CW + l + 128] += sums[l // 128]
-        for q in range(PER1):
-            part = jnp.sum(jnp.transpose(racc[q * SH : (q + 1) * SH, :]), axis=0, keepdims=True)
-            tr[pl.ds(t * PER1 + q, 1), 0:SH] = part
+        for q in range(0, PER1, 2):
+            part = [jnp.sum(jnp.transpose(racc[k * SH : (k + 1) * SH, :]), axis=0, keepdims=True) for k in (q, q + 1)]
+            tr[pl.ds(t * (PER1 // 2) + q // 2, 1), :] = jnp.concatenate(part, axis=1)
         return jnp.sum(hval[...].reshape(T1 // 8, 8, 128), axis=0)
 
-    tr[...] = jnp.ones_like(tr)
     own_tile = b // PER1
     pos = tile(own_tile, True)
 
@@ -121,33 +135,30 @@
         return pos + tile((own_tile + k) & (N1 - 1), False)
 
     pos = lax.fori_loop(1, N1, step, pos)
+    keep = pltpu.make_async_copy(rows, rows_out, sems)
+    keep.start()
     total = jnp.sum(cacc[...], axis=0, keepdims=True)
     for k in range(NZ):
-        at = (z + k) & 7
-        tc[pl.ds(at, 1), :] = total[:, k * 2 * SH : k * 2 * SH + 256]
-        tail[pl.ds(at, 1), :] = total[:, k * 2 * SH + 256 : (k + 1) * 2 * SH]
-    by_rows = tr[...]
-    by_cols = jnp.concatenate([tc[...], jnp.concatenate([tail[...], pos], axis=1)], axis=0)
+        tc[pl.ds((z + k) & 7, 1), :] = total[:, k * 2 * SH : (k + 1) * 2 * SH]
+    none = jnp.zeros((8, 256), jnp.float32)
+    by_rows = jnp.concatenate([tr[...], jnp.zeros((8, 2 * SH), jnp.float32)], axis=0)
+    by_cols = jnp.concatenate([tc[...], jnp.concatenate([pos, none], axis=1)], axis=0)
     keep_ref[...] = jnp.where(core == 0, by_rows, by_cols)
     give_ref[...] = jnp.where(core == 0, by_cols, by_rows)
     keep.wait()
 
 
-def k1(own, rows, pieces, colid):
+def k1(own, rows, colsT, colid):
     return pl.pallas_call(
         k1_body,
         out_shape=(
-            jax.ShapeDtypeStruct((16, 256), jnp.float32),
-            jax.ShapeDtypeStruct((16, 256), jnp.float32),
-            jax.ShapeDtypeStruct((C, 128), jnp.bfloat16),
+            jax.ShapeDtypeStruct((16, 2 * SH), jnp.float32),
+            jax.ShapeDtypeStruct((16, 2 * SH), jnp.float32),
             pltpu.HBM((R, 128), jnp.bfloat16),
             jax.ShapeDtypeStruct((R, 128), jnp.float32),
         ),
-        in_specs=[pl.BlockSpec(memory_space=pltpu.SMEM), pl.BlockSpec(memory_space=pltpu.VMEM)]
-        + [pl.BlockSpec(memory_space=pltpu.HBM)] * len(pieces)
-        + [pl.BlockSpec(memory_space=pltpu.VMEM)],
+        in_specs=[pl.BlockSpec(memory_space=pltpu.SMEM)] + [pl.BlockSpec(memory_space=pltpu.VMEM)] * 3,
         out_specs=(
-            pl.BlockSpec(memory_space=pltpu.VMEM),
             pl.BlockSpec(memory_space=pltpu.VMEM),
             pl.BlockSpec(memory_space=pltpu.VMEM),
             pl.BlockSpec(memory_space=pltpu.HBM),
@@ -155,25 +166,24 @@
         ),
         scratch_shapes=[
             pltpu.VMEM((R, 128), jnp.bfloat16),
-            pltpu.VMEM((128, C), jnp.bfloat16),
             pltpu.VMEM((T1, 128), jnp.float32),
             pltpu.VMEM((T1, 128), jnp.float32),
             pltpu.VMEM((8, C), jnp.float32),
-            pltpu.VMEM((NB, 256), jnp.float32),
-            pltpu.VMEM((8, 256), jnp.float32),
-            pltpu.VMEM((8, 128), jnp.float32),
-            pltpu.SemaphoreType.DMA((17,)),
+            pltpu.VMEM((8, 2 * SH), jnp.float32),
+            pltpu.VMEM((8, 2 * SH), jnp.float32),
+            pltpu.SemaphoreType.DMA,
         ],
         compiler_params=pltpu.CompilerParams(vmem_limit_bytes=12 << 20),
-    )(own, rows, *pieces, colid)
+    )(own, rows, colsT, colid)
 
 
 def pack_body(own_ref, keep_ref, got_ref, pay_ref, both, sems):
     core = own_ref[2]
     mine = keep_ref[...]
     got = got_ref[...]
-    both[0] = mine + jnp.where(core == 0, 0.0, got)
-    both[1] = got
+    low = jnp.where(core == 0, mine[0:8], mine[0:8] + got[0:8])
+    high = jnp.where(core == 0, got[0:8], mine[8:16] + got[8:16])
+    both[...] = jnp.concatenate([low, high], axis=0)
     copies = [pltpu.make_async_copy(both, pay_ref.at[d], sems.at[d]) for d in range(NB)]
     for copy in copies:
         copy.start()
@@ -184,10 +194,10 @@
 def pack(own, keep, got):
     return pl.pallas_call(
         pack_body,
-        out_shape=pltpu.HBM((NB, 2, 16, 256), jnp.float32),
+        out_shape=pltpu.HBM((NB, 16, 2 * SH), jnp.float32),
         in_specs=[pl.BlockSpec(memory_space=pltpu.SMEM)] + [pl.BlockSpec(memory_space=pltpu.VMEM)] * 2,
         out_specs=pl.BlockSpec(memory_space=pltpu.HBM),
-        scratch_shapes=[pltpu.VMEM((2, 16, 256), jnp.float32), pltpu.SemaphoreType.DMA((NB,))],
+        scratch_shapes=[pltpu.VMEM((16, 2 * SH), jnp.float32), pltpu.SemaphoreType.DMA((NB,))],
         compiler_params=pltpu.CompilerParams(vmem_limit_bytes=6 << 20),
     )(own, keep, got)
 
@@ -196,49 +206,44 @@
     core = own_ref[2]
     line = own_ref[3]
 
-    def total(lo, hi, which):
-        out = part_ref[lo, which]
+    def total(lo, hi):
+        out = part_ref[lo]
         for d in range(lo + 1, hi):
-            out = out + part_ref[d, which]
+            out = out + part_ref[d]
         return out
 
-    low = total(0, 8, 0)
-    high = total(8, 16, 0)
+    low = total(0, 8)
+    high = total(8, 16)
     rows = low + high
-    other = total(0, 16, 1)
     cols = jnp.where(line == 0, low, high)
     keep_ref[...] = jnp.where(core == 0, rows, cols)
-    give_ref[...] = jnp.where(core == 0, other, cols)
+    give_ref[...] = jnp.where(core == 0, jnp.concatenate([rows[8:16], rows[0:8]], axis=0), cols)
 
 
 def mid(own, part):
     return pl.pallas_call(
         mid_body,
-        out_shape=(jax.ShapeDtypeStruct((16, 256), jnp.float32),) * 2,
+        out_shape=(jax.ShapeDtypeStruct((16, 2 * SH), jnp.float32),) * 2,
         in_specs=[pl.BlockSpec(memory_space=pltpu.SMEM), pl.BlockSpec(memory_space=pltpu.VMEM)],
         out_specs=(pl.BlockSpec(memory_space=pltpu.VMEM),) * 2,
         compiler_params=pltpu.CompilerParams(vmem_limit_bytes=6 << 20),
     )(own, part)
 
 
-def k2_body(own_ref, rows_in, mates, cols_ref, colid_ref, keep_ref, got_ref, g_ref, rows, ris, colsT, rcol, sem):
+def k2_body(own_ref, rows_in, mates, cols_ref, colsT, colid_ref, keep_ref, got_ref, g_ref, rows, ris, rrow, rcol, sem):
     fetch = pltpu.make_async_copy(rows_in, rows, sem)
     fetch.start()
     b = own_ref[0]
     z = own_ref[1]
     core = own_ref[2]
-    for c in range(NCH):
-        colsT[:, c * CH : (c + 1) * CH] = jnp.transpose(cols_ref[c * CH : (c + 1) * CH, :])
     mine = keep_ref[...]
     got = got_ref[...]
     by_rows = jnp.where(core == 0, mine, got)
     by_cols = jnp.where(core == 0, got, mine)
-    rrow = (1.0 / TAU) / by_rows
-    for q in range(NB):
-        ris[q * SH : (q + 1) * SH, :] = col_bcast(rrow[q : q + 1, 0:SH])
-    tall = jnp.concatenate([by_cols[0:8], by_cols[8:16, 0:128]], axis=1)
+    rrow[...] = (1.0 / TAU) / by_rows[0:8]
+    tall = by_cols[0:8]
     logs = jnp.sum(jnp.log(tall), axis=0, keepdims=True)
-    pos = jnp.sum(by_cols[8:16, 128:256], axis=0, keepdims=True)
+    pos = jnp.sum(by_cols[8:16, 0:128], axis=0, keepdims=True)
     loss = logs[:, 0:128] + logs[:, 128:256] + logs[:, 256:384] - pos * (1.0 / TAU)
     loss = jnp.concatenate([loss, jnp.zeros((7, 128), jnp.float32)], axis=0)
     for d in range(NB):
@@ -249,6 +254,9 @@
 
     def tile(t, masked):
         at = pl.multiple_of(t * T2, T2)
+        for q in range(0, PER2, 2):
+            two = rrow[pl.ds(t * (PER2 // 2) + q // 2, 1), :]
+            ris[q * SH : (q + 2) * SH, :] = col_bcast(two)
         u = rows[pl.ds(at, T2), :]
         rid = diag_rows(b, T2) if masked else None
         acc = jnp.zeros((T2, 128), jnp.float32)
@@ -258,7 +266,7 @@
             for r in range(0, T2, SUB):
                 here = pl.ds(pl.multiple_of(at + r, SUB), SUB)
                 m = mates[here, :]
-                ri = ris[here, :]
+                ri = ris[r : r + SUB, :]
                 ws = []
                 for l in range(0, CW, 128):
                     p = c * CW + l
@@ -285,29 +293,37 @@
     lax.fori_loop(1, N2, step, 0)
 
 
-def k2(own, rows, mates, cols, colid, keep, got):
+def k2(own, rows, mates, cols, colsT, colid, keep, got):
     return pl.pallas_call(
         k2_body,
         out_shape=jax.ShapeDtypeStruct((NB, SH + 8, 128), jnp.float32),
         in_specs=[pl.BlockSpec(memory_space=pltpu.SMEM), pl.BlockSpec(memory_space=pltpu.HBM)]
-        + [pl.BlockSpec(memory_space=pltpu.VMEM)] * 5,
+        + [pl.BlockSpec(memory_space=pltpu.VMEM)] * 6,
         out_specs=pl.BlockSpec(memory_space=pltpu.VMEM),
         scratch_shapes=[
             pltpu.VMEM((R, 128), jnp.bfloat16),
-            pltpu.VMEM((R, 128), jnp.float32),
-            pltpu.VMEM((128, C), jnp.bfloat16),
+            pltpu.VMEM((T2, 128), jnp.float32),
+            pltpu.VMEM((8, 2 * SH), jnp.float32),
             pltpu.VMEM((16, 2 * SH), jnp.float32),
             pltpu.SemaphoreType.DMA,
         ],
         compiler_params=pltpu.CompilerParams(vmem_limit_bytes=12 << 20),
-    )(own, rows, mates, cols, colid, keep, got)
+    )(own, rows, mates, cols, colsT, colid, keep, got)
 
 
 def inverse_norm(p):
     return lax.rsqrt(jnp.sum(p * p, axis=1, keepdims=True) + EPS)
 
 
-def prep_body(p_ref, mate_ref, pay_ref, low_ref, one, sems):
+def prep_body(p_hbm, mate_hbm, q_ref, pay_ref, pair_ref, low_ref, p_ref, mate_ref, one, sems):
+    first = pltpu.make_async_copy(p_hbm, p_ref, sems.at[NB])
+    second = pltpu.make_async_copy(mate_hbm, mate_ref, sems.at[NB + 1])
+    first.start()
+    second.start()
+    q = q_ref[...]
+    pair_ref[1] = (q * inverse_norm(q)).astype(jnp.bfloat16)
+    first.wait()
+    second.wait()
     p = p_ref[...]
     low = (p * inverse_norm(p)).astype(jnp.bfloat16)
     m = mate_ref[...].reshape(1, SH)
@@ -320,23 +336,30 @@
     copies = [pltpu.make_async_copy(one, pay_ref.at[d], sems.at[d]) for d in range(NB)]
     for copy in copies:
         copy.start()
+    pair_ref[0] = low
     low_ref[...] = low
     for copy in copies:
         copy.wait()
 
 
-def prep(p, mate):
+def prep(p, mate, q):
     return pl.pallas_call(
         prep_body,
         out_shape=(
             pltpu.HBM((NB, PADR, 128), jnp.bfloat16),
+            jax.ShapeDtypeStruct((2, SH, 128), jnp.bfloat16),
             jax.ShapeDtypeStruct((SH, 128), jnp.bfloat16),
         ),
-        in_specs=[pl.BlockSpec(memory_space=pltpu.VMEM)] * 2,
-        out_specs=(pl.BlockSpec(memory_space=pltpu.HBM), pl.BlockSpec(memory_space=pltpu.VMEM)),
-        scratch_shapes=[pltpu.VMEM((PADR, 128), jnp.bfloat16), pltpu.SemaphoreType.DMA((NB,))],
+        in_specs=[pl.BlockSpec(memory_space=pltpu.HBM)] * 2 + [pl.BlockSpec(memory_space=pltpu.VMEM)],
+        out_specs=(pl.BlockSpec(memory_space=pltpu.HBM),) + (pl.BlockSpec(memory_space=pltpu.VMEM),) * 2,
+        scratch_shapes=[
+            pltpu.VMEM((SH, 128), jnp.float32),
+            pltpu.VMEM((SH,), jnp.int32),
+            pltpu.VMEM((PADR, 128), jnp.bfloat16),
+            pltpu.SemaphoreType.DMA((NB + 2,)),
+        ],
         compiler_params=pltpu.CompilerParams(vmem_limit_bytes=6 << 20),
-    )(p, mate)
+    )(p, mate, q)
 
 
 def final_body(p_ref, g_ref, loss_ref, grad_ref):
@@ -396,9 +419,10 @@
     z = lax.axis_index(("zh", "zl"))
     core = lax.axis_index("c")
     own = jnp.stack([xy, z, core, lax.axis_index("y") % 2]).astype(jnp.int32)
-    pay, low = prep(projections, partner)
+    near = pltpu.with_memory_space_constraint(projections, pltpu.HBM)
+    mate = pltpu.with_memory_space_constraint(partner, pltpu.HBM)
+    pay, pair, low = prep(near, mate, swap(projections))
     rows = lax.all_to_all(pay, XY, 0, 0)
-    pair = jnp.stack([low, swap(low)])
     direct = [along_z(pair, k) for k in (1, 2, 3)] + [along_z(low, 4)]
     crossed = [swap(piece) for piece in direct]
     pieces = [pair, *direct[:3], *crossed[:3], direct[3], crossed[3]]
@@ -407,12 +431,13 @@
     shard = (zp % 4) * 4 + (p // SH % 2) * 2 + zp // 4
     colid = ((xy * NA + shard) * SH + p % SH).astype(jnp.float32).reshape(16, CH)
     pieces = [pltpu.with_memory_space_constraint(piece, pltpu.HBM) for piece in pieces]
-    keep, give, cols, rows, mates = k1(own, rows, pieces, colid)
+    cols, colsT = kcols(own, pieces)
+    keep, give, rows, mates = k1(own, rows, colsT, colid)
     part = lax.all_to_all(pack(own, keep, swap(give)), AXES, 0, 0, axis_index_groups=total_groups())
     keep, give = mid(own, part)
     rows = pltpu.with_memory_space_constraint(rows, pltpu.HBM)
-    g = k2(own, rows, mates, cols, colid, keep, swap(give))
-    g = pltpu.with_memory_space_constraint(lax.all_to_all(g, XY, 0, 0), pltpu.HBM)
+    g = k2(own, rows, mates, cols, colsT, colid, keep, swap(give))
+    g = lax.all_to_all(g, XY, 0, 0)
     loss, grad = final(projections, g)
     return (loss[0, 0], grad)
 

time: 110 us -> 108 us (0.982)
  blocking collectives: 44.3 us -> 42 us
  waiting for transfers between devices: 10.3 us -> 12.4 us
  local copies, waits for them, and re-layouts: 2.16 us -> 0.9 us
    all_to_all x1, waiting for transfers between devices: 0.01 us -> 6.71 us  [body(): rows = lax.all_to_all(pay, XY, 0, 0)]
    ppermute x4, waiting for transfers between devices: 6.88 us -> 1.26 us  [along_z(): return lax.ppermute(value, ZC, pairs)]
    all_to_all x1, blocking collectives: 15.8 us -> 13.6 us  [body(): lax.all_to_all(pack(own, keep, swap(give)), AXES, 0, 0, axis_index_groups...]
    pallas_call x1, Pallas kernels: 2.27 us -> 0.84 us  [final(): pl.pallas_call(final_body, out_shape=(jax.ShapeDtypeStruct((1, 1), jnp.fl...]
    unnamed x24 -> x20, local copies, waits for them, and re-layouts: 2.16 us -> 0.9 us
    pallas_call x3 -> x4, Pallas kernels: 13.1 us -> 13.2 us  [the longest x1 9.15 us: k1(): pl.pallas_call(k1_body, out_shape=(jax.ShapeDtypeStruct((16, 2 * SH), jnp...]
  transfers between devices with their start and end apart: 12 -> 12, of which waited for: 6 -> 8; matrix products, arithmetic and copies ran while one was open for 0% -> 0% of each run, Pallas kernels for 0% -> 2%
where the time goes in v5:
time: 108 us; the launch traced here: 106 us
  blocking collectives  42 us (39%)
  Pallas kernels  29.4 us (27%)
  starting transfers between devices  20 us (19%)
  waiting for transfers between devices  12.4 us (11%)
    all_to_all x1, blocking collectives, body(): g = lax.all_to_all(g, XY, 0, 0)  28.4 us
    all_to_all x1, blocking collectives, body(): lax.all_to_all(pack(own, keep, swap(give)), AXES, 0, 0, axis_index_groups...  13.6 us
    pallas_call x1, Pallas kernels, k2(): pl.pallas_call(k2_body, out_shape=jax.ShapeDtypeStruct((NB, SH + 8, 128),...  13.3 us
    ppermute x4, starting transfers between devices, along_z(): return lax.ppermute(value, ZC, pairs)  9.85 us
    pallas_call x1, Pallas kernels, k1(): pl.pallas_call(k1_body, out_shape=(jax.ShapeDtypeStruct((16, 2 * SH), jnp...  9.15 us
    all_to_all x1, starting transfers between devices, body(): rows = lax.all_to_all(pay, XY, 0, 0)  7.49 us
    all_to_all x1, waiting for transfers between devices, body(): rows = lax.all_to_all(pay, XY, 0, 0)  6.71 us
    ppermute x7, waiting for transfers between devices, swap(): return lax.ppermute(value, 'c', [(0, 1), (1, 0)])  4.45 us
  transfers between devices with their start and end apart: 12, of which 8 were waited for; matrix products, arithmetic and copies ran while one was open for 0% of the time, Pallas kernels for 2%

profile of v5, /device:TPU:2, one launch (start us, length us, event | category | flops | bytes accessed | tf_op | source)
XLA Modules:
  0.0 105.8 jit_solution(10796571700170780513)
XLA Ops:
  0.6 0.1 collective-permute-start
  0.7 1.5 %collective-permute-done.q_ref = f32[192,128]{1,0:T(8,128)S(1)} collective-permute-done((f32[192,128]{1,0:T(8,128)}, f32[192,128]{1,0:T(8,128)S(1)}, u32[]{:S(2)}, u32[]{:S(2)}) %collective-permute-start) | collective-permute-done | bytes 98336 | tf_op jit(solution)/shard_map/ppermute | solution.py:392
  2.2 2.1 %shard_map.41 = (bf16[16,208,128]{2,1,0:T(8,128)(2,1)}, bf16[2,192,128]{2,1,0:T(8,128)(2,1)S(1)}, bf16[192,128]{1,0:T(8,128)(2,1)S(1)}) custom-call(f32[192,128]{1,0:T(8,128)} %p_ref.1, s32[192]{0:T(256)} %mate_hbm.1, f32[192,128]{1,0:T(8,128)S(1)} %collective-permute-done.q_ref), custom_call_target="tpu_custom_call" | custom-call | tf_op jit(solution)/shard_map/pallas_call | solution.py:346
  4.3 0.0 copy-start.1
  4.3 4.7 %collective-permute-start.3 = (bf16[2,192,128]{2,1,0:T(8,128)(2,1)S(1)}, bf16[2,192,128]{2,1,0:T(8,128)(2,1)S(1)}, u32[]{:S(2)}, u32[]{:S(2)}) collective-permute-start(bf16[2,192,128]{2,1,0:T(8,128)(2,1)S(1)} %get-tuple-element.16.pair_ref), channel_id=1, source_target_pairs={{0,12},{2,7},{4,1},{6,11},{8,5},{10,15},{12,9},{14,2},{1,13},{3,6}... | collective-permute-start | bytes 294920 | tf_op jit(solution)/shard_map/ppermute | solution.py:414
  9.0 3.6 %collective-permute-start.2 = (bf16[2,192,128]{2,1,0:T(8,128)(2,1)S(1)}, bf16[2,192,128]{2,1,0:T(8,128)(2,1)S(1)}, u32[]{:S(2)}, u32[]{:S(2)}) collective-permute-start(bf16[2,192,128]{2,1,0:T(8,128)(2,1)S(1)} %get-tuple-element.16.pair_ref), channel_id=1, source_target_pairs={{0,8},{2,11},{4,12},{6,15},{8,1},{10,2},{12,5},{14,6},{1,9},{3,10}... | collective-permute-start | bytes 294920 | tf_op jit(solution)/shard_map/ppermute | solution.py:414
  12.6 1.0 collective-permute-start.1
  13.6 0.5 collective-permute-start.7
  14.2 0.1 fusion.8.colid_ref
  14.3 7.5 %all-to-all-start = ((bf16[16,208,128]{2,1,0:T(8,128)(2,1)}), bf16[16,208,128]{2,1,0:T(8,128)(2,1)S(1)}, u32[]{:S(2)}, u32[]{:S(2)}) async-start(bf16[16,208,128]{2,1,0:T(8,128)(2,1)} %get-tuple-element.15), calls=%async_computation | async-start | bytes 1703936 | tf_op jit(solution)/shard_map/all_to_all | solution.py:425
  21.8 1.3 %collective-permute-done.7.d4 = bf16[192,128]{1,0:T(8,128)(2,1)S(1)} collective-permute-done((bf16[192,128]{1,0:T(8,128)(2,1)S(1)}, bf16[192,128]{1,0:T(8,128)(2,1)S(1)}, u32[]{:S(2)}, u32[]{:S(2)}) %collective-permute-start.7) | collective-permute-done | bytes 49184 | tf_op jit(solution)/shard_map/ppermute | solution.py:414
  23.0 0.0 copy-start.8
  23.0 0.3 collective-permute-start.8
  23.4 0.0 collective-permute-done.3.d3
  23.4 0.0 copy-start.2
  23.4 0.2 collective-permute-start.6
  23.5 0.0 collective-permute-done.2.d2
  23.5 0.0 copy-start.3
  23.5 0.3 collective-permute-start.5
  23.9 0.0 collective-permute-done.1.d1
  23.9 0.0 copy-start.4
  23.9 0.3 collective-permute-start.4
  24.2 0.1 pad_add_fusion.own_ref
  24.3 0.0 collective-permute-done.8.s4
  24.3 0.0 copy-start.9
  24.3 0.4 collective-permute-done.6.s3
  24.7 0.0 copy-start.5
  24.7 0.2 collective-permute-done.5.s2
  24.8 0.0 copy-start.6
  24.8 0.4 collective-permute-done.4.s1
  25.2 0.0 copy-done.1
  25.2 0.0 copy-done.8
  25.2 0.0 copy-done.2
  25.2 0.0 copy-done.3
  25.2 0.0 copy-done.4
  25.2 0.0 copy-done.9
  25.2 0.1 copy-done.5
  25.3 0.2 copy-done.6
  25.5 0.0 copy-start.7
  25.5 0.6 copy-done.7
  26.1 2.1 %shard_map.42 = (bf16[3072,128]{1,0:T(8,128)(2,1)S(1)}, bf16[128,3072]{1,0:T(8,128)(2,1)S(1)}) custom-call(s32[4]{0:T(128)S(1)} %pad_add_fusion.own_ref, bf16[2,192,128]{2,1,0:T(8,128)(2,1)} %copy-done.1, bf16[2,192,128]{2,1,0:T(8,128)(2,1)} %copy-done.4, bf16[2,192,128]{2,1,0:T(8,128)(2,1)} %copy-done.3, bf16[2,192,128]{2,1,0:T(8,128)(2,1)} %copy-done.2, ...), custom_call_target="tpu_custom_call" | custom-call | flops 8000000000 | bytes 2097152 | tf_op jit(solution)/shard_map/pallas_call | solution.py:79
  28.2 6.7 %all-to-all-done.rows_ref = bf16[16,208,128]{2,1,0:T(8,128)(2,1)S(1)} async-done(((bf16[16,208,128]{2,1,0:T(8,128)(2,1)}), bf16[16,208,128]{2,1,0:T(8,128)(2,1)S(1)}, u32[]{:S(2)}, u32[]{:S(2)}) %all-to-all-start) | async-done | bytes 852000 | tf_op jit(solution)/shard_map/all_to_all | solution.py:425
  34.9 9.1 %shard_map.43 = (f32[16,384]{1,0:T(8,128)S(1)}, f32[16,384]{1,0:T(8,128)S(1)}, bf16[3072,128]{1,0:T(8,128)(2,1)}, f32[3072,128]{1,0:T(8,128)S(1)}) custom-call(s32[4]{0:T(128)S(1)} %pad_add_fusion.own_ref, bf16[16,208,128]{2,1,0:T(8,128)(2,1)S(1)} %all-to-all-done.rows_ref, bf16[128,3072]{1,0:T(8,128)(2,1)S(1)} %get-tuple-element.18.colsT, ...), custom_call_target="tpu_custom_call" | custom-call | tf_op jit(solution)/shard_map/pallas_call | solution.py:152
  44.0 1.1 %collective-permute-start.9 = (f32[16,384]{1,0:T(8,128)S(1)}, f32[16,384]{1,0:T(8,128)S(1)}, u32[]{:S(2)}, u32[]{:S(2)}) collective-permute-start(f32[16,384]{1,0:T(8,128)S(1)} %get-tuple-element.23), channel_id=1, source_target_pairs={{0,2},{2,0},{1,3},{3,1},{4,6},{6,4},{5,7},{7,5},{8,10},{10,8},{9,1... | collective-permute-start | bytes 73736 | tf_op jit(solution)/shard_map/ppermute | solution.py:392
  45.1 0.8 collective-permute-done.9.got_ref
  46.0 1.5 %shard_map.44 = f32[16,16,384]{2,1,0:T(8,128)} custom-call(s32[4]{0:T(128)S(1)} %pad_add_fusion.own_ref, f32[16,384]{1,0:T(8,128)S(1)} %get-tuple-element.22.keep_ref, f32[16,384]{1,0:T(8,128)S(1)} %collective-permute-done.9.got_ref), custom_call_target="tpu_custom_call" | custom-call | tf_op jit(solution)/shard_map/pallas_call | solution.py:195
  47.4 13.6 %all_to_all.15.part_ref = f32[16,16,384]{2,1,0:T(8,128)S(1)} all-to-all(f32[16,16,384]{2,1,0:T(8,128)} %shard_map.44), channel_id=1, replica_groups={{0,16,32,48,64,80,96,112,128,144,160,176,192,208,224,240},{4,20,36,52,6..., dimensions={0} | all-to-all | bytes 786432 | tf_op jit(solution)/shard_map/all_to_all | solution.py:436
  61.0 0.6 shard_map.45
  61.6 0.3 collective-permute-start.10
  61.9 1.2 %collective-permute-done.10.got_ref = f32[16,384]{1,0:T(8,128)S(1)} collective-permute-done((f32[16,384]{1,0:T(8,128)S(1)}, f32[16,384]{1,0:T(8,128)S(1)}, u32[]{:S(2)}, u32[]{:S(2)}) %collective-permute-start.10) | collective-permute-done | bytes 24608 | tf_op jit(solution)/shard_map/ppermute | solution.py:392
  63.1 13.3 %shard_map.46 = f32[16,200,128]{2,1,0:T(8,128)S(1)} custom-call(s32[4]{0:T(128)S(1)} %pad_add_fusion.own_ref, bf16[3072,128]{1,0:T(8,128)(2,1)} %get-tuple-element.19.rows_in, f32[3072,128]{1,0:T(8,128)S(1)} %get-tuple-element.20.mates, bf16[3072,128]{1,0:T(8,128)(2,1)S(1)} %get-tuple-element.21.cols_ref, bf16[128,3072]{1,0:T(8,128)(2,1)S(1)} %get-tuple-element.18.colsT, ...), custom_call_target="tpu_custom_call" | custom-call | tf_op jit(solution)/shard_map/pallas_call | solution.py:297
  76.4 0.0 copy-start
  76.4 28.4 %all_to_all.16.g_ref = f32[16,200,128]{2,1,0:T(8,128)S(1)} all-to-all(f32[16,200,128]{2,1,0:T(8,128)S(1)} %shard_map.46), channel_id=1, replica_groups=mesh['x'=4,'y'=4,'zl'=4,'c'=2,'zh'=2] {'x','y'}, dimensions={0} | all-to-all | bytes 3276800 | tf_op jit(solution)/shard_map/all_to_all | solution.py:440
  104.8 0.0 copy-done
  104.8 0.8 shard_map.47
Async XLA Ops:
  0.6 1.6 %collective-permute-start = (f32[192,128]{1,0:T(8,128)}, f32[192,128]{1,0:T(8,128)S(1)}, u32[]{:S(2)}, u32[]{:S(2)}) collective-permute-start(f32[192,128]{1,0:T(8,128)} %p_ref.1), channel_id=1, source_target_pairs={{0,2},{2,0},{1,3},{3,1},{4,6},{6,4},{5,7},{7,5},{8,10},{10,8},{9,1... | collective-permute-start | bytes 294920 | tf_op jit(solution)/shard_map/ppermute | solution.py:392
  4.3 20.9 %copy-start.1 = (bf16[2,192,128]{2,1,0:T(8,128)(2,1)}, bf16[2,192,128]{2,1,0:T(8,128)(2,1)S(1)}, u32[]{:S(2)}) copy-start(bf16[2,192,128]{2,1,0:T(8,128)(2,1)S(1)} %get-tuple-element.16.pair_ref) | copy-start | bytes 294916
  4.3 19.0 %collective-permute-start.3 = (bf16[2,192,128]{2,1,0:T(8,128)(2,1)S(1)}, bf16[2,192,128]{2,1,0:T(8,128)(2,1)S(1)}, u32[]{:S(2)}, u32[]{:S(2)}) collective-permute-start(bf16[2,192,128]{2,1,0:T(8,128)(2,1)S(1)} %get-tuple-element.16.pair_ref), channel_id=1, source_target_pairs={{0,12},{2,7},{4,1},{6,11},{8,5},{10,15},{12,9},{14,2},{1,13},{3,6}... | collective-permute-start | bytes 294920 | tf_op jit(solution)/shard_map/ppermute | solution.py:414
  9.0 14.5 %collective-permute-start.2 = (bf16[2,192,128]{2,1,0:T(8,128)(2,1)S(1)}, bf16[2,192,128]{2,1,0:T(8,128)(2,1)S(1)}, u32[]{:S(2)}, u32[]{:S(2)}) collective-permute-start(bf16[2,192,128]{2,1,0:T(8,128)(2,1)S(1)} %get-tuple-element.16.pair_ref), channel_id=1, source_target_pairs={{0,8},{2,11},{4,12},{6,15},{8,1},{10,2},{12,5},{14,6},{1,9},{3,10}... | collective-permute-start | bytes 294920 | tf_op jit(solution)/shard_map/ppermute | solution.py:414
  12.6 11.3 %collective-permute-start.1 = (bf16[2,192,128]{2,1,0:T(8,128)(2,1)S(1)}, bf16[2,192,128]{2,1,0:T(8,128)(2,1)S(1)}, u32[]{:S(2)}, u32[]{:S(2)}) collective-permute-start(bf16[2,192,128]{2,1,0:T(8,128)(2,1)S(1)} %get-tuple-element.16.pair_ref), channel_id=1, source_target_pairs={{0,4},{2,15},{4,8},{6,2},{8,12},{10,6},{12,1},{14,10},{1,5},{3,14}... | collective-permute-start | bytes 294920 | tf_op jit(solution)/shard_map/ppermute | solution.py:414
  13.6 9.4 %collective-permute-start.7 = (bf16[192,128]{1,0:T(8,128)(2,1)S(1)}, bf16[192,128]{1,0:T(8,128)(2,1)S(1)}, u32[]{:S(2)}, u32[]{:S(2)}) collective-permute-start(bf16[192,128]{1,0:T(8,128)(2,1)S(1)} %get-tuple-element.17), channel_id=1, source_target_pairs={{0,1},{2,3},{4,5},{6,7},{8,9},{10,11},{12,13},{14,15},{1,0},{3,2},... | collective-permute-start | bytes 147464 | tf_op jit(solution)/shard_map/ppermute | solution.py:414
  14.3 20.6 %all-to-all-start = ((bf16[16,208,128]{2,1,0:T(8,128)(2,1)}), bf16[16,208,128]{2,1,0:T(8,128)(2,1)S(1)}, u32[]{:S(2)}, u32[]{:S(2)}) async-start(bf16[16,208,128]{2,1,0:T(8,128)(2,1)} %get-tuple-element.15), calls=%async_computation | async-start | bytes 1703936 | tf_op jit(solution)/shard_map/all_to_all | solution.py:425
  23.0 2.2 %copy-start.8 = (bf16[192,128]{1,0:T(8,128)(2,1)}, bf16[192,128]{1,0:T(8,128)(2,1)S(1)}, u32[]{:S(2)}) copy-start(bf16[192,128]{1,0:T(8,128)(2,1)S(1)} %collective-permute-done.7.d4) | copy-start | bytes 147460
  23.0 1.2 %collective-permute-start.8 = (bf16[192,128]{1,0:T(8,128)(2,1)S(1)}, bf16[192,128]{1,0:T(8,128)(2,1)S(1)}, u32[]{:S(2)}, u32[]{:S(2)}) collective-permute-start(bf16[192,128]{1,0:T(8,128)(2,1)S(1)} %collective-permute-done.7.d4), channel_id=1, source_target_pairs={{0,2},{2,0},{1,3},{3,1},{4,6},{6,4},{5,7},{7,5},{8,10},{10,8},{9,1... | collective-permute-start | bytes 147464 | tf_op jit(solution)/shard_map/ppermute | solution.py:392
  23.4 1.8 %copy-start.2 = (bf16[2,192,128]{2,1,0:T(8,128)(2,1)}, bf16[2,192,128]{2,1,0:T(8,128)(2,1)S(1)}, u32[]{:S(2)}) copy-start(bf16[2,192,128]{2,1,0:T(8,128)(2,1)S(1)} %collective-permute-done.3.d3) | copy-start | bytes 294916
  23.4 1.3 %collective-permute-start.6 = (bf16[2,192,128]{2,1,0:T(8,128)(2,1)S(1)}, bf16[2,192,128]{2,1,0:T(8,128)(2,1)S(1)}, u32[]{:S(2)}, u32[]{:S(2)}) collective-permute-start(bf16[2,192,128]{2,1,0:T(8,128)(2,1)S(1)} %collective-permute-done.3.d3), channel_id=1, source_target_pairs={{0,2},{2,0},{1,3},{3,1},{4,6},{6,4},{5,7},{7,5},{8,10},{10,8},{9,1... | collective-permute-start | bytes 294920 | tf_op jit(solution)/shard_map/ppermute | solution.py:392
  23.5 1.7 %copy-start.3 = (bf16[2,192,128]{2,1,0:T(8,128)(2,1)}, bf16[2,192,128]{2,1,0:T(8,128)(2,1)S(1)}, u32[]{:S(2)}) copy-start(bf16[2,192,128]{2,1,0:T(8,128)(2,1)S(1)} %collective-permute-done.2.d2) | copy-start | bytes 294916
  23.5 1.3 %collective-permute-start.5 = (bf16[2,192,128]{2,1,0:T(8,128)(2,1)S(1)}, bf16[2,192,128]{2,1,0:T(8,128)(2,1)S(1)}, u32[]{:S(2)}, u32[]{:S(2)}) collective-permute-start(bf16[2,192,128]{2,1,0:T(8,128)(2,1)S(1)} %collective-permute-done.2.d2), channel_id=1, source_target_pairs={{0,2},{2,0},{1,3},{3,1},{4,6},{6,4},{5,7},{7,5},{8,10},{10,8},{9,1... | collective-permute-start | bytes 294920 | tf_op jit(solution)/shard_map/ppermute | solution.py:392
  23.9 1.3 %copy-start.4 = (bf16[2,192,128]{2,1,0:T(8,128)(2,1)}, bf16[2,192,128]{2,1,0:T(8,128)(2,1)S(1)}, u32[]{:S(2)}) copy-start(bf16[2,192,128]{2,1,0:T(8,128)(2,1)S(1)} %collective-permute-done.1.d1) | copy-start | bytes 294916
  23.9 1.3 %collective-permute-start.4 = (bf16[2,192,128]{2,1,0:T(8,128)(2,1)S(1)}, bf16[2,192,128]{2,1,0:T(8,128)(2,1)S(1)}, u32[]{:S(2)}, u32[]{:S(2)}) collective-permute-start(bf16[2,192,128]{2,1,0:T(8,128)(2,1)S(1)} %collective-permute-done.1.d1), channel_id=1, source_target_pairs={{0,2},{2,0},{1,3},{3,1},{4,6},{6,4},{5,7},{7,5},{8,10},{10,8},{9,1... | collective-permute-start | bytes 294920 | tf_op jit(solution)/shard_map/ppermute | solution.py:392
  24.3 1.0 copy-start.9
  24.7 0.6 copy-start.5
  24.8 0.6 copy-start.6
  25.5 0.6 copy-start.7
  44.0 1.9 %collective-permute-start.9 = (f32[16,384]{1,0:T(8,128)S(1)}, f32[16,384]{1,0:T(8,128)S(1)}, u32[]{:S(2)}, u32[]{:S(2)}) collective-permute-start(f32[16,384]{1,0:T(8,128)S(1)} %get-tuple-element.23), channel_id=1, source_target_pairs={{0,2},{2,0},{1,3},{3,1},{4,6},{6,4},{5,7},{7,5},{8,10},{10,8},{9,1... | collective-permute-start | bytes 73736 | tf_op jit(solution)/shard_map/ppermute | solution.py:392
  61.6 1.5 %collective-permute-start.10 = (f32[16,384]{1,0:T(8,128)S(1)}, f32[16,384]{1,0:T(8,128)S(1)}, u32[]{:S(2)}, u32[]{:S(2)}) collective-permute-start(f32[16,384]{1,0:T(8,128)S(1)} %get-tuple-element.25), channel_id=1, source_target_pairs={{0,2},{2,0},{1,3},{3,1},{4,6},{6,4},{5,7},{7,5},{8,10},{10,8},{9,1... | collective-permute-start | bytes 73736 | tf_op jit(solution)/shard_map/ppermute | solution.py:392
  76.4 28.4 %copy-start = (f32[192,128]{1,0:T(8,128)S(1)}, f32[192,128]{1,0:T(8,128)}, u32[]{:S(2)}) copy-start(f32[192,128]{1,0:T(8,128)} %p_ref.1) | copy-start | bytes 294916

commit v6 on v5

--- a/solution.py
+++ b/solution.py
@@ -86,7 +86,7 @@
         out_specs=(pl.BlockSpec(memory_space=pltpu.VMEM),) * 2,
         scratch_shapes=[pltpu.SemaphoreType.DMA((16,))],
         compiler_params=pltpu.CompilerParams(vmem_limit_bytes=6 << 20),
-        cost_estimate=pl.CostEstimate(flops=8*10**9, transcendentals=0, bytes_accessed=1 << 21),
+        cost_estimate=pl.CostEstimate(flops=10**9, transcendentals=0, bytes_accessed=1 << 21),
     )(own, *pieces)
 
 
@@ -315,13 +315,11 @@
     return lax.rsqrt(jnp.sum(p * p, axis=1, keepdims=True) + EPS)
 
 
-def prep_body(p_hbm, mate_hbm, q_ref, pay_ref, pair_ref, low_ref, p_ref, mate_ref, one, sems):
+def prep_body(p_hbm, mate_hbm, pay_ref, low_ref, p_ref, mate_ref, one, sems):
     first = pltpu.make_async_copy(p_hbm, p_ref, sems.at[NB])
     second = pltpu.make_async_copy(mate_hbm, mate_ref, sems.at[NB + 1])
     first.start()
     second.start()
-    q = q_ref[...]
-    pair_ref[1] = (q * inverse_norm(q)).astype(jnp.bfloat16)
     first.wait()
     second.wait()
     p = p_ref[...]
@@ -336,22 +334,20 @@
     copies = [pltpu.make_async_copy(one, pay_ref.at[d], sems.at[d]) for d in range(NB)]
     for copy in copies:
         copy.start()
-    pair_ref[0] = low
     low_ref[...] = low
     for copy in copies:
         copy.wait()
 
 
-def prep(p, mate, q):
+def prep(p, mate):
     return pl.pallas_call(
         prep_body,
         out_shape=(
             pltpu.HBM((NB, PADR, 128), jnp.bfloat16),
-            jax.ShapeDtypeStruct((2, SH, 128), jnp.bfloat16),
             jax.ShapeDtypeStruct((SH, 128), jnp.bfloat16),
         ),
-        in_specs=[pl.BlockSpec(memory_space=pltpu.HBM)] * 2 + [pl.BlockSpec(memory_space=pltpu.VMEM)],
-        out_specs=(pl.BlockSpec(memory_space=pltpu.HBM),) + (pl.BlockSpec(memory_space=pltpu.VMEM),) * 2,
+        in_specs=[pl.BlockSpec(memory_space=pltpu.HBM)] * 2,
+        out_specs=(pl.BlockSpec(memory_space=pltpu.HBM), pl.BlockSpec(memory_space=pltpu.VMEM)),
         scratch_shapes=[
             pltpu.VMEM((SH, 128), jnp.float32),
             pltpu.VMEM((SH,), jnp.int32),
@@ -359,7 +355,7 @@
             pltpu.SemaphoreType.DMA((NB + 2,)),
         ],
         compiler_params=pltpu.CompilerParams(vmem_limit_bytes=6 << 20),
-    )(p, mate, q)
+    )(p, mate)
 
 
 def final_body(p_ref, g_ref, loss_ref, grad_ref):
@@ -419,10 +415,9 @@
     z = lax.axis_index(("zh", "zl"))
     core = lax.axis_index("c")
     own = jnp.stack([xy, z, core, lax.axis_index("y") % 2]).astype(jnp.int32)
-    near = pltpu.with_memory_space_constraint(projections, pltpu.HBM)
-    mate = pltpu.with_memory_space_constraint(partner, pltpu.HBM)
-    pay, pair, low = prep(near, mate, swap(projections))
+    pay, low = prep(pltpu.with_memory_space_constraint(projections, pltpu.HBM), pltpu.with_memory_space_constraint(partner, pltpu.HBM))
     rows = lax.all_to_all(pay, XY, 0, 0)
+    pair = jnp.stack([low, swap(low)])
     direct = [along_z(pair, k) for k in (1, 2, 3)] + [along_z(low, 4)]
     crossed = [swap(piece) for piece in direct]
     pieces = [pair, *direct[:3], *crossed[:3], direct[3], crossed[3]]

time: 108 us -> 106 us (0.981); the launches traced: 106 us -> 105 us
  waiting for transfers between devices: 12.4 us -> 10.3 us
  blocking collectives: 42 us -> 43.1 us
    all_to_all x1, waiting for transfers between devices: 6.71 us -> 0.01 us  [body(): rows = lax.all_to_all(pay, XY, 0, 0)]
    ppermute x4, waiting for transfers between devices: 1.26 us -> 6.88 us  [along_z(): return lax.ppermute(value, ZC, pairs)]
  transfers between devices with their start and end apart: 12 -> 12, of which waited for: 8 -> 6; matrix products, arithmetic and copies ran while one was open for 0% -> 0% of each run, Pallas kernels for 2% -> 2%
where the time goes in v6:
time: 106 us; the launch traced here: 105 us
  blocking collectives  43.1 us (41%)
  Pallas kernels  29.4 us (28%)
  starting transfers between devices  20.4 us (19%)
  waiting for transfers between devices  10.3 us (10%)
    all_to_all x1, blocking collectives, body(): g = lax.all_to_all(g, XY, 0, 0)  28.5 us
    all_to_all x1, blocking collectives, body(): lax.all_to_all(pack(own, keep, swap(give)), AXES, 0, 0, axis_index_groups...  14.6 us
    pallas_call x1, Pallas kernels, k2(): pl.pallas_call(k2_body, out_shape=jax.ShapeDtypeStruct((NB, SH + 8, 128),...  13.3 us
    ppermute x4, starting transfers between devices, along_z(): return lax.ppermute(value, ZC, pairs)  10.5 us
    pallas_call x1, Pallas kernels, k1(): pl.pallas_call(k1_body, out_shape=(jax.ShapeDtypeStruct((16, 2 * SH), jnp...  9.15 us
    all_to_all x1, starting transfers between devices, body(): rows = lax.all_to_all(pay, XY, 0, 0)  7.49 us
    ppermute x4, waiting for transfers between devices, along_z(): return lax.ppermute(value, ZC, pairs)  6.88 us
    ppermute x7, waiting for transfers between devices, swap(): return lax.ppermute(value, 'c', [(0, 1), (1, 0)])  3.41 us
  transfers between devices with their start and end apart: 12, of which 6 were waited for; matrix products, arithmetic and copies ran while one was open for 0% of the time, Pallas kernels for 2%

profile of v6, /device:TPU:2, one launch (start us, length us, event | category | flops | bytes accessed | tf_op | source)
XLA Modules:
  0.0 105.0 jit_solution(15790862103257726177)
XLA Ops:
  0.6 2.1 %shard_map.41 = (bf16[16,208,128]{2,1,0:T(8,128)(2,1)}, bf16[192,128]{1,0:T(8,128)(2,1)S(1)}) custom-call(f32[192,128]{1,0:T(8,128)} %p_ref.1, s32[192]{0:T(256)} %mate_hbm.1), custom_call_target="tpu_custom_call" | custom-call | tf_op jit(solution)/shard_map/pallas_call | solution.py:343
  2.7 7.5 %all-to-all-start = ((bf16[16,208,128]{2,1,0:T(8,128)(2,1)}), bf16[16,208,128]{2,1,0:T(8,128)(2,1)S(1)}, u32[]{:S(2)}, u32[]{:S(2)}) async-start(bf16[16,208,128]{2,1,0:T(8,128)(2,1)} %get-tuple-element.14), calls=%async_computation | async-start | bytes 1703936 | tf_op jit(solution)/shard_map/all_to_all | solution.py:419
  10.2 0.0 collective-permute-start
  10.2 7.3 %collective-permute-start.7 = (bf16[192,128]{1,0:T(8,128)(2,1)S(1)}, bf16[192,128]{1,0:T(8,128)(2,1)S(1)}, u32[]{:S(2)}, u32[]{:S(2)}) collective-permute-start(bf16[192,128]{1,0:T(8,128)(2,1)S(1)} %get-tuple-element.15), channel_id=1, source_target_pairs={{0,1},{2,3},{4,5},{6,7},{8,9},{10,11},{12,13},{14,15},{1,0},{3,2},... | collective-permute-start | bytes 147464 | tf_op jit(solution)/shard_map/ppermute | solution.py:410
  17.5 0.0 collective-permute-done
  17.5 0.0 copy-start.1
  17.5 2.0 %collective-permute-start.3 = (bf16[2,192,128]{2,1,0:T(8,128)(2,1)S(1)}, bf16[2,192,128]{2,1,0:T(8,128)(2,1)S(1)}, u32[]{:S(2)}, u32[]{:S(2)}) collective-permute-start(bf16[2,192,128]{2,1,0:T(8,128)(2,1)S(1)} %pad_maximum_fusion.pair_ref), channel_id=1, source_target_pairs={{0,12},{2,7},{4,1},{6,11},{8,5},{10,15},{12,9},{14,2},{1,13},{3,6}... | collective-permute-start | bytes 294920 | tf_op jit(solution)/shard_map/ppermute | solution.py:410
  19.5 0.2 collective-permute-start.2
  19.8 1.0 collective-permute-start.1
  20.8 0.1 fusion.8.colid_ref
  20.9 0.0 collective-permute-done.7.d4
  20.9 0.0 copy-start.8
  20.9 1.8 %collective-permute-start.8 = (bf16[192,128]{1,0:T(8,128)(2,1)S(1)}, bf16[192,128]{1,0:T(8,128)(2,1)S(1)}, u32[]{:S(2)}, u32[]{:S(2)}) collective-permute-start(bf16[192,128]{1,0:T(8,128)(2,1)S(1)} %collective-permute-done.7.d4), channel_id=1, source_target_pairs={{0,2},{2,0},{1,3},{3,1},{4,6},{6,4},{5,7},{7,5},{8,10},{10,8},{9,1... | collective-permute-start | bytes 147464 | tf_op jit(solution)/shard_map/ppermute | solution.py:388
  22.7 3.1 %collective-permute-done.3.d3 = bf16[2,192,128]{2,1,0:T(8,128)(2,1)S(1)} collective-permute-done((bf16[2,192,128]{2,1,0:T(8,128)(2,1)S(1)}, bf16[2,192,128]{2,1,0:T(8,128)(2,1)S(1)}, u32[]{:S(2)}, u32[]{:S(2)}) %collective-permute-start.3) | collective-permute-done | bytes 98336 | tf_op jit(solution)/shard_map/ppermute | solution.py:410
  25.8 0.0 copy-start.2
  25.8 0.0 collective-permute-start.6
  25.8 2.0 %collective-permute-done.2.d2 = bf16[2,192,128]{2,1,0:T(8,128)(2,1)S(1)} collective-permute-done((bf16[2,192,128]{2,1,0:T(8,128)(2,1)S(1)}, bf16[2,192,128]{2,1,0:T(8,128)(2,1)S(1)}, u32[]{:S(2)}, u32[]{:S(2)}) %collective-permute-start.2) | collective-permute-done | bytes 98336 | tf_op jit(solution)/shard_map/ppermute | solution.py:410
  27.8 0.0 copy-start.3
  27.8 0.0 collective-permute-start.5
  27.8 1.8 %collective-permute-done.1.d1 = bf16[2,192,128]{2,1,0:T(8,128)(2,1)S(1)} collective-permute-done((bf16[2,192,128]{2,1,0:T(8,128)(2,1)S(1)}, bf16[2,192,128]{2,1,0:T(8,128)(2,1)S(1)}, u32[]{:S(2)}, u32[]{:S(2)}) %collective-permute-start.1) | collective-permute-done | bytes 98336 | tf_op jit(solution)/shard_map/ppermute | solution.py:410
  29.6 0.0 copy-start.4
  29.6 0.0 collective-permute-start.4
  29.6 0.1 pad_add_fusion.own_ref
  29.7 0.0 collective-permute-done.8.s4
  29.7 0.0 copy-start.9
  29.7 0.0 collective-permute-done.6.s3
  29.7 0.0 copy-start.5
  29.7 0.0 collective-permute-done.5.s2
  29.7 0.0 copy-start.6
  29.7 1.2 %collective-permute-done.4.s1 = bf16[2,192,128]{2,1,0:T(8,128)(2,1)S(1)} collective-permute-done((bf16[2,192,128]{2,1,0:T(8,128)(2,1)S(1)}, bf16[2,192,128]{2,1,0:T(8,128)(2,1)S(1)}, u32[]{:S(2)}, u32[]{:S(2)}) %collective-permute-start.4) | collective-permute-done | bytes 98336 | tf_op jit(solution)/shard_map/ppermute | solution.py:388
  30.9 0.0 copy-done.1
  30.9 0.0 copy-done.8
  30.9 0.0 copy-done.2
  30.9 0.0 copy-done.3
  30.9 0.0 copy-done.4
  30.9 0.0 copy-done.9
  31.0 0.0 copy-done.5
  31.0 0.0 copy-done.6
  31.0 0.0 copy-start.7
  31.0 0.6 copy-done.7
  31.6 2.1 %shard_map.42 = (bf16[3072,128]{1,0:T(8,128)(2,1)S(1)}, bf16[128,3072]{1,0:T(8,128)(2,1)S(1)}) custom-call(s32[4]{0:T(128)S(1)} %pad_add_fusion.own_ref, bf16[2,192,128]{2,1,0:T(8,128)(2,1)} %copy-done.1, bf16[2,192,128]{2,1,0:T(8,128)(2,1)} %copy-done.4, bf16[2,192,128]{2,1,0:T(8,128)(2,1)} %copy-done.3, bf16[2,192,128]{2,1,0:T(8,128)(2,1)} %copy-done.2, ...), custom_call_target="tpu_custom_call" | custom-call | flops 1000000000 | bytes 2097152 | tf_op jit(solution)/shard_map/pallas_call | solution.py:79
  33.7 0.0 all-to-all-done.rows_ref
  33.7 9.1 %shard_map.43 = (f32[16,384]{1,0:T(8,128)S(1)}, f32[16,384]{1,0:T(8,128)S(1)}, bf16[3072,128]{1,0:T(8,128)(2,1)}, f32[3072,128]{1,0:T(8,128)S(1)}) custom-call(s32[4]{0:T(128)S(1)} %pad_add_fusion.own_ref, bf16[16,208,128]{2,1,0:T(8,128)(2,1)S(1)} %all-to-all-done.rows_ref, bf16[128,3072]{1,0:T(8,128)(2,1)S(1)} %get-tuple-element.16.colsT, ...), custom_call_target="tpu_custom_call" | custom-call | tf_op jit(solution)/shard_map/pallas_call | solution.py:152
  42.9 0.2 collective-permute-start.9
  43.1 1.0 collective-permute-done.9.got_ref
  44.1 1.5 %shard_map.44 = f32[16,16,384]{2,1,0:T(8,128)} custom-call(s32[4]{0:T(128)S(1)} %pad_add_fusion.own_ref, f32[16,384]{1,0:T(8,128)S(1)} %get-tuple-element.20.keep_ref, f32[16,384]{1,0:T(8,128)S(1)} %collective-permute-done.9.got_ref), custom_call_target="tpu_custom_call" | custom-call | tf_op jit(solution)/shard_map/pallas_call | solution.py:195
  45.6 14.6 %all_to_all.15.part_ref = f32[16,16,384]{2,1,0:T(8,128)S(1)} all-to-all(f32[16,16,384]{2,1,0:T(8,128)} %shard_map.44), channel_id=1, replica_groups={{0,16,32,48,64,80,96,112,128,144,160,176,192,208,224,240},{4,20,36,52,6..., dimensions={0} | all-to-all | bytes 786432 | tf_op jit(solution)/shard_map/all_to_all | solution.py:431
  60.2 0.6 shard_map.45
  60.7 0.3 collective-permute-start.10
  61.1 1.2 %collective-permute-done.10.got_ref = f32[16,384]{1,0:T(8,128)S(1)} collective-permute-done((f32[16,384]{1,0:T(8,128)S(1)}, f32[16,384]{1,0:T(8,128)S(1)}, u32[]{:S(2)}, u32[]{:S(2)}) %collective-permute-start.10) | collective-permute-done | bytes 24608 | tf_op jit(solution)/shard_map/ppermute | solution.py:388
  62.2 13.3 %shard_map.46 = f32[16,200,128]{2,1,0:T(8,128)S(1)} custom-call(s32[4]{0:T(128)S(1)} %pad_add_fusion.own_ref, bf16[3072,128]{1,0:T(8,128)(2,1)} %get-tuple-element.17.rows_in, f32[3072,128]{1,0:T(8,128)S(1)} %get-tuple-element.18.mates, bf16[3072,128]{1,0:T(8,128)(2,1)S(1)} %get-tuple-element.19.cols_ref, bf16[128,3072]{1,0:T(8,128)(2,1)S(1)} %get-tuple-element.16.colsT, ...), custom_call_target="tpu_custom_call" | custom-call | tf_op jit(solution)/shard_map/pallas_call | solution.py:297
  75.5 0.0 copy-start
  75.5 28.5 %all_to_all.16.g_ref = f32[16,200,128]{2,1,0:T(8,128)S(1)} all-to-all(f32[16,200,128]{2,1,0:T(8,128)S(1)} %shard_map.46), channel_id=1, replica_groups=mesh['x'=4,'y'=4,'zl'=4,'c'=2,'zh'=2] {'x','y'}, dimensions={0} | all-to-all | bytes 3276800 | tf_op jit(solution)/shard_map/all_to_all | solution.py:435
  104.0 0.0 copy-done
  104.0 0.8 shard_map.47
  (1 shorter events, 0.0 us)
Async XLA Ops:
  2.7 31.0 %all-to-all-start = ((bf16[16,208,128]{2,1,0:T(8,128)(2,1)}), bf16[16,208,128]{2,1,0:T(8,128)(2,1)S(1)}, u32[]{:S(2)}, u32[]{:S(2)}) async-start(bf16[16,208,128]{2,1,0:T(8,128)(2,1)} %get-tuple-element.14), calls=%async_computation | async-start | bytes 1703936 | tf_op jit(solution)/shard_map/all_to_all | solution.py:419
  10.2 7.3 %collective-permute-start = (bf16[192,128]{1,0:T(8,128)(2,1)S(1)}, bf16[192,128]{1,0:T(8,128)(2,1)S(1)}, u32[]{:S(2)}, u32[]{:S(2)}) collective-permute-start(bf16[192,128]{1,0:T(8,128)(2,1)S(1)} %get-tuple-element.15), channel_id=1, source_target_pairs={{0,2},{2,0},{1,3},{3,1},{4,6},{6,4},{5,7},{7,5},{8,10},{10,8},{9,1... | collective-permute-start | bytes 147464 | tf_op jit(solution)/shard_map/ppermute | solution.py:388
  10.2 10.6 %collective-permute-start.7 = (bf16[192,128]{1,0:T(8,128)(2,1)S(1)}, bf16[192,128]{1,0:T(8,128)(2,1)S(1)}, u32[]{:S(2)}, u32[]{:S(2)}) collective-permute-start(bf16[192,128]{1,0:T(8,128)(2,1)S(1)} %get-tuple-element.15), channel_id=1, source_target_pairs={{0,1},{2,3},{4,5},{6,7},{8,9},{10,11},{12,13},{14,15},{1,0},{3,2},... | collective-permute-start | bytes 147464 | tf_op jit(solution)/shard_map/ppermute | solution.py:410
  17.5 13.4 %copy-start.1 = (bf16[2,192,128]{2,1,0:T(8,128)(2,1)}, bf16[2,192,128]{2,1,0:T(8,128)(2,1)S(1)}, u32[]{:S(2)}) copy-start(bf16[2,192,128]{2,1,0:T(8,128)(2,1)S(1)} %pad_maximum_fusion.pair_ref) | copy-start | bytes 294916
  17.5 8.2 %collective-permute-start.3 = (bf16[2,192,128]{2,1,0:T(8,128)(2,1)S(1)}, bf16[2,192,128]{2,1,0:T(8,128)(2,1)S(1)}, u32[]{:S(2)}, u32[]{:S(2)}) collective-permute-start(bf16[2,192,128]{2,1,0:T(8,128)(2,1)S(1)} %pad_maximum_fusion.pair_ref), channel_id=1, source_target_pairs={{0,12},{2,7},{4,1},{6,11},{8,5},{10,15},{12,9},{14,2},{1,13},{3,6}... | collective-permute-start | bytes 294920 | tf_op jit(solution)/shard_map/ppermute | solution.py:410
  19.5 8.3 %collective-permute-start.2 = (bf16[2,192,128]{2,1,0:T(8,128)(2,1)S(1)}, bf16[2,192,128]{2,1,0:T(8,128)(2,1)S(1)}, u32[]{:S(2)}, u32[]{:S(2)}) collective-permute-start(bf16[2,192,128]{2,1,0:T(8,128)(2,1)S(1)} %pad_maximum_fusion.pair_ref), channel_id=1, source_target_pairs={{0,8},{2,11},{4,12},{6,15},{8,1},{10,2},{12,5},{14,6},{1,9},{3,10}... | collective-permute-start | bytes 294920 | tf_op jit(solution)/shard_map/ppermute | solution.py:410
  19.8 9.9 %collective-permute-start.1 = (bf16[2,192,128]{2,1,0:T(8,128)(2,1)S(1)}, bf16[2,192,128]{2,1,0:T(8,128)(2,1)S(1)}, u32[]{:S(2)}, u32[]{:S(2)}) collective-permute-start(bf16[2,192,128]{2,1,0:T(8,128)(2,1)S(1)} %pad_maximum_fusion.pair_ref), channel_id=1, source_target_pairs={{0,4},{2,15},{4,8},{6,2},{8,12},{10,6},{12,1},{14,10},{1,5},{3,14}... | collective-permute-start | bytes 294920 | tf_op jit(solution)/shard_map/ppermute | solution.py:410
  20.9 10.0 %copy-start.8 = (bf16[192,128]{1,0:T(8,128)(2,1)}, bf16[192,128]{1,0:T(8,128)(2,1)S(1)}, u32[]{:S(2)}) copy-start(bf16[192,128]{1,0:T(8,128)(2,1)S(1)} %collective-permute-done.7.d4) | copy-start | bytes 147460
  20.9 8.8 %collective-permute-start.8 = (bf16[192,128]{1,0:T(8,128)(2,1)S(1)}, bf16[192,128]{1,0:T(8,128)(2,1)S(1)}, u32[]{:S(2)}, u32[]{:S(2)}) collective-permute-start(bf16[192,128]{1,0:T(8,128)(2,1)S(1)} %collective-permute-done.7.d4), channel_id=1, source_target_pairs={{0,2},{2,0},{1,3},{3,1},{4,6},{6,4},{5,7},{7,5},{8,10},{10,8},{9,1... | collective-permute-start | bytes 147464 | tf_op jit(solution)/shard_map/ppermute | solution.py:388
  25.8 5.1 %copy-start.2 = (bf16[2,192,128]{2,1,0:T(8,128)(2,1)}, bf16[2,192,128]{2,1,0:T(8,128)(2,1)S(1)}, u32[]{:S(2)}) copy-start(bf16[2,192,128]{2,1,0:T(8,128)(2,1)S(1)} %collective-permute-done.3.d3) | copy-start | bytes 294916
  25.8 3.9 %collective-permute-start.6 = (bf16[2,192,128]{2,1,0:T(8,128)(2,1)S(1)}, bf16[2,192,128]{2,1,0:T(8,128)(2,1)S(1)}, u32[]{:S(2)}, u32[]{:S(2)}) collective-permute-start(bf16[2,192,128]{2,1,0:T(8,128)(2,1)S(1)} %collective-permute-done.3.d3), channel_id=1, source_target_pairs={{0,2},{2,0},{1,3},{3,1},{4,6},{6,4},{5,7},{7,5},{8,10},{10,8},{9,1... | collective-permute-start | bytes 294920 | tf_op jit(solution)/shard_map/ppermute | solution.py:388
  27.8 3.1 %copy-start.3 = (bf16[2,192,128]{2,1,0:T(8,128)(2,1)}, bf16[2,192,128]{2,1,0:T(8,128)(2,1)S(1)}, u32[]{:S(2)}) copy-start(bf16[2,192,128]{2,1,0:T(8,128)(2,1)S(1)} %collective-permute-done.2.d2) | copy-start | bytes 294916
  27.8 1.9 %collective-permute-start.5 = (bf16[2,192,128]{2,1,0:T(8,128)(2,1)S(1)}, bf16[2,192,128]{2,1,0:T(8,128)(2,1)S(1)}, u32[]{:S(2)}, u32[]{:S(2)}) collective-permute-start(bf16[2,192,128]{2,1,0:T(8,128)(2,1)S(1)} %collective-permute-done.2.d2), channel_id=1, source_target_pairs={{0,2},{2,0},{1,3},{3,1},{4,6},{6,4},{5,7},{7,5},{8,10},{10,8},{9,1... | collective-permute-start | bytes 294920 | tf_op jit(solution)/shard_map/ppermute | solution.py:388
  29.6 1.3 %copy-start.4 = (bf16[2,192,128]{2,1,0:T(8,128)(2,1)}, bf16[2,192,128]{2,1,0:T(8,128)(2,1)S(1)}, u32[]{:S(2)}) copy-start(bf16[2,192,128]{2,1,0:T(8,128)(2,1)S(1)} %collective-permute-done.1.d1) | copy-start | bytes 294916
  29.6 1.3 %collective-permute-start.4 = (bf16[2,192,128]{2,1,0:T(8,128)(2,1)S(1)}, bf16[2,192,128]{2,1,0:T(8,128)(2,1)S(1)}, u32[]{:S(2)}, u32[]{:S(2)}) collective-permute-start(bf16[2,192,128]{2,1,0:T(8,128)(2,1)S(1)} %collective-permute-done.1.d1), channel_id=1, source_target_pairs={{0,2},{2,0},{1,3},{3,1},{4,6},{6,4},{5,7},{7,5},{8,10},{10,8},{9,1... | collective-permute-start | bytes 294920 | tf_op jit(solution)/shard_map/ppermute | solution.py:388
  29.7 1.3 %copy-start.9 = (bf16[192,128]{1,0:T(8,128)(2,1)}, bf16[192,128]{1,0:T(8,128)(2,1)S(1)}, u32[]{:S(2)}) copy-start(bf16[192,128]{1,0:T(8,128)(2,1)S(1)} %collective-permute-done.8.s4) | copy-start | bytes 147460
  29.7 1.3 %copy-start.5 = (bf16[2,192,128]{2,1,0:T(8,128)(2,1)}, bf16[2,192,128]{2,1,0:T(8,128)(2,1)S(1)}, u32[]{:S(2)}) copy-start(bf16[2,192,128]{2,1,0:T(8,128)(2,1)S(1)} %collective-permute-done.6.s3) | copy-start | bytes 294916
  29.7 1.2 %copy-start.6 = (bf16[2,192,128]{2,1,0:T(8,128)(2,1)}, bf16[2,192,128]{2,1,0:T(8,128)(2,1)S(1)}, u32[]{:S(2)}) copy-start(bf16[2,192,128]{2,1,0:T(8,128)(2,1)S(1)} %collective-permute-done.5.s2) | copy-start | bytes 294916
  31.0 0.6 copy-start.7
  42.9 1.3 %collective-permute-start.9 = (f32[16,384]{1,0:T(8,128)S(1)}, f32[16,384]{1,0:T(8,128)S(1)}, u32[]{:S(2)}, u32[]{:S(2)}) collective-permute-start(f32[16,384]{1,0:T(8,128)S(1)} %get-tuple-element.21), channel_id=1, source_target_pairs={{0,2},{2,0},{1,3},{3,1},{4,6},{6,4},{5,7},{7,5},{8,10},{10,8},{9,1... | collective-permute-start | bytes 73736 | tf_op jit(solution)/shard_map/ppermute | solution.py:388
  60.7 1.5 %collective-permute-start.10 = (f32[16,384]{1,0:T(8,128)S(1)}, f32[16,384]{1,0:T(8,128)S(1)}, u32[]{:S(2)}, u32[]{:S(2)}) collective-permute-start(f32[16,384]{1,0:T(8,128)S(1)} %get-tuple-element.23), channel_id=1, source_target_pairs={{0,2},{2,0},{1,3},{3,1},{4,6},{6,4},{5,7},{7,5},{8,10},{10,8},{9,1... | collective-permute-start | bytes 73736 | tf_op jit(solution)/shard_map/ppermute | solution.py:388
  75.5 28.5 %copy-start = (f32[192,128]{1,0:T(8,128)S(1)}, f32[192,128]{1,0:T(8,128)}, u32[]{:S(2)}) copy-start(f32[192,128]{1,0:T(8,128)} %p_ref.1) | copy-start | bytes 294916

commit v7 on v6

--- a/solution.py
+++ b/solution.py
@@ -56,13 +56,12 @@
     return rid == lanes
 
 
-def kcols_body(own_ref, pair_ref, d1, d2, d3, s1, s2, s3, d4, s4, cols_ref, colsT, sems):
-    core = own_ref[2]
-    places = [(pair_ref.at[0], core), (pair_ref.at[1], 1 - core), (d4, 8 + core), (s4, 9 - core)]
-    for off, ref in ((-1, d1), (-2, d2), (-3, d3), (1, s1), (2, s2), (3, s3)):
-        slot = jnp.where(core == 0, off & 7, (-off) & 7) * 2
-        first = core if off < 0 else 1 - core
-        places += [(ref.at[0], slot + first), (ref.at[1], slot + 1 - first)]
+def chip_at(k, z, core):
+    far = (k + 1) // 2
+    return (z + jnp.where(core == 0, 1, -1) * (-far if k % 2 else far)) & (NZ - 1)
+
+
+def place_columns(places, cols_ref, colsT, sems):
     copies = []
     for n, (piece, slot) in enumerate(places):
         to = cols_ref.at[pl.ds(pl.multiple_of(slot * SH, SH), SH), :]
@@ -71,133 +70,185 @@
         copy.start()
     for copy in copies:
         copy.wait()
-    for c in range(NCH):
+    for c in range(NCH // 2):
         colsT[:, c * CH : (c + 1) * CH] = jnp.transpose(cols_ref[c * CH : (c + 1) * CH, :])
 
 
-def kcols(own, pieces):
-    return pl.pallas_call(
-        kcols_body,
+def early_body(own_ref, pair_ref, d1, s1, d2, cols_ref, colsT, sems):
+    core = own_ref[2]
+    places = []
+    for slot, ref, first in ((0, pair_ref, core), (2, d1, core), (4, s1, 1 - core), (6, d2, core)):
+        places += [(ref.at[0], slot + first), (ref.at[1], slot + 1 - first)]
+    place_columns(places, cols_ref, colsT, sems)
+
+
+def late_body(own_ref, s2, d3, s3, d4, s4, after, cols_ref, colsT, sems):
+    core = own_ref[2]
+    places = [(d4, 6 + core), (s4, 7 - core)]
+    for slot, ref, first in ((0, s2, 1 - core), (2, d3, core), (4, s3, 1 - core)):
+        places += [(ref.at[0], slot + first), (ref.at[1], slot + 1 - first)]
+    place_columns(places, cols_ref, colsT, sems)
+
+
+def kcols(place, own, pieces, flops):
+    return pl.pallas_call(
+        place,
         out_shape=(
-            jax.ShapeDtypeStruct((C, 128), jnp.bfloat16),
-            jax.ShapeDtypeStruct((128, C), jnp.bfloat16),
+            jax.ShapeDtypeStruct((C // 2, 128), jnp.bfloat16),
+            jax.ShapeDtypeStruct((128, C // 2), jnp.bfloat16),
         ),
         in_specs=[pl.BlockSpec(memory_space=pltpu.SMEM)] + [pl.BlockSpec(memory_space=pltpu.HBM)] * len(pieces),
         out_specs=(pl.BlockSpec(memory_space=pltpu.VMEM),) * 2,
-        scratch_shapes=[pltpu.SemaphoreType.DMA((16,))],
+        scratch_shapes=[pltpu.SemaphoreType.DMA((8,))],
         compiler_params=pltpu.CompilerParams(vmem_limit_bytes=6 << 20),
-        cost_estimate=pl.CostEstimate(flops=10**9, transcendentals=0, bytes_accessed=1 << 21),
+        cost_estimate=pl.CostEstimate(flops=flops, transcendentals=0, bytes_accessed=1 << 20),
     )(own, *pieces)
 
 
-def k1_body(own_ref, rows_ref, colsT, colid_ref, keep_ref, give_ref, rows_out, mates, rows, racc, hval, cacc, tr, tc, sems):
+def score_tile(at, base, b, core, rows, mates, colsT, colid_ref, racc, hval, cacc):
+    u = rows[pl.ds(at, T1), :]
+    rid = None if b is None else diag_rows(b, T1)
+    for c in range(NW // 2):
+        s = jnp.dot(u, colsT[:, c * CW : (c + 1) * CW], preferred_element_type=jnp.float32)
+        sums = [None] * (CW // 128)
+        for r in range(0, T1, SUB):
+            m = mates[pl.ds(pl.multiple_of(at + r, SUB), SUB), :]
+            ra = None if c == 0 else racc[r : r + SUB, :]
+            hv = jnp.zeros((SUB, 128), jnp.float32) if c == 0 else hval[r : r + SUB, :]
+            for l in range(0, CW, 128):
+                p = c * CW + l
+                sl = s[r : r + SUB, l : l + 128]
+                el = jnp.exp2(sl * KS)
+                if rid is not None and p < 2 * SH:
+                    el = jnp.where(diag_of(rid[r : r + SUB], p, core), 0.0, el)
+                ra = el if ra is None else ra + el
+                hv = jnp.where(m == colid_ref[base + p // 256 : base + p // 256 + 1, p % 256 : p % 256 + 128], sl, hv)
+                cs = jnp.sum(el.reshape(SUB // 8, 8, 128), axis=0)
+                sums[l // 128] = cs if r == 0 else sums[l // 128] + cs
+            racc[r : r + SUB, :] = ra
+            hval[r : r + SUB, :] = hv
+        for l in range(0, CW, 128):
+            cacc[:, c * CW + l : c * CW + l + 128] += sums[l // 128]
+    parts = []
+    for q in range(0, PER1, 2):
+        part = [jnp.sum(jnp.transpose(racc[k * SH : (k + 1) * SH, :]), axis=0, keepdims=True) for k in (q, q + 1)]
+        parts.append(jnp.concatenate(part, axis=1))
+    return parts, jnp.sum(hval[...].reshape(T1 // 8, 8, 128), axis=0)
+
+
+def k1a_body(own_ref, rows_ref, colsT, colid_ref, tr, tc, pos_ref, rows_out, mates, rows, racc, hval, cacc, sem):
     b = own_ref[0]
     z = own_ref[1]
     core = own_ref[2]
     cacc[...] = jnp.zeros_like(cacc)
-
-    def tile(t, masked):
+    tc[...] = jnp.zeros_like(tc)
+
+    def tile(t, own_b):
         at = pl.multiple_of(t * T1, T1)
         for q in range(PER1):
             load_rows(rows_ref, rows, mates, t * PER1 + q)
-        u = rows[pl.ds(at, T1), :]
-        rid = diag_rows(b, T1) if masked else None
-        for c in range(NW):
-            s = jnp.dot(u, colsT[:, c * CW : (c + 1) * CW], preferred_element_type=jnp.float32)
-            sums = [None] * (CW // 128)
-            for r in range(0, T1, SUB):
-                m = mates[pl.ds(pl.multiple_of(at + r, SUB), SUB), :]
-                ra = None if c == 0 else racc[r : r + SUB, :]
-                hv = jnp.zeros((SUB, 128), jnp.float32) if c == 0 else hval[r : r + SUB, :]
-                for l in range(0, CW, 128):
-                    p = c * CW + l
-                    sl = s[r : r + SUB, l : l + 128]
-                    el = jnp.exp2(sl * KS)
-                    if masked and p < 2 * SH:
-                        el = jnp.where(diag_of(rid[r : r + SUB], p, core), 0.0, el)
-                    ra = el if ra is None else ra + el
-                    hv = jnp.where(m == colid_ref[p // 256 : p // 256 + 1, p % 256 : p % 256 + 128], sl, hv)
-                    cs = jnp.sum(el.reshape(SUB // 8, 8, 128), axis=0)
-                    sums[l // 128] = cs if r == 0 else sums[l // 128] + cs
-                racc[r : r + SUB, :] = ra
-                hval[r : r + SUB, :] = hv
-            for l in range(0, CW, 128):
-                cacc[:, c * CW + l : c * CW + l + 128] += sums[l // 128]
-        for q in range(0, PER1, 2):
-            part = [jnp.sum(jnp.transpose(racc[k * SH : (k + 1) * SH, :]), axis=0, keepdims=True) for k in (q, q + 1)]
-            tr[pl.ds(t * (PER1 // 2) + q // 2, 1), :] = jnp.concatenate(part, axis=1)
-        return jnp.sum(hval[...].reshape(T1 // 8, 8, 128), axis=0)
+        parts, pos = score_tile(at, 0, own_b, core, rows, mates, colsT, colid_ref, racc, hval, cacc)
+        for q, part in enumerate(parts):
+            tr[pl.ds(t * (PER1 // 2) + q, 1), :] = part
+        return pos
 
     own_tile = b // PER1
-    pos = tile(own_tile, True)
-
-    def step(k, pos):
-        return pos + tile((own_tile + k) & (N1 - 1), False)
-
-    pos = lax.fori_loop(1, N1, step, pos)
-    keep = pltpu.make_async_copy(rows, rows_out, sems)
+    pos = tile(own_tile, b)
+    pos_ref[...] = lax.fori_loop(1, N1, lambda k, v: v + tile((own_tile + k) & (N1 - 1), None), pos)
+    keep = pltpu.make_async_copy(rows, rows_out, sem)
     keep.start()
     total = jnp.sum(cacc[...], axis=0, keepdims=True)
-    for k in range(NZ):
-        tc[pl.ds((z + k) & 7, 1), :] = total[:, k * 2 * SH : (k + 1) * 2 * SH]
-    none = jnp.zeros((8, 256), jnp.float32)
-    by_rows = jnp.concatenate([tr[...], jnp.zeros((8, 2 * SH), jnp.float32)], axis=0)
-    by_cols = jnp.concatenate([tc[...], jnp.concatenate([pos, none], axis=1)], axis=0)
-    keep_ref[...] = jnp.where(core == 0, by_rows, by_cols)
-    give_ref[...] = jnp.where(core == 0, by_cols, by_rows)
+    for k in range(NZ // 2):
+        tc[pl.ds(chip_at(k, z, core), 1), :] = total[:, k * 2 * SH : (k + 1) * 2 * SH]
     keep.wait()
 
 
-def k1(own, rows, colsT, colid):
-    return pl.pallas_call(
-        k1_body,
+def k1a(own, rows, colsT, colid):
+    vmem = pl.BlockSpec(memory_space=pltpu.VMEM)
+    return pl.pallas_call(
+        k1a_body,
         out_shape=(
-            jax.ShapeDtypeStruct((16, 2 * SH), jnp.float32),
-            jax.ShapeDtypeStruct((16, 2 * SH), jnp.float32),
+            jax.ShapeDtypeStruct((8, 2 * SH), jnp.float32),
+            jax.ShapeDtypeStruct((8, 2 * SH), jnp.float32),
+            jax.ShapeDtypeStruct((8, 128), jnp.float32),
             pltpu.HBM((R, 128), jnp.bfloat16),
             jax.ShapeDtypeStruct((R, 128), jnp.float32),
         ),
-        in_specs=[pl.BlockSpec(memory_space=pltpu.SMEM)] + [pl.BlockSpec(memory_space=pltpu.VMEM)] * 3,
-        out_specs=(
-            pl.BlockSpec(memory_space=pltpu.VMEM),
-            pl.BlockSpec(memory_space=pltpu.VMEM),
-            pl.BlockSpec(memory_space=pltpu.HBM),
-            pl.BlockSpec(memory_space=pltpu.VMEM),
-        ),
+        in_specs=[pl.BlockSpec(memory_space=pltpu.SMEM)] + [vmem] * 3,
+        out_specs=(vmem, vmem, vmem, pl.BlockSpec(memory_space=pltpu.HBM), vmem),
         scratch_shapes=[
             pltpu.VMEM((R, 128), jnp.bfloat16),
             pltpu.VMEM((T1, 128), jnp.float32),
             pltpu.VMEM((T1, 128), jnp.float32),
-            pltpu.VMEM((8, C), jnp.float32),
+            pltpu.VMEM((8, C // 2), jnp.float32),
+            pltpu.SemaphoreType.DMA,
+        ],
+        compiler_params=pltpu.CompilerParams(vmem_limit_bytes=14 << 20),
+    )(own, rows, colsT, colid)
+
+
+def k1b_body(own_ref, rows_ref, mates, colsT, colid_ref, tra, tca, posa, keep_ref, give_ref, rows, racc, hval, cacc, tr, tc):
+    z = own_ref[1]
+    core = own_ref[2]
+    cacc[...] = jnp.zeros_like(cacc)
+    tc[...] = tca[...]
+
+    def tile(t, pos):
+        at = pl.multiple_of(t * T1, T1)
+        for q in range(PER1):
+            rows[pl.ds(pl.multiple_of(at + q * SH, SH), SH), :] = rows_ref[t * PER1 + q, 0:SH, :]
+        parts, more = score_tile(at, NCH // 2, None, core, rows, mates, colsT, colid_ref, racc, hval, cacc)
+        for q, part in enumerate(parts):
+            tr[pl.ds(t * (PER1 // 2) + q, 1), :] = part
+        return pos + more
+
+    pos = lax.fori_loop(0, N1, tile, posa[...])
+    total = jnp.sum(cacc[...], axis=0, keepdims=True)
+    for k in range(NZ // 2):
+        tc[pl.ds(chip_at(k + NZ // 2, z, core), 1), :] = total[:, k * 2 * SH : (k + 1) * 2 * SH]
+    none = jnp.zeros((8, 256), jnp.float32)
+    by_rows = jnp.concatenate([tra[...] + tr[...], jnp.zeros((8, 2 * SH), jnp.float32)], axis=0)
+    by_cols = jnp.concatenate([tc[...], jnp.concatenate([pos, none], axis=1)], axis=0)
+    keep_ref[...] = jnp.where(core == 0, by_rows, by_cols)
+    give_ref[...] = jnp.where(core == 0, by_cols, by_rows)
+
+
+def k1b(own, rows, mates, colsT, colid, sums):
+    vmem = pl.BlockSpec(memory_space=pltpu.VMEM)
+    return pl.pallas_call(
+        k1b_body,
+        out_shape=(jax.ShapeDtypeStruct((16, 2 * SH), jnp.float32),) * 2,
+        in_specs=[pl.BlockSpec(memory_space=pltpu.SMEM)] + [vmem] * 7,
+        out_specs=(vmem, vmem),
+        scratch_shapes=[
+            pltpu.VMEM((R, 128), jnp.bfloat16),
+            pltpu.VMEM((T1, 128), jnp.float32),
+            pltpu.VMEM((T1, 128), jnp.float32),
+            pltpu.VMEM((8, C // 2), jnp.float32),
             pltpu.VMEM((8, 2 * SH), jnp.float32),
             pltpu.VMEM((8, 2 * SH), jnp.float32),
-            pltpu.SemaphoreType.DMA,
         ],
-        compiler_params=pltpu.CompilerParams(vmem_limit_bytes=12 << 20),
-    )(own, rows, colsT, colid)
-
-
-def pack_body(own_ref, keep_ref, got_ref, pay_ref, both, sems):
+        compiler_params=pltpu.CompilerParams(vmem_limit_bytes=14 << 20),
+    )(own, rows, mates, colsT, colid, *sums)
+
+
+def pack_body(own_ref, keep_ref, got_ref, pay_ref):
     core = own_ref[2]
     mine = keep_ref[...]
     got = got_ref[...]
     low = jnp.where(core == 0, mine[0:8], mine[0:8] + got[0:8])
     high = jnp.where(core == 0, got[0:8], mine[8:16] + got[8:16])
-    both[...] = jnp.concatenate([low, high], axis=0)
-    copies = [pltpu.make_async_copy(both, pay_ref.at[d], sems.at[d]) for d in range(NB)]
-    for copy in copies:
-        copy.start()
-    for copy in copies:
-        copy.wait()
+    both = jnp.concatenate([low, high], axis=0)
+    for d in range(NB):
+        pay_ref[d] = both
 
 
 def pack(own, keep, got):
     return pl.pallas_call(
         pack_body,
-        out_shape=pltpu.HBM((NB, 16, 2 * SH), jnp.float32),
+        out_shape=jax.ShapeDtypeStruct((NB, 16, 2 * SH), jnp.float32),
         in_specs=[pl.BlockSpec(memory_space=pltpu.SMEM)] + [pl.BlockSpec(memory_space=pltpu.VMEM)] * 2,
-        out_specs=pl.BlockSpec(memory_space=pltpu.HBM),
-        scratch_shapes=[pltpu.VMEM((16, 2 * SH), jnp.float32), pltpu.SemaphoreType.DMA((NB,))],
+        out_specs=pl.BlockSpec(memory_space=pltpu.VMEM),
         compiler_params=pltpu.CompilerParams(vmem_limit_bytes=6 << 20),
     )(own, keep, got)
 
@@ -230,7 +281,7 @@
     )(own, part)
 
 
-def k2_body(own_ref, rows_in, mates, cols_ref, colsT, colid_ref, keep_ref, got_ref, g_ref, rows, ris, rrow, rcol, sem):
+def k2_body(own_ref, rows_in, mates, colsa, colsb, colsTa, colsTb, colid_ref, keep_ref, got_ref, g_ref, rows, ris, rrow, rcol, sem):
     fetch = pltpu.make_async_copy(rows_in, rows, sem)
     fetch.start()
     b = own_ref[0]
@@ -250,7 +301,7 @@
         g_ref[d, SH : SH + 8, :] = loss
     rcol[8:16, :] = (1.0 / TAU) / tall
     for k in range(NZ):
-        rcol[k : k + 1, :] = rcol[pl.ds(8 + ((z + k) & 7), 1), :]
+        rcol[k : k + 1, :] = rcol[pl.ds(8 + chip_at(k, z, core), 1), :]
 
     def tile(t, masked):
         at = pl.multiple_of(t * T2, T2)
@@ -261,7 +312,10 @@
         rid = diag_rows(b, T2) if masked else None
         acc = jnp.zeros((T2, 128), jnp.float32)
         for c in range(NW):
-            s = jnp.dot(u, colsT[:, c * CW : (c + 1) * CW], preferred_element_type=jnp.float32)
+            h = c % (NW // 2)
+            colsT = colsTa if c < NW // 2 else colsTb
+            cols = colsa if c < NW // 2 else colsb
+            s = jnp.dot(u, colsT[:, h * CW : (h + 1) * CW], preferred_element_type=jnp.float32)
             blocks = []
             for r in range(0, T2, SUB):
                 here = pl.ds(pl.multiple_of(at + r, SUB), SUB)
@@ -278,7 +332,7 @@
                     ws.append(w.astype(jnp.bfloat16))
                 blocks.append(jnp.concatenate(ws, axis=1))
             w = jnp.concatenate(blocks, axis=0)
-            acc = acc + jnp.dot(w, cols_ref[c * CW : (c + 1) * CW, :], preferred_element_type=jnp.float32)
+            acc = acc + jnp.dot(w, cols[h * CW : (h + 1) * CW, :], preferred_element_type=jnp.float32)
         for q in range(PER2):
             g_ref[t * PER2 + q, 0:SH, :] = acc[q * SH : (q + 1) * SH]
 
@@ -293,12 +347,12 @@
     lax.fori_loop(1, N2, step, 0)
 
 
-def k2(own, rows, mates, cols, colsT, colid, keep, got):
+def k2(own, rows, mates, cols, colid, keep, got):
     return pl.pallas_call(
         k2_body,
         out_shape=jax.ShapeDtypeStruct((NB, SH + 8, 128), jnp.float32),
         in_specs=[pl.BlockSpec(memory_space=pltpu.SMEM), pl.BlockSpec(memory_space=pltpu.HBM)]
-        + [pl.BlockSpec(memory_space=pltpu.VMEM)] * 6,
+        + [pl.BlockSpec(memory_space=pltpu.VMEM)] * 8,
         out_specs=pl.BlockSpec(memory_space=pltpu.VMEM),
         scratch_shapes=[
             pltpu.VMEM((R, 128), jnp.bfloat16),
@@ -308,7 +362,7 @@
             pltpu.SemaphoreType.DMA,
         ],
         compiler_params=pltpu.CompilerParams(vmem_limit_bytes=12 << 20),
-    )(own, rows, mates, cols, colsT, colid, keep, got)
+    )(own, rows, mates, *cols, colid, keep, got)
 
 
 def inverse_norm(p):
@@ -419,19 +473,26 @@
     rows = lax.all_to_all(pay, XY, 0, 0)
     pair = jnp.stack([low, swap(low)])
     direct = [along_z(pair, k) for k in (1, 2, 3)] + [along_z(low, 4)]
-    crossed = [swap(piece) for piece in direct]
-    pieces = [pair, *direct[:3], *crossed[:3], direct[3], crossed[3]]
+    crossed = [swap(piece) for piece in direct[:2]]
+    d1, d2 = [pltpu.with_memory_space_constraint(piece, pltpu.HBM) for piece in direct[:2]]
+    s1, s2 = [pltpu.with_memory_space_constraint(piece, pltpu.HBM) for piece in crossed]
     p = jnp.arange(16 * CH, dtype=jnp.int32)
-    zp = (z + p // (2 * SH)) % NZ
+    k = p // (2 * SH)
+    far = jnp.where(k % 2 == 1, -((k + 1) // 2), k // 2)
+    zp = (z + jnp.where(core == 0, far, -far)) & (NZ - 1)
     shard = (zp % 4) * 4 + (p // SH % 2) * 2 + zp // 4
     colid = ((xy * NA + shard) * SH + p % SH).astype(jnp.float32).reshape(16, CH)
-    pieces = [pltpu.with_memory_space_constraint(piece, pltpu.HBM) for piece in pieces]
-    cols, colsT = kcols(own, pieces)
-    keep, give, rows, mates = k1(own, rows, colsT, colid)
+    colsa, colsTa = kcols(early_body, own, [pltpu.with_memory_space_constraint(pair, pltpu.HBM), d1, s1, d2], 10**9)
+    *sums, kept, mates = k1a(own, rows, colsTa, colid)
+    d3, d4, after = lax.optimization_barrier((direct[2], direct[3], sums[2]))
+    late = [pltpu.with_memory_space_constraint(piece, pltpu.HBM) for piece in (d3, swap(d3), d4, swap(d4))]
+    colsb, colsTb = kcols(late_body, own, [s2, *late, after], 10**9)
+    keep, give = k1b(own, rows, mates, colsTb, colid, sums)
+    rows = kept
     part = lax.all_to_all(pack(own, keep, swap(give)), AXES, 0, 0, axis_index_groups=total_groups())
     keep, give = mid(own, part)
     rows = pltpu.with_memory_space_constraint(rows, pltpu.HBM)
-    g = k2(own, rows, mates, cols, colsT, colid, keep, swap(give))
+    g = k2(own, rows, mates, (colsa, colsb, colsTa, colsTb), colid, keep, swap(give))
     g = lax.all_to_all(g, XY, 0, 0)
     loss, grad = final(projections, g)
     return (loss[0, 0], grad)

time: 106 us -> 111 us (1.047)
  Pallas kernels: 29.4 us -> 32 us
  local copies, waits for them, and re-layouts: 0.66 us -> 2.49 us
  waiting for transfers between devices: 10.3 us -> 11.6 us
    pallas_call x3 -> x5, Pallas kernels: 12.7 us -> 15.2 us  [the longest x1 6.09 us: k1a(): pl.pallas_call(k1a_body, out_shape=(jax.ShapeDtypeStruct((8, 2 * SH), jnp...]
    unnamed x20, local copies, waits for them, and re-layouts: 0.66 us -> 2.49 us
    ppermute x4, waiting for transfers between devices: 6.88 us -> 8.42 us  [along_z(): return lax.ppermute(value, ZC, pairs)]
    ppermute x7, starting transfers between devices: 2.4 us -> 1.24 us  [swap(): return lax.ppermute(value, 'c', [(0, 1), (1, 0)])]
  transfers between devices with their start and end apart: 12 -> 12, of which waited for: 6 -> 5; matrix products, arithmetic and copies ran while one was open for 0% -> 0% of each run, Pallas kernels for 2% -> 7%
where the time goes in v7:
time: 111 us; the launch traced here: 109 us
  blocking collectives  42.9 us (39%)
  Pallas kernels  32 us (29%)
  starting transfers between devices  19.3 us (17%)
  waiting for transfers between devices  11.6 us (10%)
  local copies, waits for them, and re-layouts  2.49 us (2%)
    all_to_all x1, blocking collectives, body(): g = lax.all_to_all(g, XY, 0, 0)  28.5 us
    all_to_all x1, blocking collectives, body(): lax.all_to_all(pack(own, keep, swap(give)), AXES, 0, 0, axis_index_groups...  14.4 us
    pallas_call x1, Pallas kernels, k2(): pl.pallas_call(k2_body, out_shape=jax.ShapeDtypeStruct((NB, SH + 8, 128),...  13.3 us
    ppermute x4, starting transfers between devices, along_z(): return lax.ppermute(value, ZC, pairs)  10.6 us
    ppermute x4, waiting for transfers between devices, along_z(): return lax.ppermute(value, ZC, pairs)  8.42 us
    all_to_all x1, starting transfers between devices, body(): rows = lax.all_to_all(pay, XY, 0, 0)  7.49 us
    pallas_call x1, Pallas kernels, k1a(): pl.pallas_call(k1a_body, out_shape=(jax.ShapeDtypeStruct((8, 2 * SH), jnp...  6.09 us
    pallas_call x1, Pallas kernels, k1b(): pl.pallas_call(k1b_body, out_shape=(jax.ShapeDtypeStruct((16, 2 * SH), jn...  5.08 us
  transfers between devices with their start and end apart: 12, of which 5 were waited for; matrix products, arithmetic and copies ran while one was open for 0% of the time, Pallas kernels for 7%

profile of v7, /device:TPU:2, one launch (start us, length us, event | category | flops | bytes accessed | tf_op | source)
XLA Modules:
  0.0 109.4 jit_solution(4330131406590231536)
XLA Ops:
  0.6 2.1 %shard_map.41 = (bf16[16,208,128]{2,1,0:T(8,128)(2,1)}, bf16[192,128]{1,0:T(8,128)(2,1)S(1)}) custom-call(f32[192,128]{1,0:T(8,128)} %p_ref.1, s32[192]{0:T(256)} %mate_hbm.1), custom_call_target="tpu_custom_call" | custom-call | tf_op jit(solution)/shard_map/pallas_call | solution.py:397
  2.7 7.5 %all-to-all-start = ((bf16[16,208,128]{2,1,0:T(8,128)(2,1)}), bf16[16,208,128]{2,1,0:T(8,128)(2,1)S(1)}, u32[]{:S(2)}, u32[]{:S(2)}) async-start(bf16[16,208,128]{2,1,0:T(8,128)(2,1)} %get-tuple-element.22), calls=%async_computation | async-start | bytes 1703936 | tf_op jit(solution)/shard_map/all_to_all | solution.py:473
  10.2 0.0 collective-permute-start
  10.2 7.3 %collective-permute-start.6 = (bf16[192,128]{1,0:T(8,128)(2,1)S(1)}, bf16[192,128]{1,0:T(8,128)(2,1)S(1)}, u32[]{:S(2)}, u32[]{:S(2)}) collective-permute-start(bf16[192,128]{1,0:T(8,128)(2,1)S(1)} %get-tuple-element.23), channel_id=1, source_target_pairs={{0,1},{2,3},{4,5},{6,7},{8,9},{10,11},{12,13},{14,15},{1,0},{3,2},... | collective-permute-start | bytes 147464 | tf_op jit(solution)/shard_map/ppermute | solution.py:464
  17.5 0.0 collective-permute-done
  17.5 0.0 copy-start.1
  17.5 1.1 %collective-permute-start.1 = (bf16[2,192,128]{2,1,0:T(8,128)(2,1)S(1)}, bf16[2,192,128]{2,1,0:T(8,128)(2,1)S(1)}, u32[]{:S(2)}, u32[]{:S(2)}) collective-permute-start(bf16[2,192,128]{2,1,0:T(8,128)(2,1)S(1)} %pad_maximum_fusion.pair_ref), channel_id=1, source_target_pairs={{0,4},{2,15},{4,8},{6,2},{8,12},{10,6},{12,1},{14,10},{1,5},{3,14}... | collective-permute-start | bytes 294920 | tf_op jit(solution)/shard_map/ppermute | solution.py:464
  18.6 0.1 fusion.12.colid_ref
  18.7 1.0 collective-permute-start.5
  19.7 1.2 %collective-permute-start.3 = (bf16[2,192,128]{2,1,0:T(8,128)(2,1)S(1)}, bf16[2,192,128]{2,1,0:T(8,128)(2,1)S(1)}, u32[]{:S(2)}, u32[]{:S(2)}) collective-permute-start(bf16[2,192,128]{2,1,0:T(8,128)(2,1)S(1)} %pad_maximum_fusion.pair_ref), channel_id=1, source_target_pairs={{0,8},{2,11},{4,12},{6,15},{8,1},{10,2},{12,5},{14,6},{1,9},{3,10}... | collective-permute-start | bytes 294920 | tf_op jit(solution)/shard_map/ppermute | solution.py:464
  21.0 2.5 %collective-permute-done.1.d1 = bf16[2,192,128]{2,1,0:T(8,128)(2,1)S(1)} collective-permute-done((bf16[2,192,128]{2,1,0:T(8,128)(2,1)S(1)}, bf16[2,192,128]{2,1,0:T(8,128)(2,1)S(1)}, u32[]{:S(2)}, u32[]{:S(2)}) %collective-permute-start.1) | collective-permute-done | bytes 98336 | tf_op jit(solution)/shard_map/ppermute | solution.py:464
  23.4 0.0 copy-start.5
  23.4 0.2 collective-permute-start.2
  23.7 0.1 pad_add_fusion.own_ref
  23.8 5.9 %collective-permute-done.3.d2 = bf16[2,192,128]{2,1,0:T(8,128)(2,1)S(1)} collective-permute-done((bf16[2,192,128]{2,1,0:T(8,128)(2,1)S(1)}, bf16[2,192,128]{2,1,0:T(8,128)(2,1)S(1)}, u32[]{:S(2)}, u32[]{:S(2)}) %collective-permute-start.3) | collective-permute-done | bytes 98336 | tf_op jit(solution)/shard_map/ppermute | solution.py:464
  29.7 0.0 copy-start.3
  29.7 0.0 collective-permute-start.4
  29.7 0.0 collective-permute-done.2.s1
  29.7 0.0 copy-done.1
  29.7 0.0 copy-done.5
  29.7 0.6 copy-done.3
  30.3 0.0 copy-start.7
  30.3 0.6 copy-done.7
  31.0 1.7 %shard_map.42 = (bf16[1536,128]{1,0:T(8,128)(2,1)S(1)}, bf16[128,1536]{1,0:T(8,128)(2,1)S(1)}) custom-call(s32[4]{0:T(128)S(1)} %pad_add_fusion.own_ref, bf16[2,192,128]{2,1,0:T(8,128)(2,1)} %copy-done.1, bf16[2,192,128]{2,1,0:T(8,128)(2,1)} %copy-done.5, bf16[2,192,128]{2,1,0:T(8,128)(2,1)} %copy-done.7, bf16[2,192,128]{2,1,0:T(8,128)(2,1)} %copy-done.3), custom_call_target="tpu_custom_call" | custom-call | flops 1000000000 | bytes 1048576 | tf_op jit(solution)/shard_map/pallas_call | solution.py:94
  32.7 0.0 all-to-all-done.rows_ref
  32.7 6.1 %shard_map.43 = (f32[8,384]{1,0:T(8,128)S(1)}, f32[8,384]{1,0:T(8,128)S(1)}, f32[8,128]{1,0:T(8,128)S(1)}, bf16[3072,128]{1,0:T(8,128)(2,1)}, f32[3072,128]{1,0:T(8,128)S(1)}) custom-call(s32[4]{0:T(128)S(1)} %pad_add_fusion.own_ref, bf16[16,208,128]{2,1,0:T(8,128)(2,1)S(1)} %all-to-all-done.rows_ref, bf16[128,1536]{1,0:T(8,128)(2,1)S(1)} %get-tuple-element.24.colsT.colsTa, ...), custom_call_target="tpu_custom_call" | custom-call | tf_op jit(solution)/shard_map/pallas_call | solution.py:168
  38.8 0.0 collective-permute-done.6.d4
  38.8 0.0 copy-start.8
  38.8 0.0 collective-permute-done.5.d3
  38.8 0.0 copy-start.2
  38.9 0.1 collective-permute-start.7
  39.0 0.5 collective-permute-start.8
  39.5 0.0 collective-permute-done.4.s2
  39.5 0.0 copy-start.4
  39.5 1.0 collective-permute-done.8.s4
  40.5 0.0 copy-start.9
  40.5 0.0 collective-permute-done.7.s3
  40.5 0.0 copy-done.8
  40.5 0.0 copy-done.2
  40.5 0.0 copy-done.4
  40.5 0.6 copy-done.9
  41.1 0.0 copy-start.6
  41.1 0.6 copy-done.6
  41.7 1.7 %shard_map.44 = (bf16[1536,128]{1,0:T(8,128)(2,1)S(1)}, bf16[128,1536]{1,0:T(8,128)(2,1)S(1)}) custom-call(s32[4]{0:T(128)S(1)} %pad_add_fusion.own_ref, bf16[2,192,128]{2,1,0:T(8,128)(2,1)} %copy-done.4, bf16[2,192,128]{2,1,0:T(8,128)(2,1)} %copy-done.2, bf16[2,192,128]{2,1,0:T(8,128)(2,1)} %copy-done.6, bf16[192,128]{1,0:T(8,128)(2,1)} %copy-done.8, ...), custom_call_target="tpu_custom_call" | custom-call | flops 1000000000 | bytes 1048576 | tf_op jit(solution)/shard_map/pallas_call | solution.py:94
  43.4 5.1 %shard_map.45 = (f32[16,384]{1,0:T(8,128)S(1)}, f32[16,384]{1,0:T(8,128)S(1)}) custom-call(s32[4]{0:T(128)S(1)} %pad_add_fusion.own_ref, bf16[16,208,128]{2,1,0:T(8,128)(2,1)S(1)} %all-to-all-done.rows_ref, f32[3072,128]{1,0:T(8,128)S(1)} %get-tuple-element.26.mates, bf16[128,1536]{1,0:T(8,128)(2,1)S(1)} %get-tuple-element.33.colsT.colsTb, ...), custom_call_target="tpu_custom_call" | custom-call | tf_op jit(solution)/shard_map/pallas_call | solution.py:218
  48.5 0.3 collective-permute-start.9
  48.8 1.0 collective-permute-done.9.got_ref
  49.8 0.6 shard_map.46
  50.4 14.4 %all_to_all.15.part_ref = f32[16,16,384]{2,1,0:T(8,128)S(1)} all-to-all(f32[16,16,384]{2,1,0:T(8,128)S(1)} %shard_map.46), channel_id=1, replica_groups={{0,16,32,48,64,80,96,112,128,144,160,176,192,208,224,240},{4,20,36,52,6..., dimensions={0} | all-to-all | bytes 786432 | tf_op jit(solution)/shard_map/all_to_all | solution.py:492
  64.8 0.6 shard_map.47
  65.3 0.1 collective-permute-start.10
  65.4 1.2 %collective-permute-done.10.got_ref = f32[16,384]{1,0:T(8,128)S(1)} collective-permute-done((f32[16,384]{1,0:T(8,128)S(1)}, f32[16,384]{1,0:T(8,128)S(1)}, u32[]{:S(2)}, u32[]{:S(2)}) %collective-permute-start.10) | collective-permute-done | bytes 24608 | tf_op jit(solution)/shard_map/ppermute | solution.py:442
  66.6 13.3 %shard_map.48 = f32[16,200,128]{2,1,0:T(8,128)S(1)} custom-call(s32[4]{0:T(128)S(1)} %pad_add_fusion.own_ref, bf16[3072,128]{1,0:T(8,128)(2,1)} %get-tuple-element.25.rows_in, f32[3072,128]{1,0:T(8,128)S(1)} %get-tuple-element.26.mates, bf16[1536,128]{1,0:T(8,128)(2,1)S(1)} %get-tuple-element.27.colsa, bf16[1536,128]{1,0:T(8,128)(2,1)S(1)} %get-tuple-element.32.colsb, ...), custom_call_target="tpu_custom_call" | custom-call | tf_op jit(solution)/shard_map/pallas_call | solution.py:351
  79.9 0.0 copy-start
  79.9 28.5 %all_to_all.16.g_ref = f32[16,200,128]{2,1,0:T(8,128)S(1)} all-to-all(f32[16,200,128]{2,1,0:T(8,128)S(1)} %shard_map.48), channel_id=1, replica_groups=mesh['x'=4,'y'=4,'zl'=4,'c'=2,'zh'=2] {'x','y'}, dimensions={0} | all-to-all | bytes 3276800 | tf_op jit(solution)/shard_map/all_to_all | solution.py:496
  108.4 0.0 copy-done
  108.4 0.8 shard_map.49
  (1 shorter events, 0.0 us)
Async XLA Ops:
  2.7 30.0 %all-to-all-start = ((bf16[16,208,128]{2,1,0:T(8,128)(2,1)}), bf16[16,208,128]{2,1,0:T(8,128)(2,1)S(1)}, u32[]{:S(2)}, u32[]{:S(2)}) async-start(bf16[16,208,128]{2,1,0:T(8,128)(2,1)} %get-tuple-element.22), calls=%async_computation | async-start | bytes 1703936 | tf_op jit(solution)/shard_map/all_to_all | solution.py:473
  10.2 7.3 %collective-permute-start = (bf16[192,128]{1,0:T(8,128)(2,1)S(1)}, bf16[192,128]{1,0:T(8,128)(2,1)S(1)}, u32[]{:S(2)}, u32[]{:S(2)}) collective-permute-start(bf16[192,128]{1,0:T(8,128)(2,1)S(1)} %get-tuple-element.23), channel_id=1, source_target_pairs={{0,2},{2,0},{1,3},{3,1},{4,6},{6,4},{5,7},{7,5},{8,10},{10,8},{9,1... | collective-permute-start | bytes 147464 | tf_op jit(solution)/shard_map/ppermute | solution.py:442
  10.2 28.6 %collective-permute-start.6 = (bf16[192,128]{1,0:T(8,128)(2,1)S(1)}, bf16[192,128]{1,0:T(8,128)(2,1)S(1)}, u32[]{:S(2)}, u32[]{:S(2)}) collective-permute-start(bf16[192,128]{1,0:T(8,128)(2,1)S(1)} %get-tuple-element.23), channel_id=1, source_target_pairs={{0,1},{2,3},{4,5},{6,7},{8,9},{10,11},{12,13},{14,15},{1,0},{3,2},... | collective-permute-start | bytes 147464 | tf_op jit(solution)/shard_map/ppermute | solution.py:464
  17.5 12.2 %copy-start.1 = (bf16[2,192,128]{2,1,0:T(8,128)(2,1)}, bf16[2,192,128]{2,1,0:T(8,128)(2,1)S(1)}, u32[]{:S(2)}) copy-start(bf16[2,192,128]{2,1,0:T(8,128)(2,1)S(1)} %pad_maximum_fusion.pair_ref) | copy-start | bytes 294916
  17.5 5.9 %collective-permute-start.1 = (bf16[2,192,128]{2,1,0:T(8,128)(2,1)S(1)}, bf16[2,192,128]{2,1,0:T(8,128)(2,1)S(1)}, u32[]{:S(2)}, u32[]{:S(2)}) collective-permute-start(bf16[2,192,128]{2,1,0:T(8,128)(2,1)S(1)} %pad_maximum_fusion.pair_ref), channel_id=1, source_target_pairs={{0,4},{2,15},{4,8},{6,2},{8,12},{10,6},{12,1},{14,10},{1,5},{3,14}... | collective-permute-start | bytes 294920 | tf_op jit(solution)/shard_map/ppermute | solution.py:464
  18.7 20.1 %collective-permute-start.5 = (bf16[2,192,128]{2,1,0:T(8,128)(2,1)S(1)}, bf16[2,192,128]{2,1,0:T(8,128)(2,1)S(1)}, u32[]{:S(2)}, u32[]{:S(2)}) collective-permute-start(bf16[2,192,128]{2,1,0:T(8,128)(2,1)S(1)} %pad_maximum_fusion.pair_ref), channel_id=1, source_target_pairs={{0,12},{2,7},{4,1},{6,11},{8,5},{10,15},{12,9},{14,2},{1,13},{3,6}... | collective-permute-start | bytes 294920 | tf_op jit(solution)/shard_map/ppermute | solution.py:464
  19.7 10.0 %collective-permute-start.3 = (bf16[2,192,128]{2,1,0:T(8,128)(2,1)S(1)}, bf16[2,192,128]{2,1,0:T(8,128)(2,1)S(1)}, u32[]{:S(2)}, u32[]{:S(2)}) collective-permute-start(bf16[2,192,128]{2,1,0:T(8,128)(2,1)S(1)} %pad_maximum_fusion.pair_ref), channel_id=1, source_target_pairs={{0,8},{2,11},{4,12},{6,15},{8,1},{10,2},{12,5},{14,6},{1,9},{3,10}... | collective-permute-start | bytes 294920 | tf_op jit(solution)/shard_map/ppermute | solution.py:464
  23.4 6.3 %copy-start.5 = (bf16[2,192,128]{2,1,0:T(8,128)(2,1)}, bf16[2,192,128]{2,1,0:T(8,128)(2,1)S(1)}, u32[]{:S(2)}) copy-start(bf16[2,192,128]{2,1,0:T(8,128)(2,1)S(1)} %collective-permute-done.1.d1) | copy-start | bytes 294916
  23.4 6.3 %collective-permute-start.2 = (bf16[2,192,128]{2,1,0:T(8,128)(2,1)S(1)}, bf16[2,192,128]{2,1,0:T(8,128)(2,1)S(1)}, u32[]{:S(2)}, u32[]{:S(2)}) collective-permute-start(bf16[2,192,128]{2,1,0:T(8,128)(2,1)S(1)} %collective-permute-done.1.d1), channel_id=1, source_target_pairs={{0,2},{2,0},{1,3},{3,1},{4,6},{6,4},{5,7},{7,5},{8,10},{10,8},{9,1... | collective-permute-start | bytes 294920 | tf_op jit(solution)/shard_map/ppermute | solution.py:442
  29.7 0.6 copy-start.3
  29.7 9.8 %collective-permute-start.4 = (bf16[2,192,128]{2,1,0:T(8,128)(2,1)S(1)}, bf16[2,192,128]{2,1,0:T(8,128)(2,1)S(1)}, u32[]{:S(2)}, u32[]{:S(2)}) collective-permute-start(bf16[2,192,128]{2,1,0:T(8,128)(2,1)S(1)} %collective-permute-done.3.d2), channel_id=1, source_target_pairs={{0,2},{2,0},{1,3},{3,1},{4,6},{6,4},{5,7},{7,5},{8,10},{10,8},{9,1... | collective-permute-start | bytes 294920 | tf_op jit(solution)/shard_map/ppermute | solution.py:442
  30.3 0.6 copy-start.7
  38.8 1.6 %copy-start.8 = (bf16[192,128]{1,0:T(8,128)(2,1)}, bf16[192,128]{1,0:T(8,128)(2,1)S(1)}, u32[]{:S(2)}) copy-start(bf16[192,128]{1,0:T(8,128)(2,1)S(1)} %collective-permute-done.6.d4) | copy-start | bytes 147460
  38.8 1.6 %copy-start.2 = (bf16[2,192,128]{2,1,0:T(8,128)(2,1)}, bf16[2,192,128]{2,1,0:T(8,128)(2,1)S(1)}, u32[]{:S(2)}) copy-start(bf16[2,192,128]{2,1,0:T(8,128)(2,1)S(1)} %collective-permute-done.5.d3) | copy-start | bytes 294916
  38.9 1.6 %collective-permute-start.7 = (bf16[2,192,128]{2,1,0:T(8,128)(2,1)S(1)}, bf16[2,192,128]{2,1,0:T(8,128)(2,1)S(1)}, u32[]{:S(2)}, u32[]{:S(2)}) collective-permute-start(bf16[2,192,128]{2,1,0:T(8,128)(2,1)S(1)} %collective-permute-done.5.d3), channel_id=1, source_target_pairs={{0,2},{2,0},{1,3},{3,1},{4,6},{6,4},{5,7},{7,5},{8,10},{10,8},{9,1... | collective-permute-start | bytes 294920 | tf_op jit(solution)/shard_map/ppermute | solution.py:442
  39.0 1.5 %collective-permute-start.8 = (bf16[192,128]{1,0:T(8,128)(2,1)S(1)}, bf16[192,128]{1,0:T(8,128)(2,1)S(1)}, u32[]{:S(2)}, u32[]{:S(2)}) collective-permute-start(bf16[192,128]{1,0:T(8,128)(2,1)S(1)} %collective-permute-done.6.d4), channel_id=1, source_target_pairs={{0,2},{2,0},{1,3},{3,1},{4,6},{6,4},{5,7},{7,5},{8,10},{10,8},{9,1... | collective-permute-start | bytes 147464 | tf_op jit(solution)/shard_map/ppermute | solution.py:442
  39.5 1.0 copy-start.4
  40.5 0.6 copy-start.9
  41.1 0.6 copy-start.6
  48.5 1.3 %collective-permute-start.9 = (f32[16,384]{1,0:T(8,128)S(1)}, f32[16,384]{1,0:T(8,128)S(1)}, u32[]{:S(2)}, u32[]{:S(2)}) collective-permute-start(f32[16,384]{1,0:T(8,128)S(1)} %get-tuple-element.37), channel_id=1, source_target_pairs={{0,2},{2,0},{1,3},{3,1},{4,6},{6,4},{5,7},{7,5},{8,10},{10,8},{9,1... | collective-permute-start | bytes 73736 | tf_op jit(solution)/shard_map/ppermute | solution.py:442
  65.3 1.3 %collective-permute-start.10 = (f32[16,384]{1,0:T(8,128)S(1)}, f32[16,384]{1,0:T(8,128)S(1)}, u32[]{:S(2)}, u32[]{:S(2)}) collective-permute-start(f32[16,384]{1,0:T(8,128)S(1)} %get-tuple-element.39), channel_id=1, source_target_pairs={{0,2},{2,0},{1,3},{3,1},{4,6},{6,4},{5,7},{7,5},{8,10},{10,8},{9,1... | collective-permute-start | bytes 73736 | tf_op jit(solution)/shard_map/ppermute | solution.py:442
  79.9 28.5 %copy-start = (f32[192,128]{1,0:T(8,128)S(1)}, f32[192,128]{1,0:T(8,128)}, u32[]{:S(2)}) copy-start(f32[192,128]{1,0:T(8,128)} %p_ref.1) | copy-start | bytes 294916

commit v8 on v6

--- a/solution.py
+++ b/solution.py
@@ -86,7 +86,7 @@
         out_specs=(pl.BlockSpec(memory_space=pltpu.VMEM),) * 2,
         scratch_shapes=[pltpu.SemaphoreType.DMA((16,))],
         compiler_params=pltpu.CompilerParams(vmem_limit_bytes=6 << 20),
-        cost_estimate=pl.CostEstimate(flops=10**9, transcendentals=0, bytes_accessed=1 << 21),
+        cost_estimate=pl.CostEstimate(flops=10**10, transcendentals=0, bytes_accessed=1 << 21),
     )(own, *pieces)
 
 
@@ -177,27 +177,23 @@
     )(own, rows, colsT, colid)
 
 
-def pack_body(own_ref, keep_ref, got_ref, pay_ref, both, sems):
+def pack_body(own_ref, keep_ref, got_ref, pay_ref):
     core = own_ref[2]
     mine = keep_ref[...]
     got = got_ref[...]
     low = jnp.where(core == 0, mine[0:8], mine[0:8] + got[0:8])
     high = jnp.where(core == 0, got[0:8], mine[8:16] + got[8:16])
-    both[...] = jnp.concatenate([low, high], axis=0)
-    copies = [pltpu.make_async_copy(both, pay_ref.at[d], sems.at[d]) for d in range(NB)]
-    for copy in copies:
-        copy.start()
-    for copy in copies:
-        copy.wait()
+    both = jnp.concatenate([low, high], axis=0)
+    for d in range(NB):
+        pay_ref[d] = both
 
 
 def pack(own, keep, got):
     return pl.pallas_call(
         pack_body,
-        out_shape=pltpu.HBM((NB, 16, 2 * SH), jnp.float32),
+        out_shape=jax.ShapeDtypeStruct((NB, 16, 2 * SH), jnp.float32),
         in_specs=[pl.BlockSpec(memory_space=pltpu.SMEM)] + [pl.BlockSpec(memory_space=pltpu.VMEM)] * 2,
-        out_specs=pl.BlockSpec(memory_space=pltpu.HBM),
-        scratch_shapes=[pltpu.VMEM((16, 2 * SH), jnp.float32), pltpu.SemaphoreType.DMA((NB,))],
+        out_specs=pl.BlockSpec(memory_space=pltpu.VMEM),
         compiler_params=pltpu.CompilerParams(vmem_limit_bytes=6 << 20),
     )(own, keep, got)
 

time: 106 us -> 105 us (level)
  no operation moved by 1% of the time
where the time goes in v8:
time: 105 us; the launch traced here: 104 us
  blocking collectives  42.7 us (41%)
  Pallas kernels  28.6 us (27%)
  starting transfers between devices  19.9 us (19%)
  waiting for transfers between devices  10.9 us (10%)
    all_to_all x1, blocking collectives, body(): g = lax.all_to_all(g, XY, 0, 0)  28.4 us
    all_to_all x1, blocking collectives, body(): lax.all_to_all(pack(own, keep, swap(give)), AXES, 0, 0, axis_index_groups...  14.3 us
    pallas_call x1, Pallas kernels, k2(): pl.pallas_call(k2_body, out_shape=jax.ShapeDtypeStruct((NB, SH + 8, 128),...  13.3 us
    ppermute x4, starting transfers between devices, along_z(): return lax.ppermute(value, ZC, pairs)  9.93 us
    pallas_call x1, Pallas kernels, k1(): pl.pallas_call(k1_body, out_shape=(jax.ShapeDtypeStruct((16, 2 * SH), jnp...  9.16 us
    all_to_all x1, starting transfers between devices, body(): rows = lax.all_to_all(pay, XY, 0, 0)  7.48 us
    ppermute x4, waiting for transfers between devices, along_z(): return lax.ppermute(value, ZC, pairs)  7.44 us
    ppermute x7, waiting for transfers between devices, swap(): return lax.ppermute(value, 'c', [(0, 1), (1, 0)])  3.43 us
  transfers between devices with their start and end apart: 12, of which 6 were waited for; matrix products, arithmetic and copies ran while one was open for 0% of the time, Pallas kernels for 2%

profile of v8, /device:TPU:2, one launch (start us, length us, event | category | flops | bytes accessed | tf_op | source)
XLA Modules:
  0.0 103.9 jit_solution(2759004662100966415)
XLA Ops:
  0.6 2.1 %shard_map.41 = (bf16[16,208,128]{2,1,0:T(8,128)(2,1)}, bf16[192,128]{1,0:T(8,128)(2,1)S(1)}) custom-call(f32[192,128]{1,0:T(8,128)} %p_ref.1, s32[192]{0:T(256)} %mate_hbm.1), custom_call_target="tpu_custom_call" | custom-call | tf_op jit(solution)/shard_map/pallas_call | solution.py:339
  2.7 0.1 collective-permute-start
  2.8 7.3 %collective-permute-start.7 = (bf16[192,128]{1,0:T(8,128)(2,1)S(1)}, bf16[192,128]{1,0:T(8,128)(2,1)S(1)}, u32[]{:S(2)}, u32[]{:S(2)}) collective-permute-start(bf16[192,128]{1,0:T(8,128)(2,1)S(1)} %get-tuple-element.15), channel_id=1, source_target_pairs={{0,1},{2,3},{4,5},{6,7},{8,9},{10,11},{12,13},{14,15},{1,0},{3,2},... | collective-permute-start | bytes 147464 | tf_op jit(solution)/shard_map/ppermute | solution.py:406
  10.1 7.5 %all-to-all-start = ((bf16[16,208,128]{2,1,0:T(8,128)(2,1)}), bf16[16,208,128]{2,1,0:T(8,128)(2,1)S(1)}, u32[]{:S(2)}, u32[]{:S(2)}) async-start(bf16[16,208,128]{2,1,0:T(8,128)(2,1)} %get-tuple-element.14), calls=%async_computation | async-start | bytes 1703936 | tf_op jit(solution)/shard_map/all_to_all | solution.py:415
  17.6 0.0 collective-permute-done
  17.6 0.0 copy-start.1
  17.6 2.0 %collective-permute-start.3 = (bf16[2,192,128]{2,1,0:T(8,128)(2,1)S(1)}, bf16[2,192,128]{2,1,0:T(8,128)(2,1)S(1)}, u32[]{:S(2)}, u32[]{:S(2)}) collective-permute-start(bf16[2,192,128]{2,1,0:T(8,128)(2,1)S(1)} %pad_maximum_fusion.pair_ref), channel_id=1, source_target_pairs={{0,12},{2,7},{4,1},{6,11},{8,5},{10,15},{12,9},{14,2},{1,13},{3,6}... | collective-permute-start | bytes 294920 | tf_op jit(solution)/shard_map/ppermute | solution.py:406
  19.6 0.0 collective-permute-start.2
  19.6 0.7 collective-permute-start.1
  20.3 0.1 fusion.8.colid_ref
  20.4 0.0 collective-permute-done.7.d4
  20.4 0.0 copy-start.8
  20.4 1.9 %collective-permute-start.8 = (bf16[192,128]{1,0:T(8,128)(2,1)S(1)}, bf16[192,128]{1,0:T(8,128)(2,1)S(1)}, u32[]{:S(2)}, u32[]{:S(2)}) collective-permute-start(bf16[192,128]{1,0:T(8,128)(2,1)S(1)} %collective-permute-done.7.d4), channel_id=1, source_target_pairs={{0,2},{2,0},{1,3},{3,1},{4,6},{6,4},{5,7},{7,5},{8,10},{10,8},{9,1... | collective-permute-start | bytes 147464 | tf_op jit(solution)/shard_map/ppermute | solution.py:384
  22.2 3.4 %collective-permute-done.3.d3 = bf16[2,192,128]{2,1,0:T(8,128)(2,1)S(1)} collective-permute-done((bf16[2,192,128]{2,1,0:T(8,128)(2,1)S(1)}, bf16[2,192,128]{2,1,0:T(8,128)(2,1)S(1)}, u32[]{:S(2)}, u32[]{:S(2)}) %collective-permute-start.3) | collective-permute-done | bytes 98336 | tf_op jit(solution)/shard_map/ppermute | solution.py:406
  25.6 0.0 copy-start.2
  25.6 0.0 collective-permute-start.6
  25.6 1.7 %collective-permute-done.2.d2 = bf16[2,192,128]{2,1,0:T(8,128)(2,1)S(1)} collective-permute-done((bf16[2,192,128]{2,1,0:T(8,128)(2,1)S(1)}, bf16[2,192,128]{2,1,0:T(8,128)(2,1)S(1)}, u32[]{:S(2)}, u32[]{:S(2)}) %collective-permute-start.2) | collective-permute-done | bytes 98336 | tf_op jit(solution)/shard_map/ppermute | solution.py:406
  27.3 0.0 copy-start.3
  27.3 0.0 collective-permute-start.5
  27.3 2.4 %collective-permute-done.1.d1 = bf16[2,192,128]{2,1,0:T(8,128)(2,1)S(1)} collective-permute-done((bf16[2,192,128]{2,1,0:T(8,128)(2,1)S(1)}, bf16[2,192,128]{2,1,0:T(8,128)(2,1)S(1)}, u32[]{:S(2)}, u32[]{:S(2)}) %collective-permute-start.1) | collective-permute-done | bytes 98336 | tf_op jit(solution)/shard_map/ppermute | solution.py:406
  29.7 0.0 copy-start.4
  29.7 0.0 collective-permute-start.4
  29.7 0.1 pad_add_fusion.own_ref
  29.8 0.0 collective-permute-done.8.s4
  29.8 0.0 copy-start.9
  29.8 0.0 collective-permute-done.6.s3
  29.8 0.0 copy-start.5
  29.8 0.0 collective-permute-done.5.s2
  29.8 0.0 copy-start.6
  29.8 1.2 %collective-permute-done.4.s1 = bf16[2,192,128]{2,1,0:T(8,128)(2,1)S(1)} collective-permute-done((bf16[2,192,128]{2,1,0:T(8,128)(2,1)S(1)}, bf16[2,192,128]{2,1,0:T(8,128)(2,1)S(1)}, u32[]{:S(2)}, u32[]{:S(2)}) %collective-permute-start.4) | collective-permute-done | bytes 98336 | tf_op jit(solution)/shard_map/ppermute | solution.py:384
  31.0 0.0 copy-done.1
  31.0 0.0 copy-done.8
  31.0 0.0 copy-done.2
  31.0 0.0 copy-done.3
  31.0 0.0 copy-done.4
  31.0 0.0 copy-done.9
  31.0 0.0 copy-done.5
  31.1 0.0 copy-done.6
  31.1 0.0 copy-start.7
  31.1 0.6 copy-done.7
  31.7 2.1 %shard_map.42 = (bf16[3072,128]{1,0:T(8,128)(2,1)S(1)}, bf16[128,3072]{1,0:T(8,128)(2,1)S(1)}) custom-call(s32[4]{0:T(128)S(1)} %pad_add_fusion.own_ref, bf16[2,192,128]{2,1,0:T(8,128)(2,1)} %copy-done.1, bf16[2,192,128]{2,1,0:T(8,128)(2,1)} %copy-done.4, bf16[2,192,128]{2,1,0:T(8,128)(2,1)} %copy-done.3, bf16[2,192,128]{2,1,0:T(8,128)(2,1)} %copy-done.2, ...), custom_call_target="tpu_custom_call" | custom-call | flops 10000000000 | bytes 2097152 | tf_op jit(solution)/shard_map/pallas_call | solution.py:79
  33.8 0.0 all-to-all-done.rows_ref
  33.8 9.2 %shard_map.43 = (f32[16,384]{1,0:T(8,128)S(1)}, f32[16,384]{1,0:T(8,128)S(1)}, bf16[3072,128]{1,0:T(8,128)(2,1)}, f32[3072,128]{1,0:T(8,128)S(1)}) custom-call(s32[4]{0:T(128)S(1)} %pad_add_fusion.own_ref, bf16[16,208,128]{2,1,0:T(8,128)(2,1)S(1)} %all-to-all-done.rows_ref, bf16[128,3072]{1,0:T(8,128)(2,1)S(1)} %get-tuple-element.16.colsT, ...), custom_call_target="tpu_custom_call" | custom-call | tf_op jit(solution)/shard_map/pallas_call | solution.py:152
  43.0 0.2 collective-permute-start.9
  43.2 1.1 %collective-permute-done.9.got_ref = f32[16,384]{1,0:T(8,128)S(1)} collective-permute-done((f32[16,384]{1,0:T(8,128)S(1)}, f32[16,384]{1,0:T(8,128)S(1)}, u32[]{:S(2)}, u32[]{:S(2)}) %collective-permute-start.9) | collective-permute-done | bytes 24608 | tf_op jit(solution)/shard_map/ppermute | solution.py:384
  44.2 0.6 shard_map.44
  44.8 14.3 %all_to_all.15.part_ref = f32[16,16,384]{2,1,0:T(8,128)S(1)} all-to-all(f32[16,16,384]{2,1,0:T(8,128)S(1)} %shard_map.44), channel_id=1, replica_groups={{0,16,32,48,64,80,96,112,128,144,160,176,192,208,224,240},{4,20,36,52,6..., dimensions={0} | all-to-all | bytes 786432 | tf_op jit(solution)/shard_map/all_to_all | solution.py:427
  59.2 0.6 shard_map.45
  59.7 0.3 collective-permute-start.10
  60.0 1.2 %collective-permute-done.10.got_ref = f32[16,384]{1,0:T(8,128)S(1)} collective-permute-done((f32[16,384]{1,0:T(8,128)S(1)}, f32[16,384]{1,0:T(8,128)S(1)}, u32[]{:S(2)}, u32[]{:S(2)}) %collective-permute-start.10) | collective-permute-done | bytes 24608 | tf_op jit(solution)/shard_map/ppermute | solution.py:384
  61.2 13.3 %shard_map.46 = f32[16,200,128]{2,1,0:T(8,128)S(1)} custom-call(s32[4]{0:T(128)S(1)} %pad_add_fusion.own_ref, bf16[3072,128]{1,0:T(8,128)(2,1)} %get-tuple-element.17.rows_in, f32[3072,128]{1,0:T(8,128)S(1)} %get-tuple-element.18.mates, bf16[3072,128]{1,0:T(8,128)(2,1)S(1)} %get-tuple-element.19.cols_ref, bf16[128,3072]{1,0:T(8,128)(2,1)S(1)} %get-tuple-element.16.colsT, ...), custom_call_target="tpu_custom_call" | custom-call | tf_op jit(solution)/shard_map/pallas_call | solution.py:293
  74.5 0.0 copy-start
  74.5 28.4 %all_to_all.16.g_ref = f32[16,200,128]{2,1,0:T(8,128)S(1)} all-to-all(f32[16,200,128]{2,1,0:T(8,128)S(1)} %shard_map.46), channel_id=1, replica_groups=mesh['x'=4,'y'=4,'zl'=4,'c'=2,'zh'=2] {'x','y'}, dimensions={0} | all-to-all | bytes 3276800 | tf_op jit(solution)/shard_map/all_to_all | solution.py:431
  102.9 0.0 copy-done
  102.9 0.8 shard_map.47
  (1 shorter events, 0.0 us)
Async XLA Ops:
  2.7 14.9 %collective-permute-start = (bf16[192,128]{1,0:T(8,128)(2,1)S(1)}, bf16[192,128]{1,0:T(8,128)(2,1)S(1)}, u32[]{:S(2)}, u32[]{:S(2)}) collective-permute-start(bf16[192,128]{1,0:T(8,128)(2,1)S(1)} %get-tuple-element.15), channel_id=1, source_target_pairs={{0,2},{2,0},{1,3},{3,1},{4,6},{6,4},{5,7},{7,5},{8,10},{10,8},{9,1... | collective-permute-start | bytes 147464 | tf_op jit(solution)/shard_map/ppermute | solution.py:384
  2.8 17.5 %collective-permute-start.7 = (bf16[192,128]{1,0:T(8,128)(2,1)S(1)}, bf16[192,128]{1,0:T(8,128)(2,1)S(1)}, u32[]{:S(2)}, u32[]{:S(2)}) collective-permute-start(bf16[192,128]{1,0:T(8,128)(2,1)S(1)} %get-tuple-element.15), channel_id=1, source_target_pairs={{0,1},{2,3},{4,5},{6,7},{8,9},{10,11},{12,13},{14,15},{1,0},{3,2},... | collective-permute-start | bytes 147464 | tf_op jit(solution)/shard_map/ppermute | solution.py:406
  10.1 23.7 %all-to-all-start = ((bf16[16,208,128]{2,1,0:T(8,128)(2,1)}), bf16[16,208,128]{2,1,0:T(8,128)(2,1)S(1)}, u32[]{:S(2)}, u32[]{:S(2)}) async-start(bf16[16,208,128]{2,1,0:T(8,128)(2,1)} %get-tuple-element.14), calls=%async_computation | async-start | bytes 1703936 | tf_op jit(solution)/shard_map/all_to_all | solution.py:415
  17.6 13.4 %copy-start.1 = (bf16[2,192,128]{2,1,0:T(8,128)(2,1)}, bf16[2,192,128]{2,1,0:T(8,128)(2,1)S(1)}, u32[]{:S(2)}) copy-start(bf16[2,192,128]{2,1,0:T(8,128)(2,1)S(1)} %pad_maximum_fusion.pair_ref) | copy-start | bytes 294916
  17.6 8.0 %collective-permute-start.3 = (bf16[2,192,128]{2,1,0:T(8,128)(2,1)S(1)}, bf16[2,192,128]{2,1,0:T(8,128)(2,1)S(1)}, u32[]{:S(2)}, u32[]{:S(2)}) collective-permute-start(bf16[2,192,128]{2,1,0:T(8,128)(2,1)S(1)} %pad_maximum_fusion.pair_ref), channel_id=1, source_target_pairs={{0,12},{2,7},{4,1},{6,11},{8,5},{10,15},{12,9},{14,2},{1,13},{3,6}... | collective-permute-start | bytes 294920 | tf_op jit(solution)/shard_map/ppermute | solution.py:406
  19.6 7.7 %collective-permute-start.2 = (bf16[2,192,128]{2,1,0:T(8,128)(2,1)S(1)}, bf16[2,192,128]{2,1,0:T(8,128)(2,1)S(1)}, u32[]{:S(2)}, u32[]{:S(2)}) collective-permute-start(bf16[2,192,128]{2,1,0:T(8,128)(2,1)S(1)} %pad_maximum_fusion.pair_ref), channel_id=1, source_target_pairs={{0,8},{2,11},{4,12},{6,15},{8,1},{10,2},{12,5},{14,6},{1,9},{3,10}... | collective-permute-start | bytes 294920 | tf_op jit(solution)/shard_map/ppermute | solution.py:406
  19.6 10.1 %collective-permute-start.1 = (bf16[2,192,128]{2,1,0:T(8,128)(2,1)S(1)}, bf16[2,192,128]{2,1,0:T(8,128)(2,1)S(1)}, u32[]{:S(2)}, u32[]{:S(2)}) collective-permute-start(bf16[2,192,128]{2,1,0:T(8,128)(2,1)S(1)} %pad_maximum_fusion.pair_ref), channel_id=1, source_target_pairs={{0,4},{2,15},{4,8},{6,2},{8,12},{10,6},{12,1},{14,10},{1,5},{3,14}... | collective-permute-start | bytes 294920 | tf_op jit(solution)/shard_map/ppermute | solution.py:406
  20.4 10.6 %copy-start.8 = (bf16[192,128]{1,0:T(8,128)(2,1)}, bf16[192,128]{1,0:T(8,128)(2,1)S(1)}, u32[]{:S(2)}) copy-start(bf16[192,128]{1,0:T(8,128)(2,1)S(1)} %collective-permute-done.7.d4) | copy-start | bytes 147460
  20.4 9.4 %collective-permute-start.8 = (bf16[192,128]{1,0:T(8,128)(2,1)S(1)}, bf16[192,128]{1,0:T(8,128)(2,1)S(1)}, u32[]{:S(2)}, u32[]{:S(2)}) collective-permute-start(bf16[192,128]{1,0:T(8,128)(2,1)S(1)} %collective-permute-done.7.d4), channel_id=1, source_target_pairs={{0,2},{2,0},{1,3},{3,1},{4,6},{6,4},{5,7},{7,5},{8,10},{10,8},{9,1... | collective-permute-start | bytes 147464 | tf_op jit(solution)/shard_map/ppermute | solution.py:384
  25.6 5.4 %copy-start.2 = (bf16[2,192,128]{2,1,0:T(8,128)(2,1)}, bf16[2,192,128]{2,1,0:T(8,128)(2,1)S(1)}, u32[]{:S(2)}) copy-start(bf16[2,192,128]{2,1,0:T(8,128)(2,1)S(1)} %collective-permute-done.3.d3) | copy-start | bytes 294916
  25.6 4.2 %collective-permute-start.6 = (bf16[2,192,128]{2,1,0:T(8,128)(2,1)S(1)}, bf16[2,192,128]{2,1,0:T(8,128)(2,1)S(1)}, u32[]{:S(2)}, u32[]{:S(2)}) collective-permute-start(bf16[2,192,128]{2,1,0:T(8,128)(2,1)S(1)} %collective-permute-done.3.d3), channel_id=1, source_target_pairs={{0,2},{2,0},{1,3},{3,1},{4,6},{6,4},{5,7},{7,5},{8,10},{10,8},{9,1... | collective-permute-start | bytes 294920 | tf_op jit(solution)/shard_map/ppermute | solution.py:384
  27.3 3.7 %copy-start.3 = (bf16[2,192,128]{2,1,0:T(8,128)(2,1)}, bf16[2,192,128]{2,1,0:T(8,128)(2,1)S(1)}, u32[]{:S(2)}) copy-start(bf16[2,192,128]{2,1,0:T(8,128)(2,1)S(1)} %collective-permute-done.2.d2) | copy-start | bytes 294916
  27.3 2.5 %collective-permute-start.5 = (bf16[2,192,128]{2,1,0:T(8,128)(2,1)S(1)}, bf16[2,192,128]{2,1,0:T(8,128)(2,1)S(1)}, u32[]{:S(2)}, u32[]{:S(2)}) collective-permute-start(bf16[2,192,128]{2,1,0:T(8,128)(2,1)S(1)} %collective-permute-done.2.d2), channel_id=1, source_target_pairs={{0,2},{2,0},{1,3},{3,1},{4,6},{6,4},{5,7},{7,5},{8,10},{10,8},{9,1... | collective-permute-start | bytes 294920 | tf_op jit(solution)/shard_map/ppermute | solution.py:384
  29.7 1.3 %copy-start.4 = (bf16[2,192,128]{2,1,0:T(8,128)(2,1)}, bf16[2,192,128]{2,1,0:T(8,128)(2,1)S(1)}, u32[]{:S(2)}) copy-start(bf16[2,192,128]{2,1,0:T(8,128)(2,1)S(1)} %collective-permute-done.1.d1) | copy-start | bytes 294916
  29.7 1.3 %collective-permute-start.4 = (bf16[2,192,128]{2,1,0:T(8,128)(2,1)S(1)}, bf16[2,192,128]{2,1,0:T(8,128)(2,1)S(1)}, u32[]{:S(2)}, u32[]{:S(2)}) collective-permute-start(bf16[2,192,128]{2,1,0:T(8,128)(2,1)S(1)} %collective-permute-done.1.d1), channel_id=1, source_target_pairs={{0,2},{2,0},{1,3},{3,1},{4,6},{6,4},{5,7},{7,5},{8,10},{10,8},{9,1... | collective-permute-start | bytes 294920 | tf_op jit(solution)/shard_map/ppermute | solution.py:384
  29.8 1.3 %copy-start.9 = (bf16[192,128]{1,0:T(8,128)(2,1)}, bf16[192,128]{1,0:T(8,128)(2,1)S(1)}, u32[]{:S(2)}) copy-start(bf16[192,128]{1,0:T(8,128)(2,1)S(1)} %collective-permute-done.8.s4) | copy-start | bytes 147460
  29.8 1.3 %copy-start.5 = (bf16[2,192,128]{2,1,0:T(8,128)(2,1)}, bf16[2,192,128]{2,1,0:T(8,128)(2,1)S(1)}, u32[]{:S(2)}) copy-start(bf16[2,192,128]{2,1,0:T(8,128)(2,1)S(1)} %collective-permute-done.6.s3) | copy-start | bytes 294916
  29.8 1.2 %copy-start.6 = (bf16[2,192,128]{2,1,0:T(8,128)(2,1)}, bf16[2,192,128]{2,1,0:T(8,128)(2,1)S(1)}, u32[]{:S(2)}) copy-start(bf16[2,192,128]{2,1,0:T(8,128)(2,1)S(1)} %collective-permute-done.5.s2) | copy-start | bytes 294916
  31.1 0.6 copy-start.7
  43.0 1.3 %collective-permute-start.9 = (f32[16,384]{1,0:T(8,128)S(1)}, f32[16,384]{1,0:T(8,128)S(1)}, u32[]{:S(2)}, u32[]{:S(2)}) collective-permute-start(f32[16,384]{1,0:T(8,128)S(1)} %get-tuple-element.21), channel_id=1, source_target_pairs={{0,2},{2,0},{1,3},{3,1},{4,6},{6,4},{5,7},{7,5},{8,10},{10,8},{9,1... | collective-permute-start | bytes 73736 | tf_op jit(solution)/shard_map/ppermute | solution.py:384
  59.7 1.5 %collective-permute-start.10 = (f32[16,384]{1,0:T(8,128)S(1)}, f32[16,384]{1,0:T(8,128)S(1)}, u32[]{:S(2)}, u32[]{:S(2)}) collective-permute-start(f32[16,384]{1,0:T(8,128)S(1)} %get-tuple-element.23), channel_id=1, source_target_pairs={{0,2},{2,0},{1,3},{3,1},{4,6},{6,4},{5,7},{7,5},{8,10},{10,8},{9,1... | collective-permute-start | bytes 73736 | tf_op jit(solution)/shard_map/ppermute | solution.py:384
  74.5 28.4 %copy-start = (f32[192,128]{1,0:T(8,128)S(1)}, f32[192,128]{1,0:T(8,128)}, u32[]{:S(2)}) copy-start(f32[192,128]{1,0:T(8,128)} %p_ref.1) | copy-start | bytes 294916

commit v9 on v8

--- a/solution.py
+++ b/solution.py
@@ -56,21 +56,21 @@
     return rid == lanes
 
 
-def kcols_body(own_ref, pair_ref, d1, d2, d3, s1, s2, s3, d4, s4, cols_ref, colsT, sems):
+def kcols_body(own_ref, pair_ref, d1, d2, d3, s1, s2, s3, d4, s4, cols_ref, colsT):
     core = own_ref[2]
-    places = [(pair_ref.at[0], core), (pair_ref.at[1], 1 - core), (d4, 8 + core), (s4, 9 - core)]
+
+    def put(slot, piece):
+        cols_ref[pl.ds(pl.multiple_of(slot * SH, SH), SH), :] = piece
+
+    put(8 + core, d4[...])
+    put(9 - core, s4[...])
+    put(core, pair_ref[0])
+    put(1 - core, pair_ref[1])
     for off, ref in ((-1, d1), (-2, d2), (-3, d3), (1, s1), (2, s2), (3, s3)):
         slot = jnp.where(core == 0, off & 7, (-off) & 7) * 2
         first = core if off < 0 else 1 - core
-        places += [(ref.at[0], slot + first), (ref.at[1], slot + 1 - first)]
-    copies = []
-    for n, (piece, slot) in enumerate(places):
-        to = cols_ref.at[pl.ds(pl.multiple_of(slot * SH, SH), SH), :]
-        copies.append(pltpu.make_async_copy(piece, to, sems.at[n]))
-    for copy in copies:
-        copy.start()
-    for copy in copies:
-        copy.wait()
+        put(slot + first, ref[0])
+        put(slot + 1 - first, ref[1])
     for c in range(NCH):
         colsT[:, c * CH : (c + 1) * CH] = jnp.transpose(cols_ref[c * CH : (c + 1) * CH, :])
 
@@ -82,9 +82,8 @@
             jax.ShapeDtypeStruct((C, 128), jnp.bfloat16),
             jax.ShapeDtypeStruct((128, C), jnp.bfloat16),
         ),
-        in_specs=[pl.BlockSpec(memory_space=pltpu.SMEM)] + [pl.BlockSpec(memory_space=pltpu.HBM)] * len(pieces),
+        in_specs=[pl.BlockSpec(memory_space=pltpu.SMEM)] + [pl.BlockSpec(memory_space=pltpu.VMEM)] * len(pieces),
         out_specs=(pl.BlockSpec(memory_space=pltpu.VMEM),) * 2,
-        scratch_shapes=[pltpu.SemaphoreType.DMA((16,))],
         compiler_params=pltpu.CompilerParams(vmem_limit_bytes=6 << 20),
         cost_estimate=pl.CostEstimate(flops=10**10, transcendentals=0, bytes_accessed=1 << 21),
     )(own, *pieces)
@@ -421,7 +420,6 @@
     zp = (z + p // (2 * SH)) % NZ
     shard = (zp % 4) * 4 + (p // SH % 2) * 2 + zp // 4
     colid = ((xy * NA + shard) * SH + p % SH).astype(jnp.float32).reshape(16, CH)
-    pieces = [pltpu.with_memory_space_constraint(piece, pltpu.HBM) for piece in pieces]
     cols, colsT = kcols(own, pieces)
     keep, give, rows, mates = k1(own, rows, colsT, colid)
     part = lax.all_to_all(pack(own, keep, swap(give)), AXES, 0, 0, axis_index_groups=total_groups())

time: 105 us -> 103 us (0.981)
  Pallas kernels: 28.6 us -> 27.3 us
    pallas_call x1, Pallas kernels: 2.07 us -> 0.85 us  [kcols(): pl.pallas_call(kcols_body, out_shape=(jax.ShapeDtypeStruct((C, 128), jnp....]
  transfers between devices with their start and end apart: 12 -> 12, of which waited for: 6 -> 6; matrix products, arithmetic and copies ran while one was open for 0% -> 0% of each run, Pallas kernels for 2% -> 1%
where the time goes in v9:
time: 103 us; the launch traced here: 102 us
  blocking collectives  42.7 us (41%)
  Pallas kernels  27.3 us (27%)
  starting transfers between devices  19.9 us (19%)
  waiting for transfers between devices  10.9 us (11%)
    all_to_all x1, blocking collectives, body(): g = lax.all_to_all(g, XY, 0, 0)  28.4 us
    all_to_all x1, blocking collectives, body(): lax.all_to_all(pack(own, keep, swap(give)), AXES, 0, 0, axis_index_groups...  14.4 us
    pallas_call x1, Pallas kernels, k2(): pl.pallas_call(k2_body, out_shape=jax.ShapeDtypeStruct((NB, SH + 8, 128),...  13.3 us
    ppermute x4, starting transfers between devices, along_z(): return lax.ppermute(value, ZC, pairs)  9.93 us
    pallas_call x1, Pallas kernels, k1(): pl.pallas_call(k1_body, out_shape=(jax.ShapeDtypeStruct((16, 2 * SH), jnp...  9.15 us
    all_to_all x1, starting transfers between devices, body(): rows = lax.all_to_all(pay, XY, 0, 0)  7.48 us
    ppermute x4, waiting for transfers between devices, along_z(): return lax.ppermute(value, ZC, pairs)  7.46 us
    ppermute x7, waiting for transfers between devices, swap(): return lax.ppermute(value, 'c', [(0, 1), (1, 0)])  3.44 us
  transfers between devices with their start and end apart: 12, of which 6 were waited for; matrix products, arithmetic and copies ran while one was open for 0% of the time, Pallas kernels for 1%

profile of v9, /device:TPU:2, one launch (start us, length us, event | category | flops | bytes accessed | tf_op | source)
XLA Modules:
  0.0 102.0 jit_solution(16530332858366776547)
XLA Ops:
  0.6 2.1 %shard_map.41 = (bf16[16,208,128]{2,1,0:T(8,128)(2,1)}, bf16[192,128]{1,0:T(8,128)(2,1)S(1)}) custom-call(f32[192,128]{1,0:T(8,128)} %p_ref.1, s32[192]{0:T(256)} %mate_hbm.1), custom_call_target="tpu_custom_call" | custom-call | tf_op jit(solution)/shard_map/pallas_call | solution.py:338
  2.7 0.1 collective-permute-start
  2.8 7.3 %collective-permute-start.7 = (bf16[192,128]{1,0:T(8,128)(2,1)S(1)}, bf16[192,128]{1,0:T(8,128)(2,1)S(1)}, u32[]{:S(2)}, u32[]{:S(2)}) collective-permute-start(bf16[192,128]{1,0:T(8,128)(2,1)S(1)} %get-tuple-element.15), channel_id=1, source_target_pairs={{0,1},{2,3},{4,5},{6,7},{8,9},{10,11},{12,13},{14,15},{1,0},{3,2},... | collective-permute-start | bytes 147464 | tf_op jit(solution)/shard_map/ppermute | solution.py:405
  10.1 7.5 %all-to-all-start = ((bf16[16,208,128]{2,1,0:T(8,128)(2,1)}), bf16[16,208,128]{2,1,0:T(8,128)(2,1)S(1)}, u32[]{:S(2)}, u32[]{:S(2)}) async-start(bf16[16,208,128]{2,1,0:T(8,128)(2,1)} %get-tuple-element.14), calls=%async_computation | async-start | bytes 1703936 | tf_op jit(solution)/shard_map/all_to_all | solution.py:414
  17.6 0.0 collective-permute-done
  17.6 2.0 %collective-permute-start.3 = (bf16[2,192,128]{2,1,0:T(8,128)(2,1)S(1)}, bf16[2,192,128]{2,1,0:T(8,128)(2,1)S(1)}, u32[]{:S(2)}, u32[]{:S(2)}) collective-permute-start(bf16[2,192,128]{2,1,0:T(8,128)(2,1)S(1)} %pad_maximum_fusion.pair_ref), channel_id=1, source_target_pairs={{0,12},{2,7},{4,1},{6,11},{8,5},{10,15},{12,9},{14,2},{1,13},{3,6}... | collective-permute-start | bytes 294920 | tf_op jit(solution)/shard_map/ppermute | solution.py:405
  19.6 0.0 collective-permute-start.2
  19.6 0.7 collective-permute-start.1
  20.3 0.1 fusion.8.colid_ref
  20.3 0.0 collective-permute-done.7.d4
  20.3 1.9 %collective-permute-start.8 = (bf16[192,128]{1,0:T(8,128)(2,1)S(1)}, bf16[192,128]{1,0:T(8,128)(2,1)S(1)}, u32[]{:S(2)}, u32[]{:S(2)}) collective-permute-start(bf16[192,128]{1,0:T(8,128)(2,1)S(1)} %collective-permute-done.7.d4), channel_id=1, source_target_pairs={{0,2},{2,0},{1,3},{3,1},{4,6},{6,4},{5,7},{7,5},{8,10},{10,8},{9,1... | collective-permute-start | bytes 147464 | tf_op jit(solution)/shard_map/ppermute | solution.py:383
  22.2 3.4 %collective-permute-done.3.d3 = bf16[2,192,128]{2,1,0:T(8,128)(2,1)S(1)} collective-permute-done((bf16[2,192,128]{2,1,0:T(8,128)(2,1)S(1)}, bf16[2,192,128]{2,1,0:T(8,128)(2,1)S(1)}, u32[]{:S(2)}, u32[]{:S(2)}) %collective-permute-start.3) | collective-permute-done | bytes 98336 | tf_op jit(solution)/shard_map/ppermute | solution.py:405
  25.6 0.0 collective-permute-start.6
  25.6 1.7 %collective-permute-done.2.d2 = bf16[2,192,128]{2,1,0:T(8,128)(2,1)S(1)} collective-permute-done((bf16[2,192,128]{2,1,0:T(8,128)(2,1)S(1)}, bf16[2,192,128]{2,1,0:T(8,128)(2,1)S(1)}, u32[]{:S(2)}, u32[]{:S(2)}) %collective-permute-start.2) | collective-permute-done | bytes 98336 | tf_op jit(solution)/shard_map/ppermute | solution.py:405
  27.3 0.0 collective-permute-start.5
  27.3 2.4 %collective-permute-done.1.d1 = bf16[2,192,128]{2,1,0:T(8,128)(2,1)S(1)} collective-permute-done((bf16[2,192,128]{2,1,0:T(8,128)(2,1)S(1)}, bf16[2,192,128]{2,1,0:T(8,128)(2,1)S(1)}, u32[]{:S(2)}, u32[]{:S(2)}) %collective-permute-start.1) | collective-permute-done | bytes 98336 | tf_op jit(solution)/shard_map/ppermute | solution.py:405
  29.7 0.0 collective-permute-start.4
  29.7 0.1 pad_add_fusion.own_ref
  29.8 0.0 collective-permute-done.8.s4
  29.8 0.0 collective-permute-done.6.s3
  29.8 0.0 collective-permute-done.5.s2
  29.8 1.2 %collective-permute-done.4.s1 = bf16[2,192,128]{2,1,0:T(8,128)(2,1)S(1)} collective-permute-done((bf16[2,192,128]{2,1,0:T(8,128)(2,1)S(1)}, bf16[2,192,128]{2,1,0:T(8,128)(2,1)S(1)}, u32[]{:S(2)}, u32[]{:S(2)}) %collective-permute-start.4) | collective-permute-done | bytes 98336 | tf_op jit(solution)/shard_map/ppermute | solution.py:383
  31.0 0.8 shard_map.42
  31.8 0.0 all-to-all-done.rows_ref
  31.8 9.1 %shard_map.43 = (f32[16,384]{1,0:T(8,128)S(1)}, f32[16,384]{1,0:T(8,128)S(1)}, bf16[3072,128]{1,0:T(8,128)(2,1)}, f32[3072,128]{1,0:T(8,128)S(1)}) custom-call(s32[4]{0:T(128)S(1)} %pad_add_fusion.own_ref, bf16[16,208,128]{2,1,0:T(8,128)(2,1)S(1)} %all-to-all-done.rows_ref, bf16[128,3072]{1,0:T(8,128)(2,1)S(1)} %get-tuple-element.16.colsT, ...), custom_call_target="tpu_custom_call" | custom-call | tf_op jit(solution)/shard_map/pallas_call | solution.py:151
  41.0 0.2 collective-permute-start.9
  41.2 1.0 %collective-permute-done.9.got_ref = f32[16,384]{1,0:T(8,128)S(1)} collective-permute-done((f32[16,384]{1,0:T(8,128)S(1)}, f32[16,384]{1,0:T(8,128)S(1)}, u32[]{:S(2)}, u32[]{:S(2)}) %collective-permute-start.9) | collective-permute-done | bytes 24608 | tf_op jit(solution)/shard_map/ppermute | solution.py:383
  42.3 0.6 shard_map.44
  42.9 14.4 %all_to_all.15.part_ref = f32[16,16,384]{2,1,0:T(8,128)S(1)} all-to-all(f32[16,16,384]{2,1,0:T(8,128)S(1)} %shard_map.44), channel_id=1, replica_groups={{0,16,32,48,64,80,96,112,128,144,160,176,192,208,224,240},{4,20,36,52,6..., dimensions={0} | all-to-all | bytes 786432 | tf_op jit(solution)/shard_map/all_to_all | solution.py:425
  57.2 0.6 shard_map.45
  57.8 0.3 collective-permute-start.10
  58.1 1.2 %collective-permute-done.10.got_ref = f32[16,384]{1,0:T(8,128)S(1)} collective-permute-done((f32[16,384]{1,0:T(8,128)S(1)}, f32[16,384]{1,0:T(8,128)S(1)}, u32[]{:S(2)}, u32[]{:S(2)}) %collective-permute-start.10) | collective-permute-done | bytes 24608 | tf_op jit(solution)/shard_map/ppermute | solution.py:383
  59.3 13.3 %shard_map.46 = f32[16,200,128]{2,1,0:T(8,128)S(1)} custom-call(s32[4]{0:T(128)S(1)} %pad_add_fusion.own_ref, bf16[3072,128]{1,0:T(8,128)(2,1)} %get-tuple-element.17.rows_in, f32[3072,128]{1,0:T(8,128)S(1)} %get-tuple-element.18.mates, bf16[3072,128]{1,0:T(8,128)(2,1)S(1)} %get-tuple-element.19.cols_ref, bf16[128,3072]{1,0:T(8,128)(2,1)S(1)} %get-tuple-element.16.colsT, ...), custom_call_target="tpu_custom_call" | custom-call | tf_op jit(solution)/shard_map/pallas_call | solution.py:292
  72.6 0.0 copy-start
  72.6 28.4 %all_to_all.16.g_ref = f32[16,200,128]{2,1,0:T(8,128)S(1)} all-to-all(f32[16,200,128]{2,1,0:T(8,128)S(1)} %shard_map.46), channel_id=1, replica_groups=mesh['x'=4,'y'=4,'zl'=4,'c'=2,'zh'=2] {'x','y'}, dimensions={0} | all-to-all | bytes 3276800 | tf_op jit(solution)/shard_map/all_to_all | solution.py:429
  100.9 0.0 copy-done
  100.9 0.8 shard_map.47
  (1 shorter events, 0.0 us)
Async XLA Ops:
  2.7 14.9 %collective-permute-start = (bf16[192,128]{1,0:T(8,128)(2,1)S(1)}, bf16[192,128]{1,0:T(8,128)(2,1)S(1)}, u32[]{:S(2)}, u32[]{:S(2)}) collective-permute-start(bf16[192,128]{1,0:T(8,128)(2,1)S(1)} %get-tuple-element.15), channel_id=1, source_target_pairs={{0,2},{2,0},{1,3},{3,1},{4,6},{6,4},{5,7},{7,5},{8,10},{10,8},{9,1... | collective-permute-start | bytes 147464 | tf_op jit(solution)/shard_map/ppermute | solution.py:383
  2.8 17.5 %collective-permute-start.7 = (bf16[192,128]{1,0:T(8,128)(2,1)S(1)}, bf16[192,128]{1,0:T(8,128)(2,1)S(1)}, u32[]{:S(2)}, u32[]{:S(2)}) collective-permute-start(bf16[192,128]{1,0:T(8,128)(2,1)S(1)} %get-tuple-element.15), channel_id=1, source_target_pairs={{0,1},{2,3},{4,5},{6,7},{8,9},{10,11},{12,13},{14,15},{1,0},{3,2},... | collective-permute-start | bytes 147464 | tf_op jit(solution)/shard_map/ppermute | solution.py:405
  10.1 21.7 %all-to-all-start = ((bf16[16,208,128]{2,1,0:T(8,128)(2,1)}), bf16[16,208,128]{2,1,0:T(8,128)(2,1)S(1)}, u32[]{:S(2)}, u32[]{:S(2)}) async-start(bf16[16,208,128]{2,1,0:T(8,128)(2,1)} %get-tuple-element.14), calls=%async_computation | async-start | bytes 1703936 | tf_op jit(solution)/shard_map/all_to_all | solution.py:414
  17.6 8.0 %collective-permute-start.3 = (bf16[2,192,128]{2,1,0:T(8,128)(2,1)S(1)}, bf16[2,192,128]{2,1,0:T(8,128)(2,1)S(1)}, u32[]{:S(2)}, u32[]{:S(2)}) collective-permute-start(bf16[2,192,128]{2,1,0:T(8,128)(2,1)S(1)} %pad_maximum_fusion.pair_ref), channel_id=1, source_target_pairs={{0,12},{2,7},{4,1},{6,11},{8,5},{10,15},{12,9},{14,2},{1,13},{3,6}... | collective-permute-start | bytes 294920 | tf_op jit(solution)/shard_map/ppermute | solution.py:405
  19.6 7.7 %collective-permute-start.2 = (bf16[2,192,128]{2,1,0:T(8,128)(2,1)S(1)}, bf16[2,192,128]{2,1,0:T(8,128)(2,1)S(1)}, u32[]{:S(2)}, u32[]{:S(2)}) collective-permute-start(bf16[2,192,128]{2,1,0:T(8,128)(2,1)S(1)} %pad_maximum_fusion.pair_ref), channel_id=1, source_target_pairs={{0,8},{2,11},{4,12},{6,15},{8,1},{10,2},{12,5},{14,6},{1,9},{3,10}... | collective-permute-start | bytes 294920 | tf_op jit(solution)/shard_map/ppermute | solution.py:405
  19.6 10.1 %collective-permute-start.1 = (bf16[2,192,128]{2,1,0:T(8,128)(2,1)S(1)}, bf16[2,192,128]{2,1,0:T(8,128)(2,1)S(1)}, u32[]{:S(2)}, u32[]{:S(2)}) collective-permute-start(bf16[2,192,128]{2,1,0:T(8,128)(2,1)S(1)} %pad_maximum_fusion.pair_ref), channel_id=1, source_target_pairs={{0,4},{2,15},{4,8},{6,2},{8,12},{10,6},{12,1},{14,10},{1,5},{3,14}... | collective-permute-start | bytes 294920 | tf_op jit(solution)/shard_map/ppermute | solution.py:405
  20.3 9.4 %collective-permute-start.8 = (bf16[192,128]{1,0:T(8,128)(2,1)S(1)}, bf16[192,128]{1,0:T(8,128)(2,1)S(1)}, u32[]{:S(2)}, u32[]{:S(2)}) collective-permute-start(bf16[192,128]{1,0:T(8,128)(2,1)S(1)} %collective-permute-done.7.d4), channel_id=1, source_target_pairs={{0,2},{2,0},{1,3},{3,1},{4,6},{6,4},{5,7},{7,5},{8,10},{10,8},{9,1... | collective-permute-start | bytes 147464 | tf_op jit(solution)/shard_map/ppermute | solution.py:383
  25.6 4.2 %collective-permute-start.6 = (bf16[2,192,128]{2,1,0:T(8,128)(2,1)S(1)}, bf16[2,192,128]{2,1,0:T(8,128)(2,1)S(1)}, u32[]{:S(2)}, u32[]{:S(2)}) collective-permute-start(bf16[2,192,128]{2,1,0:T(8,128)(2,1)S(1)} %collective-permute-done.3.d3), channel_id=1, source_target_pairs={{0,2},{2,0},{1,3},{3,1},{4,6},{6,4},{5,7},{7,5},{8,10},{10,8},{9,1... | collective-permute-start | bytes 294920 | tf_op jit(solution)/shard_map/ppermute | solution.py:383
  27.3 2.5 %collective-permute-start.5 = (bf16[2,192,128]{2,1,0:T(8,128)(2,1)S(1)}, bf16[2,192,128]{2,1,0:T(8,128)(2,1)S(1)}, u32[]{:S(2)}, u32[]{:S(2)}) collective-permute-start(bf16[2,192,128]{2,1,0:T(8,128)(2,1)S(1)} %collective-permute-done.2.d2), channel_id=1, source_target_pairs={{0,2},{2,0},{1,3},{3,1},{4,6},{6,4},{5,7},{7,5},{8,10},{10,8},{9,1... | collective-permute-start | bytes 294920 | tf_op jit(solution)/shard_map/ppermute | solution.py:383
  29.7 1.3 %collective-permute-start.4 = (bf16[2,192,128]{2,1,0:T(8,128)(2,1)S(1)}, bf16[2,192,128]{2,1,0:T(8,128)(2,1)S(1)}, u32[]{:S(2)}, u32[]{:S(2)}) collective-permute-start(bf16[2,192,128]{2,1,0:T(8,128)(2,1)S(1)} %collective-permute-done.1.d1), channel_id=1, source_target_pairs={{0,2},{2,0},{1,3},{3,1},{4,6},{6,4},{5,7},{7,5},{8,10},{10,8},{9,1... | collective-permute-start | bytes 294920 | tf_op jit(solution)/shard_map/ppermute | solution.py:383
  41.0 1.3 %collective-permute-start.9 = (f32[16,384]{1,0:T(8,128)S(1)}, f32[16,384]{1,0:T(8,128)S(1)}, u32[]{:S(2)}, u32[]{:S(2)}) collective-permute-start(f32[16,384]{1,0:T(8,128)S(1)} %get-tuple-element.21), channel_id=1, source_target_pairs={{0,2},{2,0},{1,3},{3,1},{4,6},{6,4},{5,7},{7,5},{8,10},{10,8},{9,1... | collective-permute-start | bytes 73736 | tf_op jit(solution)/shard_map/ppermute | solution.py:383
  57.8 1.5 %collective-permute-start.10 = (f32[16,384]{1,0:T(8,128)S(1)}, f32[16,384]{1,0:T(8,128)S(1)}, u32[]{:S(2)}, u32[]{:S(2)}) collective-permute-start(f32[16,384]{1,0:T(8,128)S(1)} %get-tuple-element.23), channel_id=1, source_target_pairs={{0,2},{2,0},{1,3},{3,1},{4,6},{6,4},{5,7},{7,5},{8,10},{10,8},{9,1... | collective-permute-start | bytes 73736 | tf_op jit(solution)/shard_map/ppermute | solution.py:383
  72.6 28.4 %copy-start = (f32[192,128]{1,0:T(8,128)S(1)}, f32[192,128]{1,0:T(8,128)}, u32[]{:S(2)}) copy-start(f32[192,128]{1,0:T(8,128)} %p_ref.1) | copy-start | bytes 294916

commit v10 on v9

--- a/solution.py
+++ b/solution.py
@@ -89,7 +89,7 @@
     )(own, *pieces)
 
 
-def k1_body(own_ref, rows_ref, colsT, colid_ref, keep_ref, give_ref, rows_out, mates, rows, racc, hval, cacc, tr, tc, sems):
+def k1_body(own_ref, rows_ref, colsT, colid_ref, keep_ref, give_ref, rows, mates, racc, hval, cacc, tr, tc):
     b = own_ref[0]
     z = own_ref[1]
     core = own_ref[2]
@@ -134,8 +134,6 @@
         return pos + tile((own_tile + k) & (N1 - 1), False)
 
     pos = lax.fori_loop(1, N1, step, pos)
-    keep = pltpu.make_async_copy(rows, rows_out, sems)
-    keep.start()
     total = jnp.sum(cacc[...], axis=0, keepdims=True)
     for k in range(NZ):
         tc[pl.ds((z + k) & 7, 1), :] = total[:, k * 2 * SH : (k + 1) * 2 * SH]
@@ -144,7 +142,6 @@
     by_cols = jnp.concatenate([tc[...], jnp.concatenate([pos, none], axis=1)], axis=0)
     keep_ref[...] = jnp.where(core == 0, by_rows, by_cols)
     give_ref[...] = jnp.where(core == 0, by_cols, by_rows)
-    keep.wait()
 
 
 def k1(own, rows, colsT, colid):
@@ -153,24 +150,22 @@
         out_shape=(
             jax.ShapeDtypeStruct((16, 2 * SH), jnp.float32),
             jax.ShapeDtypeStruct((16, 2 * SH), jnp.float32),
-            pltpu.HBM((R, 128), jnp.bfloat16),
+            jax.ShapeDtypeStruct((R, 128), jnp.bfloat16),
             jax.ShapeDtypeStruct((R, 128), jnp.float32),
         ),
         in_specs=[pl.BlockSpec(memory_space=pltpu.SMEM)] + [pl.BlockSpec(memory_space=pltpu.VMEM)] * 3,
         out_specs=(
             pl.BlockSpec(memory_space=pltpu.VMEM),
             pl.BlockSpec(memory_space=pltpu.VMEM),
-            pl.BlockSpec(memory_space=pltpu.HBM),
+            pl.BlockSpec(memory_space=pltpu.VMEM),
             pl.BlockSpec(memory_space=pltpu.VMEM),
         ),
         scratch_shapes=[
-            pltpu.VMEM((R, 128), jnp.bfloat16),
             pltpu.VMEM((T1, 128), jnp.float32),
             pltpu.VMEM((T1, 128), jnp.float32),
             pltpu.VMEM((8, C), jnp.float32),
             pltpu.VMEM((8, 2 * SH), jnp.float32),
             pltpu.VMEM((8, 2 * SH), jnp.float32),
-            pltpu.SemaphoreType.DMA,
         ],
         compiler_params=pltpu.CompilerParams(vmem_limit_bytes=12 << 20),
     )(own, rows, colsT, colid)
@@ -225,9 +220,7 @@
     )(own, part)
 
 
-def k2_body(own_ref, rows_in, mates, cols_ref, colsT, colid_ref, keep_ref, got_ref, g_ref, rows, ris, rrow, rcol, sem):
-    fetch = pltpu.make_async_copy(rows_in, rows, sem)
-    fetch.start()
+def k2_body(own_ref, rows, mates, cols_ref, colsT, colid_ref, keep_ref, got_ref, g_ref, ris, rrow, rcol):
     b = own_ref[0]
     z = own_ref[1]
     core = own_ref[2]
@@ -277,7 +270,6 @@
         for q in range(PER2):
             g_ref[t * PER2 + q, 0:SH, :] = acc[q * SH : (q + 1) * SH]
 
-    fetch.wait()
     own_tile = b // PER2
     tile(own_tile, True)
 
@@ -292,15 +284,12 @@
     return pl.pallas_call(
         k2_body,
         out_shape=jax.ShapeDtypeStruct((NB, SH + 8, 128), jnp.float32),
-        in_specs=[pl.BlockSpec(memory_space=pltpu.SMEM), pl.BlockSpec(memory_space=pltpu.HBM)]
-        + [pl.BlockSpec(memory_space=pltpu.VMEM)] * 6,
+        in_specs=[pl.BlockSpec(memory_space=pltpu.SMEM)] + [pl.BlockSpec(memory_space=pltpu.VMEM)] * 7,
         out_specs=pl.BlockSpec(memory_space=pltpu.VMEM),
         scratch_shapes=[
-            pltpu.VMEM((R, 128), jnp.bfloat16),
             pltpu.VMEM((T2, 128), jnp.float32),
             pltpu.VMEM((8, 2 * SH), jnp.float32),
             pltpu.VMEM((16, 2 * SH), jnp.float32),
-            pltpu.SemaphoreType.DMA,
         ],
         compiler_params=pltpu.CompilerParams(vmem_limit_bytes=12 << 20),
     )(own, rows, mates, cols, colsT, colid, keep, got)
@@ -424,7 +413,6 @@
     keep, give, rows, mates = k1(own, rows, colsT, colid)
     part = lax.all_to_all(pack(own, keep, swap(give)), AXES, 0, 0, axis_index_groups=total_groups())
     keep, give = mid(own, part)
-    rows = pltpu.with_memory_space_constraint(rows, pltpu.HBM)
     g = k2(own, rows, mates, cols, colsT, colid, keep, swap(give))
     g = lax.all_to_all(g, XY, 0, 0)
     loss, grad = final(projections, g)

time: 103 us -> 102 us (level)
  Pallas kernels: 27.3 us -> 26.2 us
    pallas_call x1, Pallas kernels: 13.3 us -> 12.1 us  [k2(): pl.pallas_call(k2_body, out_shape=jax.ShapeDtypeStruct((NB, SH + 8, 128),...]
where the time goes in v10:
time: 102 us; the launch traced here: 101 us
  blocking collectives  42.7 us (42%)
  Pallas kernels  26.2 us (26%)
  starting transfers between devices  19.9 us (20%)
  waiting for transfers between devices  10.9 us (11%)
    all_to_all x1, blocking collectives, body(): g = lax.all_to_all(g, XY, 0, 0)  28.4 us
    all_to_all x1, blocking collectives, body(): lax.all_to_all(pack(own, keep, swap(give)), AXES, 0, 0, axis_index_groups...  14.4 us
    pallas_call x1, Pallas kernels, k2(): pl.pallas_call(k2_body, out_shape=jax.ShapeDtypeStruct((NB, SH + 8, 128),...  12.1 us
    ppermute x4, starting transfers between devices, along_z(): return lax.ppermute(value, ZC, pairs)  9.93 us
    pallas_call x1, Pallas kernels, k1(): pl.pallas_call(k1_body, out_shape=(jax.ShapeDtypeStruct((16, 2 * SH), jnp...  9.13 us
    all_to_all x1, starting transfers between devices, body(): rows = lax.all_to_all(pay, XY, 0, 0)  7.48 us
    ppermute x4, waiting for transfers between devices, along_z(): return lax.ppermute(value, ZC, pairs)  7.46 us
    ppermute x7, waiting for transfers between devices, swap(): return lax.ppermute(value, 'c', [(0, 1), (1, 0)])  3.44 us
  transfers between devices with their start and end apart: 12, of which 6 were waited for; matrix products, arithmetic and copies ran while one was open for 0% of the time, Pallas kernels for 1%

profile of v10, /device:TPU:2, one launch (start us, length us, event | category | flops | bytes accessed | tf_op | source)
XLA Modules:
  0.0 100.8 jit_solution(1602542827346691805)
XLA Ops:
  0.6 2.1 %shard_map.41 = (bf16[16,208,128]{2,1,0:T(8,128)(2,1)}, bf16[192,128]{1,0:T(8,128)(2,1)S(1)}) custom-call(f32[192,128]{1,0:T(8,128)} %p_ref.1, s32[192]{0:T(256)} %mate_hbm.1), custom_call_target="tpu_custom_call" | custom-call | tf_op jit(solution)/shard_map/pallas_call | solution.py:327
  2.7 0.1 collective-permute-start
  2.8 7.3 %collective-permute-start.7 = (bf16[192,128]{1,0:T(8,128)(2,1)S(1)}, bf16[192,128]{1,0:T(8,128)(2,1)S(1)}, u32[]{:S(2)}, u32[]{:S(2)}) collective-permute-start(bf16[192,128]{1,0:T(8,128)(2,1)S(1)} %get-tuple-element.15), channel_id=1, source_target_pairs={{0,1},{2,3},{4,5},{6,7},{8,9},{10,11},{12,13},{14,15},{1,0},{3,2},... | collective-permute-start | bytes 147464 | tf_op jit(solution)/shard_map/ppermute | solution.py:394
  10.1 7.5 %all-to-all-start = ((bf16[16,208,128]{2,1,0:T(8,128)(2,1)}), bf16[16,208,128]{2,1,0:T(8,128)(2,1)S(1)}, u32[]{:S(2)}, u32[]{:S(2)}) async-start(bf16[16,208,128]{2,1,0:T(8,128)(2,1)} %get-tuple-element.14), calls=%async_computation | async-start | bytes 1703936 | tf_op jit(solution)/shard_map/all_to_all | solution.py:403
  17.6 0.0 collective-permute-done
  17.6 2.0 %collective-permute-start.3 = (bf16[2,192,128]{2,1,0:T(8,128)(2,1)S(1)}, bf16[2,192,128]{2,1,0:T(8,128)(2,1)S(1)}, u32[]{:S(2)}, u32[]{:S(2)}) collective-permute-start(bf16[2,192,128]{2,1,0:T(8,128)(2,1)S(1)} %pad_maximum_fusion.pair_ref), channel_id=1, source_target_pairs={{0,12},{2,7},{4,1},{6,11},{8,5},{10,15},{12,9},{14,2},{1,13},{3,6}... | collective-permute-start | bytes 294920 | tf_op jit(solution)/shard_map/ppermute | solution.py:394
  19.6 0.0 collective-permute-start.2
  19.6 0.7 collective-permute-start.1
  20.3 0.1 fusion.8.colid_ref
  20.3 0.0 collective-permute-done.7.d4
  20.3 1.9 %collective-permute-start.8 = (bf16[192,128]{1,0:T(8,128)(2,1)S(1)}, bf16[192,128]{1,0:T(8,128)(2,1)S(1)}, u32[]{:S(2)}, u32[]{:S(2)}) collective-permute-start(bf16[192,128]{1,0:T(8,128)(2,1)S(1)} %collective-permute-done.7.d4), channel_id=1, source_target_pairs={{0,2},{2,0},{1,3},{3,1},{4,6},{6,4},{5,7},{7,5},{8,10},{10,8},{9,1... | collective-permute-start | bytes 147464 | tf_op jit(solution)/shard_map/ppermute | solution.py:372
  22.2 3.4 %collective-permute-done.3.d3 = bf16[2,192,128]{2,1,0:T(8,128)(2,1)S(1)} collective-permute-done((bf16[2,192,128]{2,1,0:T(8,128)(2,1)S(1)}, bf16[2,192,128]{2,1,0:T(8,128)(2,1)S(1)}, u32[]{:S(2)}, u32[]{:S(2)}) %collective-permute-start.3) | collective-permute-done | bytes 98336 | tf_op jit(solution)/shard_map/ppermute | solution.py:394
  25.6 0.0 collective-permute-start.6
  25.6 1.7 %collective-permute-done.2.d2 = bf16[2,192,128]{2,1,0:T(8,128)(2,1)S(1)} collective-permute-done((bf16[2,192,128]{2,1,0:T(8,128)(2,1)S(1)}, bf16[2,192,128]{2,1,0:T(8,128)(2,1)S(1)}, u32[]{:S(2)}, u32[]{:S(2)}) %collective-permute-start.2) | collective-permute-done | bytes 98336 | tf_op jit(solution)/shard_map/ppermute | solution.py:394
  27.3 0.0 collective-permute-start.5
  27.3 2.4 %collective-permute-done.1.d1 = bf16[2,192,128]{2,1,0:T(8,128)(2,1)S(1)} collective-permute-done((bf16[2,192,128]{2,1,0:T(8,128)(2,1)S(1)}, bf16[2,192,128]{2,1,0:T(8,128)(2,1)S(1)}, u32[]{:S(2)}, u32[]{:S(2)}) %collective-permute-start.1) | collective-permute-done | bytes 98336 | tf_op jit(solution)/shard_map/ppermute | solution.py:394
  29.7 0.0 collective-permute-start.4
  29.7 0.1 pad_add_fusion.own_ref
  29.8 0.0 collective-permute-done.8.s4
  29.8 0.0 collective-permute-done.6.s3
  29.8 0.0 collective-permute-done.5.s2
  29.8 1.2 %collective-permute-done.4.s1 = bf16[2,192,128]{2,1,0:T(8,128)(2,1)S(1)} collective-permute-done((bf16[2,192,128]{2,1,0:T(8,128)(2,1)S(1)}, bf16[2,192,128]{2,1,0:T(8,128)(2,1)S(1)}, u32[]{:S(2)}, u32[]{:S(2)}) %collective-permute-start.4) | collective-permute-done | bytes 98336 | tf_op jit(solution)/shard_map/ppermute | solution.py:372
  31.0 0.8 shard_map.42
  31.8 0.0 all-to-all-done.rows_ref
  31.8 9.1 %shard_map.43 = (f32[16,384]{1,0:T(8,128)S(1)}, f32[16,384]{1,0:T(8,128)S(1)}, bf16[3072,128]{1,0:T(8,128)(2,1)S(1)}, f32[3072,128]{1,0:T(8,128)S(1)}) custom-call(s32[4]{0:T(128)S(1)} %pad_add_fusion.own_ref, bf16[16,208,128]{2,1,0:T(8,128)(2,1)S(1)} %all-to-all-done.rows_ref, bf16[128,3072]{1,0:T(8,128)(2,1)S(1)} %get-tuple-element.16.colsT, ...), custom_call_target="tpu_custom_call" | custom-call | tf_op jit(solution)/shard_map/pallas_call | solution.py:148
  41.0 0.2 collective-permute-start.9
  41.2 1.0 %collective-permute-done.9.got_ref = f32[16,384]{1,0:T(8,128)S(1)} collective-permute-done((f32[16,384]{1,0:T(8,128)S(1)}, f32[16,384]{1,0:T(8,128)S(1)}, u32[]{:S(2)}, u32[]{:S(2)}) %collective-permute-start.9) | collective-permute-done | bytes 24608 | tf_op jit(solution)/shard_map/ppermute | solution.py:372
  42.2 0.6 shard_map.44
  42.8 14.4 %all_to_all.15.part_ref = f32[16,16,384]{2,1,0:T(8,128)S(1)} all-to-all(f32[16,16,384]{2,1,0:T(8,128)S(1)} %shard_map.44), channel_id=1, replica_groups={{0,16,32,48,64,80,96,112,128,144,160,176,192,208,224,240},{4,20,36,52,6..., dimensions={0} | all-to-all | bytes 786432 | tf_op jit(solution)/shard_map/all_to_all | solution.py:414
  57.1 0.6 shard_map.45
  57.7 0.3 collective-permute-start.10
  58.0 1.2 %collective-permute-done.10.got_ref = f32[16,384]{1,0:T(8,128)S(1)} collective-permute-done((f32[16,384]{1,0:T(8,128)S(1)}, f32[16,384]{1,0:T(8,128)S(1)}, u32[]{:S(2)}, u32[]{:S(2)}) %collective-permute-start.10) | collective-permute-done | bytes 24608 | tf_op jit(solution)/shard_map/ppermute | solution.py:372
  59.2 12.1 %shard_map.46 = f32[16,200,128]{2,1,0:T(8,128)S(1)} custom-call(s32[4]{0:T(128)S(1)} %pad_add_fusion.own_ref, bf16[3072,128]{1,0:T(8,128)(2,1)S(1)} %get-tuple-element.17.rows, f32[3072,128]{1,0:T(8,128)S(1)} %get-tuple-element.18.mates, bf16[3072,128]{1,0:T(8,128)(2,1)S(1)} %get-tuple-element.19.cols_ref, bf16[128,3072]{1,0:T(8,128)(2,1)S(1)} %get-tuple-element.16.colsT, ...), custom_call_target="tpu_custom_call" | custom-call | tf_op jit(solution)/shard_map/pallas_call | solution.py:284
  71.4 0.0 copy-start
  71.4 28.4 %all_to_all.16.g_ref = f32[16,200,128]{2,1,0:T(8,128)S(1)} all-to-all(f32[16,200,128]{2,1,0:T(8,128)S(1)} %shard_map.46), channel_id=1, replica_groups=mesh['x'=4,'y'=4,'zl'=4,'c'=2,'zh'=2] {'x','y'}, dimensions={0} | all-to-all | bytes 3276800 | tf_op jit(solution)/shard_map/all_to_all | solution.py:417
  99.8 0.0 copy-done
  99.8 0.8 shard_map.47
  (1 shorter events, 0.0 us)
Async XLA Ops:
  2.7 14.9 %collective-permute-start = (bf16[192,128]{1,0:T(8,128)(2,1)S(1)}, bf16[192,128]{1,0:T(8,128)(2,1)S(1)}, u32[]{:S(2)}, u32[]{:S(2)}) collective-permute-start(bf16[192,128]{1,0:T(8,128)(2,1)S(1)} %get-tuple-element.15), channel_id=1, source_target_pairs={{0,2},{2,0},{1,3},{3,1},{4,6},{6,4},{5,7},{7,5},{8,10},{10,8},{9,1... | collective-permute-start | bytes 147464 | tf_op jit(solution)/shard_map/ppermute | solution.py:372
  2.8 17.5 %collective-permute-start.7 = (bf16[192,128]{1,0:T(8,128)(2,1)S(1)}, bf16[192,128]{1,0:T(8,128)(2,1)S(1)}, u32[]{:S(2)}, u32[]{:S(2)}) collective-permute-start(bf16[192,128]{1,0:T(8,128)(2,1)S(1)} %get-tuple-element.15), channel_id=1, source_target_pairs={{0,1},{2,3},{4,5},{6,7},{8,9},{10,11},{12,13},{14,15},{1,0},{3,2},... | collective-permute-start | bytes 147464 | tf_op jit(solution)/shard_map/ppermute | solution.py:394
  10.1 21.7 %all-to-all-start = ((bf16[16,208,128]{2,1,0:T(8,128)(2,1)}), bf16[16,208,128]{2,1,0:T(8,128)(2,1)S(1)}, u32[]{:S(2)}, u32[]{:S(2)}) async-start(bf16[16,208,128]{2,1,0:T(8,128)(2,1)} %get-tuple-element.14), calls=%async_computation | async-start | bytes 1703936 | tf_op jit(solution)/shard_map/all_to_all | solution.py:403
  17.6 8.0 %collective-permute-start.3 = (bf16[2,192,128]{2,1,0:T(8,128)(2,1)S(1)}, bf16[2,192,128]{2,1,0:T(8,128)(2,1)S(1)}, u32[]{:S(2)}, u32[]{:S(2)}) collective-permute-start(bf16[2,192,128]{2,1,0:T(8,128)(2,1)S(1)} %pad_maximum_fusion.pair_ref), channel_id=1, source_target_pairs={{0,12},{2,7},{4,1},{6,11},{8,5},{10,15},{12,9},{14,2},{1,13},{3,6}... | collective-permute-start | bytes 294920 | tf_op jit(solution)/shard_map/ppermute | solution.py:394
  19.6 7.7 %collective-permute-start.2 = (bf16[2,192,128]{2,1,0:T(8,128)(2,1)S(1)}, bf16[2,192,128]{2,1,0:T(8,128)(2,1)S(1)}, u32[]{:S(2)}, u32[]{:S(2)}) collective-permute-start(bf16[2,192,128]{2,1,0:T(8,128)(2,1)S(1)} %pad_maximum_fusion.pair_ref), channel_id=1, source_target_pairs={{0,8},{2,11},{4,12},{6,15},{8,1},{10,2},{12,5},{14,6},{1,9},{3,10}... | collective-permute-start | bytes 294920 | tf_op jit(solution)/shard_map/ppermute | solution.py:394
  19.6 10.1 %collective-permute-start.1 = (bf16[2,192,128]{2,1,0:T(8,128)(2,1)S(1)}, bf16[2,192,128]{2,1,0:T(8,128)(2,1)S(1)}, u32[]{:S(2)}, u32[]{:S(2)}) collective-permute-start(bf16[2,192,128]{2,1,0:T(8,128)(2,1)S(1)} %pad_maximum_fusion.pair_ref), channel_id=1, source_target_pairs={{0,4},{2,15},{4,8},{6,2},{8,12},{10,6},{12,1},{14,10},{1,5},{3,14}... | collective-permute-start | bytes 294920 | tf_op jit(solution)/shard_map/ppermute | solution.py:394
  20.3 9.4 %collective-permute-start.8 = (bf16[192,128]{1,0:T(8,128)(2,1)S(1)}, bf16[192,128]{1,0:T(8,128)(2,1)S(1)}, u32[]{:S(2)}, u32[]{:S(2)}) collective-permute-start(bf16[192,128]{1,0:T(8,128)(2,1)S(1)} %collective-permute-done.7.d4), channel_id=1, source_target_pairs={{0,2},{2,0},{1,3},{3,1},{4,6},{6,4},{5,7},{7,5},{8,10},{10,8},{9,1... | collective-permute-start | bytes 147464 | tf_op jit(solution)/shard_map/ppermute | solution.py:372
  25.6 4.2 %collective-permute-start.6 = (bf16[2,192,128]{2,1,0:T(8,128)(2,1)S(1)}, bf16[2,192,128]{2,1,0:T(8,128)(2,1)S(1)}, u32[]{:S(2)}, u32[]{:S(2)}) collective-permute-start(bf16[2,192,128]{2,1,0:T(8,128)(2,1)S(1)} %collective-permute-done.3.d3), channel_id=1, source_target_pairs={{0,2},{2,0},{1,3},{3,1},{4,6},{6,4},{5,7},{7,5},{8,10},{10,8},{9,1... | collective-permute-start | bytes 294920 | tf_op jit(solution)/shard_map/ppermute | solution.py:372
  27.3 2.5 %collective-permute-start.5 = (bf16[2,192,128]{2,1,0:T(8,128)(2,1)S(1)}, bf16[2,192,128]{2,1,0:T(8,128)(2,1)S(1)}, u32[]{:S(2)}, u32[]{:S(2)}) collective-permute-start(bf16[2,192,128]{2,1,0:T(8,128)(2,1)S(1)} %collective-permute-done.2.d2), channel_id=1, source_target_pairs={{0,2},{2,0},{1,3},{3,1},{4,6},{6,4},{5,7},{7,5},{8,10},{10,8},{9,1... | collective-permute-start | bytes 294920 | tf_op jit(solution)/shard_map/ppermute | solution.py:372
  29.7 1.3 %collective-permute-start.4 = (bf16[2,192,128]{2,1,0:T(8,128)(2,1)S(1)}, bf16[2,192,128]{2,1,0:T(8,128)(2,1)S(1)}, u32[]{:S(2)}, u32[]{:S(2)}) collective-permute-start(bf16[2,192,128]{2,1,0:T(8,128)(2,1)S(1)} %collective-permute-done.1.d1), channel_id=1, source_target_pairs={{0,2},{2,0},{1,3},{3,1},{4,6},{6,4},{5,7},{7,5},{8,10},{10,8},{9,1... | collective-permute-start | bytes 294920 | tf_op jit(solution)/shard_map/ppermute | solution.py:372
  41.0 1.2 %collective-permute-start.9 = (f32[16,384]{1,0:T(8,128)S(1)}, f32[16,384]{1,0:T(8,128)S(1)}, u32[]{:S(2)}, u32[]{:S(2)}) collective-permute-start(f32[16,384]{1,0:T(8,128)S(1)} %get-tuple-element.21), channel_id=1, source_target_pairs={{0,2},{2,0},{1,3},{3,1},{4,6},{6,4},{5,7},{7,5},{8,10},{10,8},{9,1... | collective-permute-start | bytes 73736 | tf_op jit(solution)/shard_map/ppermute | solution.py:372
  57.7 1.5 %collective-permute-start.10 = (f32[16,384]{1,0:T(8,128)S(1)}, f32[16,384]{1,0:T(8,128)S(1)}, u32[]{:S(2)}, u32[]{:S(2)}) collective-permute-start(f32[16,384]{1,0:T(8,128)S(1)} %get-tuple-element.23), channel_id=1, source_target_pairs={{0,2},{2,0},{1,3},{3,1},{4,6},{6,4},{5,7},{7,5},{8,10},{10,8},{9,1... | collective-permute-start | bytes 73736 | tf_op jit(solution)/shard_map/ppermute | solution.py:372
  71.4 28.4 %copy-start = (f32[192,128]{1,0:T(8,128)S(1)}, f32[192,128]{1,0:T(8,128)}, u32[]{:S(2)}) copy-start(f32[192,128]{1,0:T(8,128)} %p_ref.1) | copy-start | bytes 294916
